TPU v7x, 512 devices: a whole 4x4x16 slice. The times are simulated.
512 devices in a mesh: req: 128 (over y, z, core), mdl: 4 (over x).
Axes of the slice: x: 4, y: 4, z: 16, core: 2. Of those that a mesh axis runs over, the one named last changes fastest.
Arguments:
- lengths: int32 [512], P('req'), may hold values from 16 to 768, as said below
- assignment: int32 [512], replicated, may hold values from 0 to 511, each once
- query: bfloat16 [512, 4096], P('req', 'mdl'), may hold values from -6 to 6
- key_value_fresh: bfloat16 [2, 512, 1024], P(None, 'req', 'mdl'), may hold values from -4.5 to 4.5
- kv_cache: bfloat16 [2, 131072, 1024], P(None, 'req', 'mdl'), may hold values from -6 to 6, as said below
- hidden_in: bfloat16 [512, 5120], P(None, ('req', 'mdl')), may hold values from -60 to 60
- out_weight: bfloat16 [4096, 5120], P('mdl', 'req'), may hold values from -0.09375 to 0.09375
- norm_gain: float32 [5120], replicated, may hold values from 0.5 to 1.5
- gate_up_weight: bfloat16 [2, 128, 4, 10, 32768], P(None, None, 'mdl', None, 'req'), may hold values from -0.078125 to 0.078125
- down_weight: bfloat16 [32768, 128, 4, 10], P('req', None, 'mdl'), may hold values from -0.125 to 0.125
Outputs:
- layer_out: bfloat16 [512, 5120], P(None, ('req', 'mdl'))
- kv_out: bfloat16 [2, 131072, 1024], P(None, 'req', 'mdl')
Inputs may be any that keep to these rules, and one draw needn't show every extreme that they name: `lengths`: each value is from 16 to 48, except in exactly 6 slots, which lie in 6 different blocks of 4 slots and hold exactly 768. `assignment`: each request appears once. `kv_cache`: the cache of block r lies in rows r * 1024 on: its slots in order, slot s taking lengths[s] + 1 rows, of which the first lengths[s] hold its cached tokens and the last is free for the new one; the rows after them belong to no slot.
All inputs are finite; a program needn't handle non-finite values.
Results may differ from a plain program's by a relative error of at most 0.017.
Values may be sent and summed in bfloat16 or wider, within the bound.
No kernel may reach another device: no remote copies, remote signals or barrier semaphores. Data moves between devices by JAX's collectives and lax.ppermute only.
A program may use at most 64 MiB of HBM per device.

v0:
```python
import jax
import jax.numpy as jnp
from jax import lax
from jax.sharding import PartitionSpec as P

D = 5120
QUERY_HEADS = 32
KEY_VALUE_HEADS = 8
HEAD_SIZE = 128


NEGATIVE_FILL = -1e30


def slot_bounds(lengths):
    span_sizes = lengths + 1
    first_rows = jnp.cumsum(span_sizes) - span_sizes
    return (first_rows, first_rows + span_sizes)


def attend_rows(query_rows, key_value_store, row_base, first_rows, end_rows):
    block_rows = 128
    slot_count, kv_heads, group_width, head_dim = query_rows.shape
    pool_rows = key_value_store.shape[1]
    key_table = key_value_store[0].reshape(pool_rows, kv_heads, head_dim)
    value_table = key_value_store[1].reshape(pool_rows, kv_heads, head_dim)
    needed = jnp.clip(jnp.max(end_rows) - row_base, 0, pool_rows)
    block_count = (needed + block_rows - 1) // block_rows
    score_scale = head_dim ** (-0.5)

    def advance(block_index, carried):
        running_max, denominator, accumulated = carried
        offset = block_index * block_rows
        key_block = lax.dynamic_slice_in_dim(key_table, offset, block_rows, 0)
        value_block = lax.dynamic_slice_in_dim(value_table, offset, block_rows, 0)
        scores = (
            jnp.einsum("sngd,tnd->sngt", query_rows, key_block, preferred_element_type=jnp.float32)
            * score_scale
        )
        row_ids = row_base + offset + jnp.arange(block_rows, dtype=jnp.int32)
        inside = (
            (row_ids[None, :] >= first_rows[:, None]) & (row_ids[None, :] < end_rows[:, None])
        )[:, None, None, :]
        scores = jnp.where(inside, scores, NEGATIVE_FILL)
        new_max = jnp.maximum(running_max, jnp.max(scores, axis=-1))
        weights = jnp.where(inside, jnp.exp(scores - new_max[..., None]), 0.0)
        factor = jnp.exp(running_max - new_max)
        denominator = denominator * factor + jnp.sum(weights, axis=-1)
        accumulated = accumulated * factor[..., None] + jnp.einsum(
            "sngt,tnd->sngd",
            weights.astype(jnp.bfloat16),
            value_block,
            preferred_element_type=jnp.float32,
        )
        return (new_max, denominator, accumulated)

    initial = (
        jnp.full((slot_count, kv_heads, group_width), NEGATIVE_FILL, jnp.float32),
        jnp.zeros((slot_count, kv_heads, group_width), jnp.float32),
        jnp.zeros((slot_count, kv_heads, group_width, head_dim), jnp.float32),
    )
    return lax.fori_loop(0, block_count, advance, initial)


def body(
    lengths,
    assignment,
    query,
    key_value_fresh,
    kv_cache,
    hidden_in,
    out_weight,
    norm_gain,
    gate_up_weight,
    down_weight,
):
    slot_count = lengths.shape[0]
    first_rows, end_rows = slot_bounds(lengths)
    key_value_store = kv_cache
    for slot_index in range(slot_count):
        key_value_store = lax.dynamic_update_slice(
            key_value_store,
            key_value_fresh[:, slot_index : slot_index + 1, :],
            (jnp.int32(0), end_rows[slot_index] - 1, jnp.int32(0)),
        )
    kv_heads = key_value_store.shape[2] // HEAD_SIZE
    group_width = QUERY_HEADS // KEY_VALUE_HEADS
    query_rows = query.reshape(slot_count, kv_heads, group_width, HEAD_SIZE)
    joint_max, denominator, accumulated = attend_rows(
        query_rows, key_value_store, 0, first_rows, end_rows
    )
    attended = (
        (accumulated / denominator[..., None])
        .astype(jnp.bfloat16)
        .reshape(slot_count, kv_heads * group_width * HEAD_SIZE)
    )
    projected = jnp.dot(
        lax.all_gather(attended, "req", axis=0, tiled=True),
        out_weight,
        preferred_element_type=jnp.float32,
    )
    head_share = lax.psum_scatter(
        projected.astype(jnp.bfloat16), "mdl", scatter_dimension=1, tiled=True
    ).astype(jnp.float32)
    total_rows = assignment.shape[0]
    inverse = (
        jnp.zeros((total_rows,), jnp.int32)
        .at[assignment]
        .set(jnp.arange(total_rows, dtype=jnp.int32))
    )
    placed = jnp.take(head_share, inverse, axis=0)
    residual_wide = hidden_in.astype(jnp.float32) + placed
    residual = residual_wide.astype(jnp.bfloat16)
    local_wide = residual.astype(jnp.float32)
    gathered = lax.all_gather(residual, "req", axis=1, tiled=True)
    widened = gathered.astype(jnp.float32)
    square_sum = lax.psum(jnp.sum(widened * widened, axis=1), "mdl")
    col_groups = gate_up_weight.shape[1]
    sub_width = hidden_in.shape[1]
    gain_table = norm_gain.reshape(col_groups, lax.axis_size("mdl"), sub_width)
    gain_cols = lax.dynamic_index_in_dim(
        gain_table, lax.axis_index("mdl"), 1, keepdims=False
    ).reshape(col_groups * sub_width)
    normed = (widened * lax.rsqrt(square_sum / D + 1e-05)[:, None] * gain_cols).astype(jnp.bfloat16)
    gate_up = gate_up_weight.reshape(2, col_groups * sub_width, gate_up_weight.shape[4])
    partial_value = jnp.einsum("rk,gkf->grf", normed, gate_up, preferred_element_type=jnp.float32)
    gate_sums = lax.psum(partial_value.astype(jnp.bfloat16), "mdl").astype(jnp.float32)
    hidden = (jax.nn.silu(gate_sums[0]) * gate_sums[1]).astype(jnp.bfloat16)
    columns = down_weight.reshape(down_weight.shape[0], col_groups * sub_width)
    summed = lax.psum_scatter(
        lax.dot_general(
            columns, hidden, (((0,), (1,)), ((), ())), preferred_element_type=jnp.float32
        ),
        "req",
        scatter_dimension=0,
        tiled=True,
    )
    layer_out = (local_wide + summed.T).astype(jnp.bfloat16)
    return (layer_out, key_value_store)


def solution(mesh):
    return jax.shard_map(
        body,
        mesh=mesh,
        in_specs=(
            P("req"),
            P(),
            P("req", "mdl"),
            P(None, "req", "mdl"),
            P(None, "req", "mdl"),
            P(None, ("req", "mdl")),
            P("mdl", "req"),
            P(),
            P(None, None, "mdl", None, "req"),
            P("req", None, "mdl", None),
        ),
        out_specs=(P(None, ("req", "mdl")), P(None, "req", "mdl")),
        check_vma=False,
    )
```

profile of v0, /device:TPU:6, one launch (start us, length us, event | category | flops | bytes accessed | tf_op | source)
XLA Modules:
  0.0 750.0 jit_solution(8639034000724909317)
XLA Ops:
  7.2 0.0 copy-start
  7.2 0.0 all-gather.5.cloned.1.call-start
  7.2 1.2 copy.84
  8.5 0.7 add_bitcast_fusion
  9.1 0.2 reduce-window.4
  9.3 0.6 reduce_max.18
  10.6 0.6 fusion.37
  16.3 0.7 add_subtract_fusion
  17.0 0.8 fusion.36
  18.0 0.0 copy-start.1
  18.0 0.1 fusion.35
  18.1 0.1 reshape_squeeze.6
  18.2 0.0 copy-start.5
  18.2 0.1 reshape_squeeze.7
  18.5 0.5 copy-done.1
  19.0 1.7 while.14
  19.0 0.1 constant_dynamic-slice_fusion.3
  19.1 0.1 compare_and_fusion.3
  19.2 0.2 fusion.49
  19.4 0.2 fusion.50
  19.6 0.2 fusion.51
  19.8 0.1 constant_dynamic-slice_fusion.3
  19.9 0.1 compare_and_fusion.3
  20.0 0.2 fusion.49
  20.3 0.2 fusion.50
  20.5 0.2 fusion.51
  20.7 0.1 divide_convert_fusion
  20.8 0.6 reshape.134
  21.4 0.0 all-gather.5.cloned.1.call-update
  21.4 0.0 all-gather.7.cloned.1.call-start
  21.5 0.1 copy.34
  21.6 1.3 dynamic-slice
  23.7 2.4 scatter_custom_fusion
  26.2 134.3 %all-gather.5.cloned.1.call-done = bf16[128,4,1024]{2,1,0:T(4,128)(2,1)} async-done(((bf16[1,4,1024]{2,1,0:T(4,128)(2,1)}), bf16[128,4,1024]{2,1,0:T(4,128)(2,1)}) %all-gather.5.cloned.1.call-update) | async-done | bytes 1048592 | tf_op jit(solution)/shard_map/all_gather | solution.py:98
  160.5 1.3 reshape.135
  161.9 0.4 convolution_convert_fusion
  162.3 14.4 %all-reduce = bf16[512,40]{0,1:T(8,128)(2,1)S(1)} all-reduce(bf16[512,40]{0,1:T(8,128)(2,1)S(1)} %convolution_convert_fusion), channel_id=2, replica_groups=mesh['req'=128,'mdl'=4] {'mdl'}, use_global_device_ids=true, to_apply=%region_7.8.clone | all-reduce | flops 20480 | bytes 81920
  176.7 0.1 copy.33
  176.9 1.0 gather_fusion
  177.9 0.1 add_convert_fusion
  178.1 0.7 copy.35
  178.8 0.0 all-gather.7.cloned.1.call-update
  178.8 0.0 all-reduce.5.cloned.1.call-start
  178.9 0.3 reshape.113
  179.2 0.2 dynamic-slice_reduce_fusion
  179.4 0.1 mul.53
  179.6 2.4 copy.36
  182.0 133.8 %all-gather.7.cloned.1.call-done = bf16[128,10,512]{2,1,0:T(8,128)(2,1)} async-done(((bf16[1,10,512]{2,1,0:T(8,128)(2,1)}), bf16[128,10,512]{2,1,0:T(8,128)(2,1)}) %all-gather.7.cloned.1.call-update) | async-done | bytes 1310736 | tf_op jit(solution)/shard_map/all_gather | solution.py:115
  315.8 2.5 reshape.139
  318.3 0.2 multiply_reduce_fusion
  318.6 7.5 psum.14
  326.1 3.2 fusion.21
  329.2 0.0 all-reduce.5.cloned.1.call-update
  329.2 0.0 all-reduce.7.cloned.1.call-start
  329.3 1.0 copy.39
  330.4 0.2 reshape.115
  330.6 53.2 %all-reduce.5.cloned.1.call-done = bf16[2,512,256]{2,1,0:T(8,128)(2,1)} async-done(((bf16[2,512,256]{2,1,0:T(8,128)(2,1)}), bf16[2,512,256]{2,1,0:T(8,128)(2,1)}) %all-reduce.5.cloned.1.call-update) | async-done | bytes 524304 | tf_op jit(solution)/shard_map/psum | solution.py:127
  383.8 1.1 convert_element_type.55
  384.9 2.1 convolution_bitcast_fusion.1
  387.0 0.0 all-reduce.7.cloned.1.call-update
  387.0 1.3 dynamic-slice.2
  388.9 352.7 %all-reduce.7.cloned.1.call-done = f32[1280,512]{0,1:T(8,128)} async-done(((f32[1280,512]{0,1:T(8,128)}), f32[1280,512]{0,1:T(8,128)}) %all-reduce.7.cloned.1.call-update) | async-done | bytes 2621456
  741.6 1.2 fusion.28
  742.8 0.7 copy.40
  (37 shorter events, 0.3 us)
Async XLA Ops:
  7.2 154.7 %copy-start = (bf16[1024,40]{0,1:T(8,128)(2,1)S(1)}, bf16[1024,40]{0,1:T(8,128)(2,1)}, u32[]{:S(2)}) copy-start(bf16[1024,40]{0,1:T(8,128)(2,1)} %param.18) | copy-start | bytes 245764
  7.2 153.3 %all-gather.5.cloned.1.call-start = ((), (), s32[]{:S(2)}) async-start(), calls=%async_computation.1 | async-start | bytes 1056768 | tf_op jit(solution)/shard_map/all_gather | solution.py:98
  8.5 9.9 %copy-start.6 = (bf16[4,1024]{1,0:T(4,128)(2,1)S(1)}, bf16[4,1024]{1,0:T(4,128)(2,1)}, u32[]{:S(2)}) copy-start(bf16[4,1024]{1,0:T(4,128)(2,1)} %param.14) | copy-start | bytes 24580
  18.0 1.0 copy-start.1
  18.2 3.3 copy-start.5
  18.2 5.4 copy-start.7
  21.4 294.4 %all-gather.7.cloned.1.call-start = ((), (), s32[]{:S(2)}) async-start(), calls=%async_computation.2 | async-start | bytes 2113536 | tf_op jit(solution)/shard_map/all_gather | solution.py:115
  161.9 17.0 %copy-start.4 = (f32[5120]{0:T(1024)S(1)}, f32[5120]{0:T(1024)}, u32[]{:S(2)}) copy-start(f32[5120]{0:T(1024)} %param.19) | copy-start | bytes 61444
  161.9 17.7 %copy-start.2 = (bf16[2,128,1,10,256]{4,1,3,2,0:T(8,128)(2,1)S(1)}, bf16[2,128,1,10,256]{4,1,3,2,0:T(8,128)(2,1)}, u32[]{:S(2)}) copy-start(bf16[2,128,1,10,256]{4,1,3,2,0:T(8,128)(2,1)} %param.20) | copy-start | bytes 3932164
  178.8 204.9 %all-reduce.5.cloned.1.call-start = ((), (), s32[]{:S(2)}) async-start(), calls=%async_computation | async-start | bytes 1048576 | tf_op jit(solution)/shard_map/psum | solution.py:127
  326.1 3.2 copy-start.3
  329.2 412.4 %all-reduce.7.cloned.1.call-start = ((), (), s32[]{:S(2)}) async-start(), calls=%async_computation.3 | async-start | bytes 5242880
Sparse Core Ops, SparseCore 0:
  21.5 138.9 all-gather.4
  178.9 136.8 all-gather.6
  329.4 54.3 all-reduce.4
  387.1 354.4 all-reduce.6
where the time goes:
time: 751 us; the launch traced here: 750 us
  waiting for transfers between devices  674 us (90%)
  blocking collectives  21.9 us (3%)
  between operations  21.3 us (3%)
  local copies, waits for them, and re-layouts  20.6 us (3%)
    unnamed x5, waiting for transfers between devices  353 us
    all_gather x1, waiting for transfers between devices, body(): lax.all_gather(attended, 'req', axis=0, tiled=True)  134 us
    all_gather x1, waiting for transfers between devices, body(): gathered = lax.all_gather(residual, 'req', axis=1, tiled=True)  134 us
    psum x1, waiting for transfers between devices, body(): lax.psum(partial_value.astype(jnp.bfloat16), 'mdl').astype(jnp.float32)  53.2 us
  transfers between devices with their start and end apart: 4, of which 4 were waited for; matrix products, arithmetic and copies ran while one was open for 1% of the time, Pallas kernels for 0%

commit v1 on v0

--- a/solution.py
+++ b/solution.py
@@ -1,7 +1,7 @@
 import jax
 import jax.numpy as jnp
 from jax import lax
-from jax.sharding import PartitionSpec as P
+from jax.sharding import Mesh, PartitionSpec as P
 
 D = 5120
 QUERY_HEADS = 32
@@ -10,6 +10,45 @@
 
 
 NEGATIVE_FILL = -1e30
+REQ = ("y", "z", "c")
+
+
+def gather_rows(part):
+    count = lax.axis_size(REQ)
+    copies = jnp.broadcast_to(part[None], (count,) + part.shape)
+    return lax.all_to_all(copies, REQ, 0, 0, tiled=True)
+
+
+def scatter_sum(parts):
+    wide = None
+    for position, name in ((2, "c"), (1, "z"), (0, "y")):
+        moved = lax.all_to_all(parts.astype(jnp.bfloat16), name, position, position, tiled=True)
+        wide = moved.astype(jnp.float32).sum(position, keepdims=True)
+        parts = wide
+    return wide
+
+
+def mdl_sum(value, wire):
+    count = lax.axis_size("mdl")
+    sent = value.astype(wire)
+    total = value.astype(jnp.float32)
+    for shift in range(1, count):
+        pairs = [(i, (i + shift) % count) for i in range(count)]
+        total = total + lax.ppermute(sent, "mdl", pairs).astype(jnp.float32)
+    return total
+
+
+def mdl_scatter_sum(value, wire):
+    count = lax.axis_size("mdl")
+    me = lax.axis_index("mdl")
+    width = value.shape[-1] // count
+    blocks = value.astype(wire).reshape(value.shape[:-1] + (count, width))
+    total = lax.dynamic_index_in_dim(blocks, me, blocks.ndim - 2, keepdims=False).astype(jnp.float32)
+    for shift in range(1, count):
+        pairs = [(i, (i + shift) % count) for i in range(count)]
+        outgoing = lax.dynamic_index_in_dim(blocks, (me + shift) % count, blocks.ndim - 2, keepdims=False)
+        total = total + lax.ppermute(outgoing, "mdl", pairs).astype(jnp.float32)
+    return total
 
 
 def slot_bounds(lengths):
@@ -94,14 +133,9 @@
         .astype(jnp.bfloat16)
         .reshape(slot_count, kv_heads * group_width * HEAD_SIZE)
     )
-    projected = jnp.dot(
-        lax.all_gather(attended, "req", axis=0, tiled=True),
-        out_weight,
-        preferred_element_type=jnp.float32,
-    )
-    head_share = lax.psum_scatter(
-        projected.astype(jnp.bfloat16), "mdl", scatter_dimension=1, tiled=True
-    ).astype(jnp.float32)
+    all_attended = gather_rows(attended).reshape(-1, attended.shape[1])
+    projected = jnp.dot(all_attended, out_weight, preferred_element_type=jnp.float32)
+    head_share = mdl_scatter_sum(projected.astype(jnp.bfloat16), jnp.bfloat16)
     total_rows = assignment.shape[0]
     inverse = (
         jnp.zeros((total_rows,), jnp.int32)
@@ -112,11 +146,11 @@
     residual_wide = hidden_in.astype(jnp.float32) + placed
     residual = residual_wide.astype(jnp.bfloat16)
     local_wide = residual.astype(jnp.float32)
-    gathered = lax.all_gather(residual, "req", axis=1, tiled=True)
-    widened = gathered.astype(jnp.float32)
-    square_sum = lax.psum(jnp.sum(widened * widened, axis=1), "mdl")
     col_groups = gate_up_weight.shape[1]
     sub_width = hidden_in.shape[1]
+    gathered = jnp.transpose(gather_rows(residual), (1, 0, 2)).reshape(total_rows, col_groups * sub_width)
+    widened = gathered.astype(jnp.float32)
+    square_sum = mdl_sum(jnp.sum(widened * widened, axis=1), jnp.float32)
     gain_table = norm_gain.reshape(col_groups, lax.axis_size("mdl"), sub_width)
     gain_cols = lax.dynamic_index_in_dim(
         gain_table, lax.axis_index("mdl"), 1, keepdims=False
@@ -124,37 +158,40 @@
     normed = (widened * lax.rsqrt(square_sum / D + 1e-05)[:, None] * gain_cols).astype(jnp.bfloat16)
     gate_up = gate_up_weight.reshape(2, col_groups * sub_width, gate_up_weight.shape[4])
     partial_value = jnp.einsum("rk,gkf->grf", normed, gate_up, preferred_element_type=jnp.float32)
-    gate_sums = lax.psum(partial_value.astype(jnp.bfloat16), "mdl").astype(jnp.float32)
+    gate_sums = mdl_sum(partial_value, jnp.bfloat16)
     hidden = (jax.nn.silu(gate_sums[0]) * gate_sums[1]).astype(jnp.bfloat16)
     columns = down_weight.reshape(down_weight.shape[0], col_groups * sub_width)
-    summed = lax.psum_scatter(
-        lax.dot_general(
-            columns, hidden, (((0,), (1,)), ((), ())), preferred_element_type=jnp.float32
-        ),
-        "req",
-        scatter_dimension=0,
-        tiled=True,
+    lowered = lax.dot_general(
+        columns, hidden, (((0,), (1,)), ((), ())), preferred_element_type=jnp.float32
     )
+    mesh_shape = (lax.axis_size("y"), lax.axis_size("z"), lax.axis_size("c"))
+    summed = scatter_sum(lowered.reshape(mesh_shape + (sub_width, total_rows))).reshape(sub_width, total_rows)
     layer_out = (local_wide + summed.T).astype(jnp.bfloat16)
     return (layer_out, key_value_store)
 
 
 def solution(mesh):
+    req_size, mdl_size = mesh.devices.shape
+    chips_y = 4
+    split = Mesh(
+        mesh.devices.reshape(chips_y, req_size // (2 * chips_y), 2, mdl_size),
+        REQ + ("mdl",),
+    )
     return jax.shard_map(
         body,
-        mesh=mesh,
+        mesh=split,
         in_specs=(
-            P("req"),
+            P(REQ),
             P(),
-            P("req", "mdl"),
-            P(None, "req", "mdl"),
-            P(None, "req", "mdl"),
-            P(None, ("req", "mdl")),
-            P("mdl", "req"),
+            P(REQ, "mdl"),
+            P(None, REQ, "mdl"),
+            P(None, REQ, "mdl"),
+            P(None, (REQ + ("mdl",))),
+            P("mdl", REQ),
             P(),
-            P(None, None, "mdl", None, "req"),
-            P("req", None, "mdl", None),
+            P(None, None, "mdl", None, REQ),
+            P(REQ, None, "mdl", None),
         ),
-        out_specs=(P(None, ("req", "mdl")), P(None, "req", "mdl")),
+        out_specs=(P(None, REQ + ("mdl",)), P(None, REQ, "mdl")),
         check_vma=False,
     )

time: 751 us -> 331 us (0.44)
  waiting for transfers between devices: 674 us -> 177 us
  starting transfers between devices: 0.16 us -> 58.1 us
  blocking collectives: 21.9 us -> 55.4 us
  between operations: 21.3 us -> 6.93 us
    unnamed x5 -> x0, waiting for transfers between devices: 353 us -> none
    all_gather x2 -> x0, waiting for transfers between devices: 268 us -> none  [the longest x1 134 us: body(): lax.all_gather(attended, 'req', axis=0, tiled=True)]
    all_to_all x0 -> x2, waiting for transfers between devices: none -> 151 us  [gather_rows(): return lax.all_to_all(copies, REQ, 0, 0, tiled=True)]
    all_to_all x0 -> x3, blocking collectives: none -> 55.4 us  [scatter_sum(): lax.all_to_all(parts.astype(jnp.bfloat16), name, position, position, tile...]
    psum x1 -> x0, waiting for transfers between devices: 53.2 us -> none  [body(): lax.psum(partial_value.astype(jnp.bfloat16), 'mdl').astype(jnp.float32)]
    all_to_all x0 -> x2, starting transfers between devices: none -> 30.5 us  [gather_rows(): return lax.all_to_all(copies, REQ, 0, 0, tiled=True)]
    ppermute x0 -> x9, starting transfers between devices: none -> 27.5 us  [the longest x6 18.9 us: mdl_sum(): total = total + lax.ppermute(sent, 'mdl', pairs).astype(jnp.float32)]
    ppermute x0 -> x9, waiting for transfers between devices: none -> 26.1 us  [the longest x6 20.3 us: mdl_sum(): total = total + lax.ppermute(sent, 'mdl', pairs).astype(jnp.float32)]
  transfers between devices with their start and end apart: 4 -> 11, of which waited for: 4 -> 7; matrix products, arithmetic and copies ran while one was open for 1% -> 3% of each run, Pallas kernels for 0% -> 0%
where the time goes in v1:
time: 331 us; the launch traced here: 330 us
  waiting for transfers between devices  177 us (53%)
  starting transfers between devices  58.1 us (18%)
  blocking collectives  55.4 us (17%)
  local copies, waits for them, and re-layouts  21.8 us (7%)
  between operations  6.93 us (2%)
  other arithmetic  6.34 us (2%)
  matrix products  3.88 us (1%)
    all_to_all x2, waiting for transfers between devices, gather_rows(): return lax.all_to_all(copies, REQ, 0, 0, tiled=True)  151 us
    all_to_all x3, blocking collectives, scatter_sum(): lax.all_to_all(parts.astype(jnp.bfloat16), name, position, position, tile...  55.4 us
    all_to_all x2, starting transfers between devices, gather_rows(): return lax.all_to_all(copies, REQ, 0, 0, tiled=True)  30.5 us
    ppermute x6, waiting for transfers between devices, mdl_sum(): total = total + lax.ppermute(sent, 'mdl', pairs).astype(jnp.float32)  20.3 us
    ppermute x6, starting transfers between devices, mdl_sum(): total = total + lax.ppermute(sent, 'mdl', pairs).astype(jnp.float32)  18.9 us
    ppermute x3, starting transfers between devices, mdl_scatter_sum(): total = total + lax.ppermute(outgoing, 'mdl', pairs).astype(jnp.float32)  8.62 us
  transfers between devices with their start and end apart: 11, of which 7 were waited for; matrix products, arithmetic and copies ran while one was open for 3% of the time, Pallas kernels for 0%

profile of v1, /device:TPU:6, one launch (start us, length us, event | category | flops | bytes accessed | tf_op | source)
XLA Modules:
  0.0 329.6 jit_solution(7796887166953461305)
XLA Ops:
  0.7 0.7 copy-done.14
  1.3 0.2 reduce-window.4
  1.5 0.6 reduce_max.18
  2.8 0.6 fusion.29
  9.0 0.6 copy-done.1
  9.7 1.7 while.14
  10.0 0.2 fusion.42
  10.2 0.2 fusion.43
  10.4 0.2 fusion.44
  10.8 0.2 fusion.42
  11.1 0.2 fusion.43
  11.3 0.2 fusion.44
  11.6 1.2 broadcast_in_dim.72
  12.9 23.2 %all-to-all-start = ((bf16[128,4,1024]{2,1,0:T(4,128)(2,1)}), bf16[128,4,1024]{2,1,0:T(4,128)(2,1)S(1)}, u32[]{:S(2)}, u32[]{:S(2)}) async-start(bf16[128,4,1024]{2,1,0:T(4,128)(2,1)} %broadcast_in_dim.72), calls=%async_computation | async-start | bytes 2097152 | tf_op jit(solution)/shard_map/all_to_all | solution.py:19
  36.2 2.4 scatter_custom_fusion
  38.7 53.1 %all-to-all-done = bf16[128,4,1024]{2,1,0:T(4,128)(2,1)S(1)} async-done(((bf16[128,4,1024]{2,1,0:T(4,128)(2,1)}), bf16[128,4,1024]{2,1,0:T(4,128)(2,1)S(1)}, u32[]{:S(2)}, u32[]{:S(2)}) %all-to-all-start) | async-done | bytes 1048608 | tf_op jit(solution)/shard_map/all_to_all | solution.py:19
  91.7 0.3 reshape.156
  92.0 0.4 convolution_convert_fusion.1
  92.5 0.2 copy.58
  92.7 2.4 collective-permute-start
  95.1 0.2 copy.59
  95.2 4.3 %collective-permute-start.1 = (bf16[512,10]{1,0:T(8,128)(2,1)S(1)}, bf16[512,10]{1,0:T(8,128)(2,1)S(1)}, u32[]{:S(2)}, u32[]{:S(2)}) collective-permute-start(bf16[512,10]{1,0:T(8,128)(2,1)S(1)} %bitcast.106), channel_id=1, source_target_pairs={{0,2},{1,3},{2,0},{3,1},{4,6},{5,7},{6,4},{7,5},{8,10},{9,11},{10,... | collective-permute-start | bytes 30728 | tf_op jit(solution)/shard_map/ppermute | solution.py:50
  99.5 0.2 copy.60
  99.7 1.9 collective-permute-start.2
  101.6 0.1 copy.61
  101.8 0.2 copy.79
  101.9 2.0 collective-permute-done.1
  104.0 3.8 %collective-permute-done.2 = bf16[512,10]{1,0:T(8,128)(2,1)S(1)} collective-permute-done((bf16[512,10]{1,0:T(8,128)(2,1)S(1)}, bf16[512,10]{1,0:T(8,128)(2,1)S(1)}, u32[]{:S(2)}, u32[]{:S(2)}) %collective-permute-start.2) | collective-permute-done | bytes 10272 | tf_op jit(solution)/shard_map/ppermute | solution.py:50
  107.8 1.0 gather_fusion
  108.9 0.1 add_convert_fusion
  109.1 1.6 broadcast_in_dim.75
  110.7 7.3 %all-to-all-start.1 = ((bf16[128,512,10]{1,2,0:T(8,128)(2,1)}), bf16[128,512,10]{1,2,0:T(8,128)(2,1)S(1)}, u32[]{:S(2)}, u32[]{:S(2)}) async-start(bf16[128,512,10]{1,2,0:T(8,128)(2,1)} %broadcast_in_dim.75), calls=%async_computation.1 | async-start | bytes 4194304 | tf_op jit(solution)/shard_map/all_to_all | solution.py:19
  118.1 1.0 reshape.158
  119.1 97.8 %all-to-all-done.1 = bf16[128,512,10]{1,2,0:T(8,128)(2,1)S(1)} async-done(((bf16[128,512,10]{1,2,0:T(8,128)(2,1)}), bf16[128,512,10]{1,2,0:T(8,128)(2,1)S(1)}, u32[]{:S(2)}, u32[]{:S(2)}) %all-to-all-start.1) | async-done | bytes 1310752 | tf_op jit(solution)/shard_map/all_to_all | solution.py:19
  216.9 0.6 fusion.10
  217.4 2.5 collective-permute-start.3
  219.9 2.9 collective-permute-start.4
  222.9 2.8 collective-permute-start.5
  225.7 1.0 constant_dynamic-slice_fusion.2
  226.7 2.4 copy.63
  229.2 0.4 collective-permute-done.5
  229.6 1.9 fusion.14
  231.4 2.7 convert_element_type.120
  234.1 2.0 fusion.30
  236.2 4.1 %collective-permute-start.6 = (bf16[2,512,256]{2,1,0:T(8,128)(2,1)}, bf16[2,512,256]{2,1,0:T(8,128)(2,1)}, u32[]{:S(2)}, u32[]{:S(2)}) collective-permute-start(bf16[2,512,256]{2,1,0:T(8,128)(2,1)} %get-tuple-element.146), channel_id=1, source_target_pairs={{0,1},{1,2},{2,3},{3,0},{4,5},{5,6},{6,7},{7,4},{8,9},{9,10},{10,1... | collective-permute-start | bytes 1572872 | tf_op jit(solution)/shard_map/ppermute | solution.py:37
  240.3 3.2 collective-permute-start.7
  243.6 3.3 %collective-permute-start.8 = (bf16[2,512,256]{2,1,0:T(8,128)(2,1)}, bf16[2,512,256]{2,1,0:T(8,128)(2,1)}, u32[]{:S(2)}, u32[]{:S(2)}) collective-permute-start(bf16[2,512,256]{2,1,0:T(8,128)(2,1)} %get-tuple-element.146), channel_id=1, source_target_pairs={{0,3},{1,0},{2,1},{3,2},{4,7},{5,4},{6,5},{7,6},{8,11},{9,8},{10,9... | collective-permute-start | bytes 1572872 | tf_op jit(solution)/shard_map/ppermute | solution.py:37
  246.9 1.0 copy.66
  248.0 0.2 reshape.160
  248.2 14.3 %collective-permute-done.6 = bf16[2,512,256]{2,1,0:T(8,128)(2,1)} collective-permute-done((bf16[2,512,256]{2,1,0:T(8,128)(2,1)}, bf16[2,512,256]{2,1,0:T(8,128)(2,1)}, u32[]{:S(2)}, u32[]{:S(2)}) %collective-permute-start.6) | collective-permute-done | bytes 524320 | tf_op jit(solution)/shard_map/ppermute | solution.py:37
  262.5 5.6 %collective-permute-done.8 = bf16[2,512,256]{2,1,0:T(8,128)(2,1)} collective-permute-done((bf16[2,512,256]{2,1,0:T(8,128)(2,1)}, bf16[2,512,256]{2,1,0:T(8,128)(2,1)}, u32[]{:S(2)}, u32[]{:S(2)}) %collective-permute-start.8) | collective-permute-done | bytes 524320 | tf_op jit(solution)/shard_map/ppermute | solution.py:37
  268.0 1.6 convert_add_fusion
  269.6 0.6 fusion.13
  270.2 0.7 copy.67
  270.9 0.5 convert_element_type.129
  271.3 0.8 copy.68
  272.1 4.8 %all_to_all.25 = bf16[4,16,2,10,512]{4,1,3,0,2:T(8,128)(2,1)S(1)} all-to-all(bf16[4,16,2,10,512]{4,1,3,0,2:T(8,128)(2,1)S(1)} %copy.68), channel_id=1, replica_groups=mesh['y'=4,'z'=16,'c'=2,'mdl'=4] {'c'}, dimensions={2} | all-to-all | bytes 2621440 | tf_op jit(solution)/shard_map/all_to_all | solution.py:25
  276.9 0.3 reduce_sum.52
  277.2 0.5 copy.69
  277.8 42.0 %all_to_all.26 = bf16[4,16,1,10,512]{4,0,3,2,1:T(4,128)(2,1)S(1)} all-to-all(bf16[4,16,1,10,512]{4,0,3,2,1:T(4,128)(2,1)S(1)} %copy.69), channel_id=1, replica_groups=mesh['y'=4,'z'=16,'c'=2,'mdl'=4] {'z'}, dimensions={1} | all-to-all | bytes 1310720 | tf_op jit(solution)/shard_map/all_to_all | solution.py:25
  319.7 0.3 reduce_sum.53
  320.0 8.6 %all_to_all.27 = bf16[4,1,1,10,512]{4,3,2,1,0:T(8,128)(2,1)S(1)} all-to-all(bf16[4,1,1,10,512]{4,3,2,1,0:T(8,128)(2,1)S(1)} %copy.70), channel_id=1, replica_groups=mesh['y'=4,'z'=16,'c'=2,'mdl'=4] {'y'}, dimensions={0} | all-to-all | bytes 81920 | tf_op jit(solution)/shard_map/all_to_all | solution.py:25
  328.6 0.1 copy.71
  328.8 0.7 copy.72
  (75 shorter events, 1.4 us)
Async XLA Ops:
  0.6 91.4 %copy-start = (bf16[1024,40]{0,1:T(8,128)(2,1)S(1)}, bf16[1024,40]{0,1:T(8,128)(2,1)}, u32[]{:S(2)}) copy-start(bf16[1024,40]{0,1:T(8,128)(2,1)} %param.18) | copy-start | bytes 245764
  0.6 0.7 copy-start.14
  0.7 7.8 %copy-start.11 = (bf16[2,4,256]{2,1,0:T(4,128)(2,1)S(1)}, bf16[2,4,256]{2,1,0:T(4,128)(2,1)}, u32[]{:S(2)}) copy-start(bf16[2,4,256]{2,1,0:T(4,128)(2,1)} %param.15) | copy-start | bytes 12292
  0.7 7.9 %copy-start.2 = (bf16[2,1024,256]{2,1,0:T(8,128)(2,1)S(1)}, bf16[2,1024,256]{2,1,0:T(8,128)(2,1)}, u32[]{:S(2)}) copy-start(bf16[2,1024,256]{2,1,0:T(8,128)(2,1)} %param.16) | copy-start | bytes 3145732
  8.7 1.0 copy-start.1
  8.7 1.0 copy-start.12
  11.5 24.7 %copy-start.13 = (s32[512]{0:T(512)S(1)}, s32[512]{0:T(512)}, u32[]{:S(2)}) copy-start(s32[512]{0:T(512)} %param.13) | copy-start | bytes 6148
  12.9 78.9 %all-to-all-start = ((bf16[128,4,1024]{2,1,0:T(4,128)(2,1)}), bf16[128,4,1024]{2,1,0:T(4,128)(2,1)S(1)}, u32[]{:S(2)}, u32[]{:S(2)}) async-start(bf16[128,4,1024]{2,1,0:T(4,128)(2,1)} %broadcast_in_dim.72), calls=%async_computation | async-start | bytes 2097152 | tf_op jit(solution)/shard_map/all_to_all | solution.py:19
  36.1 65.5 %copy-start.10 = (bf16[512,10]{0,1:T(8,128)(2,1)S(1)}, bf16[512,10]{0,1:T(8,128)(2,1)}, u32[]{:S(2)}) copy-start(bf16[512,10]{0,1:T(8,128)(2,1)} %param.17) | copy-start | bytes 30724
  92.7 9.3 %collective-permute-start = (bf16[512,10]{1,0:T(8,128)(2,1)S(1)}, bf16[512,10]{1,0:T(8,128)(2,1)S(1)}, u32[]{:S(2)}, u32[]{:S(2)}) collective-permute-start(bf16[512,10]{1,0:T(8,128)(2,1)S(1)} %bitcast.105), channel_id=1, source_target_pairs={{0,1},{1,2},{2,3},{3,0},{4,5},{5,6},{6,7},{7,4},{8,9},{9,10},{10,1... | collective-permute-start | bytes 30728 | tf_op jit(solution)/shard_map/ppermute | solution.py:50
  95.2 8.8 %collective-permute-start.1 = (bf16[512,10]{1,0:T(8,128)(2,1)S(1)}, bf16[512,10]{1,0:T(8,128)(2,1)S(1)}, u32[]{:S(2)}, u32[]{:S(2)}) collective-permute-start(bf16[512,10]{1,0:T(8,128)(2,1)S(1)} %bitcast.106), channel_id=1, source_target_pairs={{0,2},{1,3},{2,0},{3,1},{4,6},{5,7},{6,4},{7,5},{8,10},{9,11},{10,... | collective-permute-start | bytes 30728 | tf_op jit(solution)/shard_map/ppermute | solution.py:50
  99.7 8.1 %collective-permute-start.2 = (bf16[512,10]{1,0:T(8,128)(2,1)S(1)}, bf16[512,10]{1,0:T(8,128)(2,1)S(1)}, u32[]{:S(2)}, u32[]{:S(2)}) collective-permute-start(bf16[512,10]{1,0:T(8,128)(2,1)S(1)} %bitcast.107), channel_id=1, source_target_pairs={{0,3},{1,0},{2,1},{3,2},{4,7},{5,4},{6,5},{7,6},{8,11},{9,8},{10,9... | collective-permute-start | bytes 30728 | tf_op jit(solution)/shard_map/ppermute | solution.py:50
  109.0 1.7 copy-start.5
  110.7 7.3 %copy-start.9 = (f32[5120]{0:T(1024)S(1)}, f32[5120]{0:T(1024)}, u32[]{:S(2)}) copy-start(f32[5120]{0:T(1024)} %param.19) | copy-start | bytes 61444
  110.7 106.2 %all-to-all-start.1 = ((bf16[128,512,10]{1,2,0:T(8,128)(2,1)}), bf16[128,512,10]{1,2,0:T(8,128)(2,1)S(1)}, u32[]{:S(2)}, u32[]{:S(2)}) async-start(bf16[128,512,10]{1,2,0:T(8,128)(2,1)} %broadcast_in_dim.75), calls=%async_computation.1 | async-start | bytes 4194304 | tf_op jit(solution)/shard_map/all_to_all | solution.py:19
  118.1 108.7 %copy-start.3 = (bf16[2,128,1,10,256]{4,1,3,2,0:T(8,128)(2,1)S(1)}, bf16[2,128,1,10,256]{4,1,3,2,0:T(8,128)(2,1)}, u32[]{:S(2)}) copy-start(bf16[2,128,1,10,256]{4,1,3,2,0:T(8,128)(2,1)} %param.20) | copy-start | bytes 3932164
  217.4 11.7 %collective-permute-start.3 = (f32[512]{0:T(512)S(1)}, f32[512]{0:T(512)S(1)}, u32[]{:S(2)}, u32[]{:S(2)}) collective-permute-start(f32[512]{0:T(512)S(1)} %fusion.10), channel_id=1, source_target_pairs={{0,1},{1,2},{2,3},{3,0},{4,5},{5,6},{6,7},{7,4},{8,9},{9,10},{10,1... | collective-permute-start | bytes 6152 | tf_op jit(solution)/shard_map/ppermute | solution.py:37
  219.9 9.2 %collective-permute-start.4 = (f32[512]{0:T(512)S(1)}, f32[512]{0:T(512)S(1)}, u32[]{:S(2)}, u32[]{:S(2)}) collective-permute-start(f32[512]{0:T(512)S(1)} %fusion.10), channel_id=1, source_target_pairs={{0,2},{1,3},{2,0},{3,1},{4,6},{5,7},{6,4},{7,5},{8,10},{9,11},{10,... | collective-permute-start | bytes 6152 | tf_op jit(solution)/shard_map/ppermute | solution.py:37
  222.9 6.7 %collective-permute-start.5 = (f32[512]{0:T(512)S(1)}, f32[512]{0:T(512)S(1)}, u32[]{:S(2)}, u32[]{:S(2)}) collective-permute-start(f32[512]{0:T(512)S(1)} %fusion.10), channel_id=1, source_target_pairs={{0,3},{1,0},{2,1},{3,2},{4,7},{5,4},{6,5},{7,6},{8,11},{9,8},{10,9... | collective-permute-start | bytes 6152 | tf_op jit(solution)/shard_map/ppermute | solution.py:37
  231.4 2.7 copy-start.4
  234.1 12.8 %copy-start.8 = (bf16[256,128,1,10]{1,0,3,2:T(8,128)(2,1)S(1)}, bf16[256,128,1,10]{1,0,3,2:T(8,128)(2,1)}, u32[]{:S(2)}) copy-start(bf16[256,128,1,10]{1,0,3,2:T(8,128)(2,1)} %param.21) | copy-start | bytes 1966084
  236.2 31.9 %copy-start.7 = (f32[2,512,256]{2,1,0:T(8,128)S(1)}, f32[2,512,256]{2,1,0:T(8,128)}, u32[]{:S(2)}) copy-start(f32[2,512,256]{2,1,0:T(8,128)} %get-tuple-element.147) | copy-start | bytes 3145732
  236.2 26.3 %collective-permute-start.6 = (bf16[2,512,256]{2,1,0:T(8,128)(2,1)}, bf16[2,512,256]{2,1,0:T(8,128)(2,1)}, u32[]{:S(2)}, u32[]{:S(2)}) collective-permute-start(bf16[2,512,256]{2,1,0:T(8,128)(2,1)} %get-tuple-element.146), channel_id=1, source_target_pairs={{0,1},{1,2},{2,3},{3,0},{4,5},{5,6},{6,7},{7,4},{8,9},{9,10},{10,1... | collective-permute-start | bytes 1572872 | tf_op jit(solution)/shard_map/ppermute | solution.py:37
  240.3 22.1 %collective-permute-start.7 = (bf16[2,512,256]{2,1,0:T(8,128)(2,1)}, bf16[2,512,256]{2,1,0:T(8,128)(2,1)}, u32[]{:S(2)}, u32[]{:S(2)}) collective-permute-start(bf16[2,512,256]{2,1,0:T(8,128)(2,1)} %get-tuple-element.146), channel_id=1, source_target_pairs={{0,2},{1,3},{2,0},{3,1},{4,6},{5,7},{6,4},{7,5},{8,10},{9,11},{10,... | collective-permute-start | bytes 1572872 | tf_op jit(solution)/shard_map/ppermute | solution.py:37
  243.6 24.5 %collective-permute-start.8 = (bf16[2,512,256]{2,1,0:T(8,128)(2,1)}, bf16[2,512,256]{2,1,0:T(8,128)(2,1)}, u32[]{:S(2)}, u32[]{:S(2)}) collective-permute-start(bf16[2,512,256]{2,1,0:T(8,128)(2,1)} %get-tuple-element.146), channel_id=1, source_target_pairs={{0,3},{1,0},{2,1},{3,2},{4,7},{5,4},{6,5},{7,6},{8,11},{9,8},{10,9... | collective-permute-start | bytes 1572872 | tf_op jit(solution)/shard_map/ppermute | solution.py:37
  277.2 51.6 %copy-start.6 = (bf16[512,10]{1,0:T(8,128)(2,1)S(1)}, bf16[512,10]{1,0:T(8,128)(2,1)}, u32[]{:S(2)}) copy-start(bf16[512,10]{1,0:T(8,128)(2,1)} %copy-done.5) | copy-start | bytes 30724

commit v2 on v1

--- a/solution.py
+++ b/solution.py
@@ -15,13 +15,14 @@
 
 def gather_rows(part):
     count = lax.axis_size(REQ)
-    copies = jnp.broadcast_to(part[None], (count,) + part.shape)
-    return lax.all_to_all(copies, REQ, 0, 0, tiled=True)
+    flat = part.reshape(-1, 128)
+    copies = jnp.broadcast_to(flat[None], (count,) + flat.shape)
+    return lax.all_to_all(copies, REQ, 0, 0, tiled=True).reshape((count,) + part.shape)
 
 
 def scatter_sum(parts):
     wide = None
-    for position, name in ((2, "c"), (1, "z"), (0, "y")):
+    for position, name in ((2, "c"), (0, "y"), (1, "z")):
         moved = lax.all_to_all(parts.astype(jnp.bfloat16), name, position, position, tiled=True)
         wide = moved.astype(jnp.float32).sum(position, keepdims=True)
         parts = wide
@@ -41,14 +42,14 @@
 def mdl_scatter_sum(value, wire):
     count = lax.axis_size("mdl")
     me = lax.axis_index("mdl")
-    width = value.shape[-1] // count
-    blocks = value.astype(wire).reshape(value.shape[:-1] + (count, width))
-    total = lax.dynamic_index_in_dim(blocks, me, blocks.ndim - 2, keepdims=False).astype(jnp.float32)
+    height = value.shape[0] // count
+    blocks = value.astype(wire).reshape((count, height * value.shape[1] // 128, 128))
+    total = lax.dynamic_index_in_dim(blocks, me, 0, keepdims=False).astype(jnp.float32)
     for shift in range(1, count):
         pairs = [(i, (i + shift) % count) for i in range(count)]
-        outgoing = lax.dynamic_index_in_dim(blocks, (me + shift) % count, blocks.ndim - 2, keepdims=False)
+        outgoing = lax.dynamic_index_in_dim(blocks, (me + shift) % count, 0, keepdims=False)
         total = total + lax.ppermute(outgoing, "mdl", pairs).astype(jnp.float32)
-    return total
+    return total.reshape(height, value.shape[1])
 
 
 def slot_bounds(lengths):
@@ -135,7 +136,7 @@
     )
     all_attended = gather_rows(attended).reshape(-1, attended.shape[1])
     projected = jnp.dot(all_attended, out_weight, preferred_element_type=jnp.float32)
-    head_share = mdl_scatter_sum(projected.astype(jnp.bfloat16), jnp.bfloat16)
+    head_share = mdl_scatter_sum(projected.T, jnp.bfloat16).T
     total_rows = assignment.shape[0]
     inverse = (
         jnp.zeros((total_rows,), jnp.int32)
@@ -148,7 +149,7 @@
     local_wide = residual.astype(jnp.float32)
     col_groups = gate_up_weight.shape[1]
     sub_width = hidden_in.shape[1]
-    gathered = jnp.transpose(gather_rows(residual), (1, 0, 2)).reshape(total_rows, col_groups * sub_width)
+    gathered = jnp.transpose(gather_rows(residual.T), (2, 0, 1)).reshape(total_rows, col_groups * sub_width)
     widened = gathered.astype(jnp.float32)
     square_sum = mdl_sum(jnp.sum(widened * widened, axis=1), jnp.float32)
     gain_table = norm_gain.reshape(col_groups, lax.axis_size("mdl"), sub_width)
@@ -165,7 +166,7 @@
         columns, hidden, (((0,), (1,)), ((), ())), preferred_element_type=jnp.float32
     )
     mesh_shape = (lax.axis_size("y"), lax.axis_size("z"), lax.axis_size("c"))
-    summed = scatter_sum(lowered.reshape(mesh_shape + (sub_width, total_rows))).reshape(sub_width, total_rows)
+    summed = scatter_sum(lowered.reshape(mesh_shape + (sub_width * total_rows // 128, 128))).reshape(sub_width, total_rows)
     layer_out = (local_wide + summed.T).astype(jnp.bfloat16)
     return (layer_out, key_value_store)
 

time: 331 us -> 280 us (0.85)
  waiting for transfers between devices: 177 us -> 143 us
  blocking collectives: 55.4 us -> 39 us
    all_to_all x2, waiting for transfers between devices: 151 us -> 119 us  [gather_rows(): lax.all_to_all(copies, REQ, 0, 0, tiled=True).reshape((count,) + part.shape)]
    all_to_all x3, blocking collectives: 55.4 us -> 39 us  [scatter_sum(): lax.all_to_all(parts.astype(jnp.bfloat16), name, position, position, tile...]
    unnamed x34 -> x29, local copies, waits for them, and re-layouts: 5.68 us -> 6.87 us
where the time goes in v2:
time: 280 us; the launch traced here: 279 us
  waiting for transfers between devices  143 us (51%)
  starting transfers between devices  58.2 us (21%)
  blocking collectives  39 us (14%)
  local copies, waits for them, and re-layouts  22.1 us (8%)
  between operations  6.96 us (2%)
  matrix products  4.84 us (2%)
  other arithmetic  4.56 us (2%)
    all_to_all x2, waiting for transfers between devices, gather_rows(): lax.all_to_all(copies, REQ, 0, 0, tiled=True).reshape((count,) + part.shape)  119 us
    all_to_all x3, blocking collectives, scatter_sum(): lax.all_to_all(parts.astype(jnp.bfloat16), name, position, position, tile...  39 us
    all_to_all x2, starting transfers between devices, gather_rows(): lax.all_to_all(copies, REQ, 0, 0, tiled=True).reshape((count,) + part.shape)  31.7 us
    ppermute x6, waiting for transfers between devices, mdl_sum(): total = total + lax.ppermute(sent, 'mdl', pairs).astype(jnp.float32)  19.5 us
    ppermute x6, starting transfers between devices, mdl_sum(): total = total + lax.ppermute(sent, 'mdl', pairs).astype(jnp.float32)  17.9 us
    ppermute x3, starting transfers between devices, mdl_scatter_sum(): total = total + lax.ppermute(outgoing, 'mdl', pairs).astype(jnp.float32)  8.63 us
    unnamed x29, local copies, waits for them, and re-layouts  6.87 us
  transfers between devices with their start and end apart: 11, of which 7 were waited for; matrix products, arithmetic and copies ran while one was open for 3% of the time, Pallas kernels for 0%

profile of v2, /device:TPU:6, one launch (start us, length us, event | category | flops | bytes accessed | tf_op | source)
XLA Modules:
  0.0 278.9 jit_solution(15982702122101734164)
XLA Ops:
  0.7 0.7 copy-done.12
  1.3 0.2 reduce-window.4
  1.5 0.6 reduce_max.18
  2.8 0.6 fusion.30
  8.7 0.1 reshape_squeeze.6
  8.9 0.7 copy-done.1
  9.6 0.1 reshape_squeeze.7
  9.8 1.7 while.14
  10.0 0.2 fusion.43
  10.3 0.2 fusion.44
  10.5 0.2 fusion.45
  10.9 0.2 fusion.43
  11.1 0.2 fusion.44
  11.3 0.2 fusion.45
  11.7 1.1 broadcast_in_dim.73
  12.8 24.4 %all-to-all-start = ((bf16[128,32,128]{2,1,0:T(8,128)(2,1)}), bf16[128,32,128]{2,1,0:T(8,128)(2,1)S(1)}, u32[]{:S(2)}, u32[]{:S(2)}) async-start(bf16[128,32,128]{2,1,0:T(8,128)(2,1)} %broadcast_in_dim.73), calls=%async_computation | async-start | bytes 2097152 | tf_op jit(solution)/shard_map/all_to_all | solution.py:20
  37.3 2.4 scatter_custom_fusion
  39.8 53.1 %all-to-all-done = bf16[128,32,128]{2,1,0:T(8,128)(2,1)S(1)} async-done(((bf16[128,32,128]{2,1,0:T(8,128)(2,1)}), bf16[128,32,128]{2,1,0:T(8,128)(2,1)S(1)}, u32[]{:S(2)}, u32[]{:S(2)}) %all-to-all-start) | async-done | bytes 1048608 | tf_op jit(solution)/shard_map/all_to_all | solution.py:20
  92.9 0.5 reshape_reshape.3
  93.4 0.4 fusion.17
  93.9 2.4 collective-permute-start
  96.2 4.3 %collective-permute-start.1 = (bf16[40,128]{1,0:T(8,128)(2,1)S(1)}, bf16[40,128]{1,0:T(8,128)(2,1)S(1)}, u32[]{:S(2)}, u32[]{:S(2)}) collective-permute-start(bf16[40,128]{1,0:T(8,128)(2,1)S(1)} %get-tuple-element.136), channel_id=1, source_target_pairs={{0,2},{1,3},{2,0},{3,1},{4,6},{5,7},{6,4},{7,5},{8,10},{9,11},{10,... | collective-permute-start | bytes 30728 | tf_op jit(solution)/shard_map/ppermute | solution.py:51
  100.6 1.9 collective-permute-start.2
  102.5 0.1 copy.52
  102.7 0.6 collective-permute-done.1
  103.3 4.0 %collective-permute-done.2 = bf16[40,128]{1,0:T(8,128)(2,1)S(1)} collective-permute-done((bf16[40,128]{1,0:T(8,128)(2,1)S(1)}, bf16[40,128]{1,0:T(8,128)(2,1)S(1)}, u32[]{:S(2)}, u32[]{:S(2)}) %collective-permute-start.2) | collective-permute-done | bytes 10272 | tf_op jit(solution)/shard_map/ppermute | solution.py:51
  107.4 0.1 copy.51
  107.5 1.0 gather_fusion
  108.6 0.1 add_convert_fusion
  108.7 0.1 copy.53
  108.9 1.3 broadcast_in_dim.77
  110.1 7.3 %all-to-all-start.1 = ((bf16[128,40,128]{2,1,0:T(8,128)(2,1)}), bf16[128,40,128]{2,1,0:T(8,128)(2,1)S(1)}, u32[]{:S(2)}, u32[]{:S(2)}) async-start(bf16[128,40,128]{2,1,0:T(8,128)(2,1)} %broadcast_in_dim.77), calls=%async_computation.1 | async-start | bytes 2621440 | tf_op jit(solution)/shard_map/all_to_all | solution.py:20
  117.5 0.3 reshape.161
  117.8 65.8 %all-to-all-done.1 = bf16[128,40,128]{2,1,0:T(8,128)(2,1)S(1)} async-done(((bf16[128,40,128]{2,1,0:T(8,128)(2,1)}), bf16[128,40,128]{2,1,0:T(8,128)(2,1)S(1)}, u32[]{:S(2)}, u32[]{:S(2)}) %all-to-all-start.1) | async-done | bytes 1310752 | tf_op jit(solution)/shard_map/all_to_all | solution.py:20
  183.6 1.4 copy.54
  185.0 0.3 fusion.11
  185.3 2.6 collective-permute-start.3
  187.9 2.2 collective-permute-start.4
  190.1 3.3 %collective-permute-start.5 = (f32[512]{0:T(512)S(1)}, f32[512]{0:T(512)S(1)}, u32[]{:S(2)}, u32[]{:S(2)}) collective-permute-start(f32[512]{0:T(512)S(1)} %fusion.11), channel_id=1, source_target_pairs={{0,3},{1,0},{2,1},{3,2},{4,7},{5,4},{6,5},{7,6},{8,11},{9,8},{10,9... | collective-permute-start | bytes 6152 | tf_op jit(solution)/shard_map/ppermute | solution.py:38
  193.5 2.4 copy.57
  196.0 1.5 collective-permute-done.5
  197.4 0.4 fusion.14
  197.9 2.1 copy.56
  200.0 1.3 convert_element_type.128
  201.3 0.3 copy-done.4
  201.6 3.0 %fusion.31 = (bf16[2,512,256]{2,1,0:T(8,128)(2,1)}, f32[2,512,256]{2,1,0:T(8,128)S(1)}) fusion(bf16[2,1280,256]{2,0,1:T(2,128)(2,1)S(1)} %bitcast.113, bf16[512,1280]{0,1:T(8,128)(2,1)} %convert_element_type.128), kind=kOutput, calls=%fused_computation.65 | convolution fusion | flops 671350784 | bytes 4194304 | tf_op jit(solution)/shard_map/rk,gkf->grf/dot_general | solution.py:161
  204.6 3.9 %collective-permute-start.6 = (bf16[2,512,256]{2,1,0:T(8,128)(2,1)}, bf16[2,512,256]{2,1,0:T(8,128)(2,1)S(1)}, u32[]{:S(2)}, u32[]{:S(2)}) collective-permute-start(bf16[2,512,256]{2,1,0:T(8,128)(2,1)} %get-tuple-element.145), channel_id=1, source_target_pairs={{0,1},{1,2},{2,3},{3,0},{4,5},{5,6},{6,7},{7,4},{8,9},{9,10},{10,1... | collective-permute-start | bytes 1572872 | tf_op jit(solution)/shard_map/ppermute | solution.py:38
  208.5 2.6 collective-permute-start.7
  211.1 3.3 %collective-permute-start.8 = (bf16[2,512,256]{2,1,0:T(8,128)(2,1)}, bf16[2,512,256]{2,1,0:T(8,128)(2,1)}, u32[]{:S(2)}, u32[]{:S(2)}) collective-permute-start(bf16[2,512,256]{2,1,0:T(8,128)(2,1)} %get-tuple-element.145), channel_id=1, source_target_pairs={{0,3},{1,0},{2,1},{3,2},{4,7},{5,4},{6,5},{7,6},{8,11},{9,8},{10,9... | collective-permute-start | bytes 1572872 | tf_op jit(solution)/shard_map/ppermute | solution.py:38
  214.4 2.0 copy.60
  216.4 0.2 reshape.163
  216.6 12.4 %collective-permute-done.6 = bf16[2,512,256]{2,1,0:T(8,128)(2,1)S(1)} collective-permute-done((bf16[2,512,256]{2,1,0:T(8,128)(2,1)}, bf16[2,512,256]{2,1,0:T(8,128)(2,1)S(1)}, u32[]{:S(2)}, u32[]{:S(2)}) %collective-permute-start.6) | collective-permute-done | bytes 524320 | tf_op jit(solution)/shard_map/ppermute | solution.py:38
  229.0 5.6 %collective-permute-done.8 = bf16[2,512,256]{2,1,0:T(8,128)(2,1)} collective-permute-done((bf16[2,512,256]{2,1,0:T(8,128)(2,1)}, bf16[2,512,256]{2,1,0:T(8,128)(2,1)}, u32[]{:S(2)}, u32[]{:S(2)}) %collective-permute-start.8) | collective-permute-done | bytes 524320 | tf_op jit(solution)/shard_map/ppermute | solution.py:38
  234.6 1.4 convert_add_fusion
  236.0 0.6 fusion.10
  236.6 0.7 copy.61
  237.3 0.8 convert_element_type.137
  238.1 0.1 copy.62
  238.3 4.8 %all_to_all.25 = bf16[4,16,2,40,128]{4,3,1,0,2:T(8,128)(2,1)S(1)} all-to-all(bf16[4,16,2,40,128]{4,3,1,0,2:T(8,128)(2,1)S(1)} %copy.62), channel_id=1, replica_groups=mesh['y'=4,'z'=16,'c'=2,'mdl'=4] {'c'}, dimensions={2} | all-to-all | bytes 2621440 | tf_op jit(solution)/shard_map/all_to_all | solution.py:26
  243.0 0.6 reduce_sum.52
  243.7 15.2 %all_to_all.26 = bf16[4,16,1,40,128]{4,3,1,2,0:T(8,128)(2,1)S(1)} all-to-all(bf16[4,16,1,40,128]{4,3,1,2,0:T(8,128)(2,1)S(1)} %bitcast.111), channel_id=1, replica_groups=mesh['y'=4,'z'=16,'c'=2,'mdl'=4] {'y'}, dimensions={0} | all-to-all | bytes 1310720 | tf_op jit(solution)/shard_map/all_to_all | solution.py:26
  259.0 19.0 %all_to_all.27 = bf16[1,16,1,40,128]{4,3,2,0,1:T(8,128)(2,1)S(1)} all-to-all(bf16[1,16,1,40,128]{4,3,2,0,1:T(8,128)(2,1)S(1)} %bitcast.115), channel_id=1, replica_groups=mesh['y'=4,'z'=16,'c'=2,'mdl'=4] {'z'}, dimensions={1} | all-to-all | bytes 327680 | tf_op jit(solution)/shard_map/all_to_all | solution.py:26
  278.0 0.1 copy.63
  278.2 0.7 copy.64
  (71 shorter events, 1.3 us)
Async XLA Ops:
  0.6 92.7 %copy-start = (bf16[1024,40]{0,1:T(8,128)(2,1)S(1)}, bf16[1024,40]{0,1:T(8,128)(2,1)}, u32[]{:S(2)}) copy-start(bf16[1024,40]{0,1:T(8,128)(2,1)} %param.18) | copy-start | bytes 245764
  0.6 0.7 copy-start.12
  0.7 7.7 %copy-start.9 = (bf16[2,4,256]{2,1,0:T(4,128)(2,1)S(1)}, bf16[2,4,256]{2,1,0:T(4,128)(2,1)}, u32[]{:S(2)}) copy-start(bf16[2,4,256]{2,1,0:T(4,128)(2,1)} %param.15) | copy-start | bytes 12292
  0.7 7.8 %copy-start.2 = (bf16[2,1024,256]{2,1,0:T(8,128)(2,1)S(1)}, bf16[2,1024,256]{2,1,0:T(8,128)(2,1)}, u32[]{:S(2)}) copy-start(bf16[2,1024,256]{2,1,0:T(8,128)(2,1)} %param.16) | copy-start | bytes 3145732
  8.6 1.0 copy-start.1
  8.7 1.0 copy-start.10
  12.8 24.5 %copy-start.11 = (s32[512]{0:T(512)S(1)}, s32[512]{0:T(512)}, u32[]{:S(2)}) copy-start(s32[512]{0:T(512)} %param.13) | copy-start | bytes 6148
  12.8 80.1 %all-to-all-start = ((bf16[128,32,128]{2,1,0:T(8,128)(2,1)}), bf16[128,32,128]{2,1,0:T(8,128)(2,1)S(1)}, u32[]{:S(2)}, u32[]{:S(2)}) async-start(bf16[128,32,128]{2,1,0:T(8,128)(2,1)} %broadcast_in_dim.73), calls=%async_computation | async-start | bytes 2097152 | tf_op jit(solution)/shard_map/all_to_all | solution.py:20
  39.8 62.8 %copy-start.8 = (bf16[512,10]{0,1:T(8,128)(2,1)S(1)}, bf16[512,10]{0,1:T(8,128)(2,1)}, u32[]{:S(2)}) copy-start(bf16[512,10]{0,1:T(8,128)(2,1)} %param.17) | copy-start | bytes 30724
  93.9 8.8 %collective-permute-start = (bf16[40,128]{1,0:T(8,128)(2,1)S(1)}, bf16[40,128]{1,0:T(8,128)(2,1)S(1)}, u32[]{:S(2)}, u32[]{:S(2)}) collective-permute-start(bf16[40,128]{1,0:T(8,128)(2,1)S(1)} %get-tuple-element.134), channel_id=1, source_target_pairs={{0,1},{1,2},{2,3},{3,0},{4,5},{5,6},{6,7},{7,4},{8,9},{9,10},{10,1... | collective-permute-start | bytes 30728 | tf_op jit(solution)/shard_map/ppermute | solution.py:51
  96.2 7.1 %collective-permute-start.1 = (bf16[40,128]{1,0:T(8,128)(2,1)S(1)}, bf16[40,128]{1,0:T(8,128)(2,1)S(1)}, u32[]{:S(2)}, u32[]{:S(2)}) collective-permute-start(bf16[40,128]{1,0:T(8,128)(2,1)S(1)} %get-tuple-element.136), channel_id=1, source_target_pairs={{0,2},{1,3},{2,0},{3,1},{4,6},{5,7},{6,4},{7,5},{8,10},{9,11},{10,... | collective-permute-start | bytes 30728 | tf_op jit(solution)/shard_map/ppermute | solution.py:51
  100.6 6.8 %collective-permute-start.2 = (bf16[40,128]{1,0:T(8,128)(2,1)S(1)}, bf16[40,128]{1,0:T(8,128)(2,1)S(1)}, u32[]{:S(2)}, u32[]{:S(2)}) collective-permute-start(bf16[40,128]{1,0:T(8,128)(2,1)S(1)} %get-tuple-element.135), channel_id=1, source_target_pairs={{0,3},{1,0},{2,1},{3,2},{4,7},{5,4},{6,5},{7,6},{8,11},{9,8},{10,9... | collective-permute-start | bytes 30728 | tf_op jit(solution)/shard_map/ppermute | solution.py:51
  108.7 1.4 copy-start.5
  110.1 7.3 %copy-start.7 = (f32[5120]{0:T(1024)S(1)}, f32[5120]{0:T(1024)}, u32[]{:S(2)}) copy-start(f32[5120]{0:T(1024)} %param.19) | copy-start | bytes 61444
  110.1 73.5 %all-to-all-start.1 = ((bf16[128,40,128]{2,1,0:T(8,128)(2,1)}), bf16[128,40,128]{2,1,0:T(8,128)(2,1)S(1)}, u32[]{:S(2)}, u32[]{:S(2)}) async-start(bf16[128,40,128]{2,1,0:T(8,128)(2,1)} %broadcast_in_dim.77), calls=%async_computation.1 | async-start | bytes 2621440 | tf_op jit(solution)/shard_map/all_to_all | solution.py:20
  185.0 8.6 %copy-start.3 = (bf16[2,128,1,10,256]{4,1,3,2,0:T(8,128)(2,1)S(1)}, bf16[2,128,1,10,256]{4,1,3,2,0:T(8,128)(2,1)}, u32[]{:S(2)}) copy-start(bf16[2,128,1,10,256]{4,1,3,2,0:T(8,128)(2,1)} %param.20) | copy-start | bytes 3932164
  185.3 10.7 %collective-permute-start.3 = (f32[512]{0:T(512)S(1)}, f32[512]{0:T(512)S(1)}, u32[]{:S(2)}, u32[]{:S(2)}) collective-permute-start(f32[512]{0:T(512)S(1)} %fusion.11), channel_id=1, source_target_pairs={{0,1},{1,2},{2,3},{3,0},{4,5},{5,6},{6,7},{7,4},{8,9},{9,10},{10,1... | collective-permute-start | bytes 6152 | tf_op jit(solution)/shard_map/ppermute | solution.py:38
  187.9 8.0 %collective-permute-start.4 = (f32[512]{0:T(512)S(1)}, f32[512]{0:T(512)S(1)}, u32[]{:S(2)}, u32[]{:S(2)}) collective-permute-start(f32[512]{0:T(512)S(1)} %fusion.11), channel_id=1, source_target_pairs={{0,2},{1,3},{2,0},{3,1},{4,6},{5,7},{6,4},{7,5},{8,10},{9,11},{10,... | collective-permute-start | bytes 6152 | tf_op jit(solution)/shard_map/ppermute | solution.py:38
  190.1 7.3 %collective-permute-start.5 = (f32[512]{0:T(512)S(1)}, f32[512]{0:T(512)S(1)}, u32[]{:S(2)}, u32[]{:S(2)}) collective-permute-start(f32[512]{0:T(512)S(1)} %fusion.11), channel_id=1, source_target_pairs={{0,3},{1,0},{2,1},{3,2},{4,7},{5,4},{6,5},{7,6},{8,11},{9,8},{10,9... | collective-permute-start | bytes 6152 | tf_op jit(solution)/shard_map/ppermute | solution.py:38
  199.9 1.6 copy-start.4
  204.6 24.5 %collective-permute-start.6 = (bf16[2,512,256]{2,1,0:T(8,128)(2,1)}, bf16[2,512,256]{2,1,0:T(8,128)(2,1)S(1)}, u32[]{:S(2)}, u32[]{:S(2)}) collective-permute-start(bf16[2,512,256]{2,1,0:T(8,128)(2,1)} %get-tuple-element.145), channel_id=1, source_target_pairs={{0,1},{1,2},{2,3},{3,0},{4,5},{5,6},{6,7},{7,4},{8,9},{9,10},{10,1... | collective-permute-start | bytes 1572872 | tf_op jit(solution)/shard_map/ppermute | solution.py:38
  208.5 20.6 %collective-permute-start.7 = (bf16[2,512,256]{2,1,0:T(8,128)(2,1)}, bf16[2,512,256]{2,1,0:T(8,128)(2,1)}, u32[]{:S(2)}, u32[]{:S(2)}) collective-permute-start(bf16[2,512,256]{2,1,0:T(8,128)(2,1)} %get-tuple-element.145), channel_id=1, source_target_pairs={{0,2},{1,3},{2,0},{3,1},{4,6},{5,7},{6,4},{7,5},{8,10},{9,11},{10,... | collective-permute-start | bytes 1572872 | tf_op jit(solution)/shard_map/ppermute | solution.py:38
  211.1 23.6 %collective-permute-start.8 = (bf16[2,512,256]{2,1,0:T(8,128)(2,1)}, bf16[2,512,256]{2,1,0:T(8,128)(2,1)}, u32[]{:S(2)}, u32[]{:S(2)}) collective-permute-start(bf16[2,512,256]{2,1,0:T(8,128)(2,1)} %get-tuple-element.145), channel_id=1, source_target_pairs={{0,3},{1,0},{2,1},{3,2},{4,7},{5,4},{6,5},{7,6},{8,11},{9,8},{10,9... | collective-permute-start | bytes 1572872 | tf_op jit(solution)/shard_map/ppermute | solution.py:38
  243.7 34.5 %copy-start.6 = (bf16[512,10]{1,0:T(8,128)(2,1)S(1)}, bf16[512,10]{1,0:T(8,128)(2,1)}, u32[]{:S(2)}) copy-start(bf16[512,10]{1,0:T(8,128)(2,1)} %copy-done.5) | copy-start | bytes 30724

commit v3 on v2

--- a/solution.py
+++ b/solution.py
@@ -16,8 +16,10 @@
 def gather_rows(part):
     count = lax.axis_size(REQ)
     flat = part.reshape(-1, 128)
-    copies = jnp.broadcast_to(flat[None], (count,) + flat.shape)
-    return lax.all_to_all(copies, REQ, 0, 0, tiled=True).reshape((count,) + part.shape)
+    flat = lax.all_gather(flat, "c", axis=0, tiled=True)
+    flat = lax.all_gather(flat, "z", axis=0, tiled=True)
+    copies = jnp.broadcast_to(flat[None], (lax.axis_size("y"),) + flat.shape)
+    return lax.all_to_all(copies, "y", 0, 0, tiled=True).reshape((count,) + part.shape)
 
 
 def scatter_sum(parts):
@@ -29,14 +31,15 @@
     return wide
 
 
-def mdl_sum(value, wire):
+def mdl_sum(values, wires):
     count = lax.axis_size("mdl")
-    sent = value.astype(wire)
-    total = value.astype(jnp.float32)
+    sent = tuple(v.astype(w) for v, w in zip(values, wires))
+    totals = [v.astype(jnp.float32) for v in values]
     for shift in range(1, count):
         pairs = [(i, (i + shift) % count) for i in range(count)]
-        total = total + lax.ppermute(sent, "mdl", pairs).astype(jnp.float32)
-    return total
+        arrived = lax.ppermute(sent, "mdl", pairs)
+        totals = [t + a.astype(jnp.float32) for t, a in zip(totals, arrived)]
+    return totals
 
 
 def mdl_scatter_sum(value, wire):
@@ -151,19 +154,29 @@
     sub_width = hidden_in.shape[1]
     gathered = jnp.transpose(gather_rows(residual.T), (2, 0, 1)).reshape(total_rows, col_groups * sub_width)
     widened = gathered.astype(jnp.float32)
-    square_sum = mdl_sum(jnp.sum(widened * widened, axis=1), jnp.float32)
+    own_squares = jnp.sum(widened * widened, axis=1)
     gain_table = norm_gain.reshape(col_groups, lax.axis_size("mdl"), sub_width)
     gain_cols = lax.dynamic_index_in_dim(
         gain_table, lax.axis_index("mdl"), 1, keepdims=False
     ).reshape(col_groups * sub_width)
-    normed = (widened * lax.rsqrt(square_sum / D + 1e-05)[:, None] * gain_cols).astype(jnp.bfloat16)
+    unscaled = (widened * gain_cols).astype(jnp.bfloat16)
     gate_up = gate_up_weight.reshape(2, col_groups * sub_width, gate_up_weight.shape[4])
-    partial_value = jnp.einsum("rk,gkf->grf", normed, gate_up, preferred_element_type=jnp.float32)
-    gate_sums = mdl_sum(partial_value, jnp.bfloat16)
+    partial_value = jnp.einsum("rk,gkf->gfr", unscaled, gate_up, preferred_element_type=jnp.float32)
+    units = partial_value.shape[1]
+    squares_high = own_squares.astype(jnp.bfloat16)
+    squares_low = (own_squares - squares_high.astype(jnp.float32)).astype(jnp.bfloat16)
+    payload = jnp.concatenate(
+        [partial_value.reshape(2 * units, total_rows).astype(jnp.bfloat16), squares_high[None], squares_low[None]],
+        axis=0,
+    )
+    (summed_payload,) = mdl_sum((payload,), (jnp.bfloat16,))
+    square_sum = summed_payload[2 * units] + summed_payload[2 * units + 1]
+    scale = lax.rsqrt(square_sum / D + 1e-05)
+    gate_sums = summed_payload[: 2 * units].reshape(2, units, total_rows) * scale[None, None, :]
     hidden = (jax.nn.silu(gate_sums[0]) * gate_sums[1]).astype(jnp.bfloat16)
     columns = down_weight.reshape(down_weight.shape[0], col_groups * sub_width)
     lowered = lax.dot_general(
-        columns, hidden, (((0,), (1,)), ((), ())), preferred_element_type=jnp.float32
+        columns, hidden, (((0,), (0,)), ((), ())), preferred_element_type=jnp.float32
     )
     mesh_shape = (lax.axis_size("y"), lax.axis_size("z"), lax.axis_size("c"))
     summed = scatter_sum(lowered.reshape(mesh_shape + (sub_width * total_rows // 128, 128))).reshape(sub_width, total_rows)

time: 280 us -> 215 us (0.77)
  waiting for transfers between devices: 143 us -> 36.9 us
  blocking collectives: 39 us -> 115 us
  starting transfers between devices: 58.2 us -> 23.7 us
  other arithmetic: 4.56 us -> 7.49 us
    all_to_all x2, waiting for transfers between devices: 119 us -> 17.7 us  [gather_rows(): lax.all_to_all(copies, 'y', 0, 0, tiled=True).reshape((count,) + part.shape)]
    all_gather x0 -> x4, blocking collectives: none -> 72.7 us  [the longest x2 68.7 us: gather_rows(): flat = lax.all_gather(flat, 'z', axis=0, tiled=True)]
    all_to_all x2, starting transfers between devices: 31.7 us -> 7.32 us  [gather_rows(): lax.all_to_all(copies, 'y', 0, 0, tiled=True).reshape((count,) + part.shape)]
    ppermute x6 -> x3, starting transfers between devices: 17.9 us -> 7.75 us  [mdl_sum(): arrived = lax.ppermute(sent, 'mdl', pairs)]
    ppermute x6 -> x3, waiting for transfers between devices: 19.5 us -> 14.5 us  [mdl_sum(): arrived = lax.ppermute(sent, 'mdl', pairs)]
    all_to_all x3, blocking collectives: 39 us -> 42.2 us  [scatter_sum(): lax.all_to_all(parts.astype(jnp.bfloat16), name, position, position, tile...]
    unnamed x29 -> x31, local copies, waits for them, and re-layouts: 6.87 us -> 5.93 us
  transfers between devices with their start and end apart: 11 -> 8, of which waited for: 7 -> 7; matrix products, arithmetic and copies ran while one was open for 3% -> 3% of each run, Pallas kernels for 0% -> 0%
where the time goes in v3:
time: 215 us; the launch traced here: 214 us
  blocking collectives  115 us (53%)
  waiting for transfers between devices  36.9 us (17%)
  starting transfers between devices  23.7 us (11%)
  local copies, waits for them, and re-layouts  19.9 us (9%)
  other arithmetic  7.49 us (3%)
  between operations  7.1 us (3%)
  matrix products  3.72 us (2%)
    all_gather x2, blocking collectives, gather_rows(): flat = lax.all_gather(flat, 'z', axis=0, tiled=True)  68.7 us
    all_to_all x3, blocking collectives, scatter_sum(): lax.all_to_all(parts.astype(jnp.bfloat16), name, position, position, tile...  42.2 us
    all_to_all x2, waiting for transfers between devices, gather_rows(): lax.all_to_all(copies, 'y', 0, 0, tiled=True).reshape((count,) + part.shape)  17.7 us
    ppermute x3, waiting for transfers between devices, mdl_sum(): arrived = lax.ppermute(sent, 'mdl', pairs)  14.5 us
    ppermute x3, starting transfers between devices, mdl_scatter_sum(): total = total + lax.ppermute(outgoing, 'mdl', pairs).astype(jnp.float32)  8.63 us
    ppermute x3, starting transfers between devices, mdl_sum(): arrived = lax.ppermute(sent, 'mdl', pairs)  7.75 us
    all_to_all x2, starting transfers between devices, gather_rows(): lax.all_to_all(copies, 'y', 0, 0, tiled=True).reshape((count,) + part.shape)  7.32 us
    unnamed x31, local copies, waits for them, and re-layouts  5.93 us
  transfers between devices with their start and end apart: 8, of which 7 were waited for; matrix products, arithmetic and copies ran while one was open for 3% of the time, Pallas kernels for 0%

profile of v3, /device:TPU:6, one launch (start us, length us, event | category | flops | bytes accessed | tf_op | source)
XLA Modules:
  0.0 213.9 jit_solution(3942518563817971451)
XLA Ops:
  0.7 0.7 copy-done.13
  1.3 0.2 reduce-window.4
  1.5 0.6 reduce_max.18
  2.8 0.7 fusion.34
  8.9 0.1 reshape_squeeze.6
  9.1 0.7 copy-done.1
  9.8 0.1 reshape_squeeze.7
  10.0 0.9 while.14
  10.0 0.1 constant_dynamic-slice_fusion.4
  10.2 0.2 fusion.46
  10.5 0.2 fusion.47
  10.7 0.2 fusion.48
  11.0 2.2 %all_gather.12 = bf16[64,128]{1,0:T(8,128)(2,1)S(1)} all-gather(bf16[32,128]{1,0:T(8,128)(2,1)S(1)} %bitcast.122), channel_id=1, replica_groups=mesh['y'=4,'z'=16,'c'=2,'mdl'=4] {'c'}, dimensions={0}, use_global_device_ids=true | all-gather | bytes 24576 | tf_op jit(solution)/shard_map/all_gather | solution.py:19
  13.2 39.1 %all_gather.13 = bf16[1024,128]{1,0:T(8,128)(2,1)S(1)} all-gather(bf16[64,128]{1,0:T(8,128)(2,1)S(1)} %all_gather.12), channel_id=1, replica_groups=mesh['y'=4,'z'=16,'c'=2,'mdl'=4] {'z'}, dimensions={0}, use_global_device_ids=true | all-gather | bytes 278528 | tf_op jit(solution)/shard_map/all_gather | solution.py:20
  52.3 1.1 broadcast_in_dim.72
  53.4 3.6 %all-to-all-start = ((bf16[4,1024,128]{2,1,0:T(8,128)(2,1)}), bf16[4,1024,128]{2,1,0:T(8,128)(2,1)S(1)}, u32[]{:S(2)}, u32[]{:S(2)}) async-start(bf16[4,1024,128]{2,1,0:T(8,128)(2,1)} %broadcast_in_dim.72), calls=%async_computation | async-start | bytes 2097152 | tf_op jit(solution)/shard_map/all_to_all | solution.py:22
  57.1 2.4 %scatter_custom_fusion = s32[512]{0:T(512)S(1)} fusion(s32[512]{0:T(512)S(1)} %compare_select_fusion.1, s32[512]{0:T(512)S(1)} %iota.8, s32[]{:T(128)} %constant.115.clone.1), kind=kCustom, calls=%fused_computation.59 | custom fusion | bytes 2052 | tf_op jit(solution)/shard_map/scatter | solution.py:147
  59.6 8.3 %all-to-all-done = bf16[4,1024,128]{2,1,0:T(8,128)(2,1)S(1)} async-done(((bf16[4,1024,128]{2,1,0:T(8,128)(2,1)}), bf16[4,1024,128]{2,1,0:T(8,128)(2,1)S(1)}, u32[]{:S(2)}, u32[]{:S(2)}) %all-to-all-start) | async-done | bytes 1048608 | tf_op jit(solution)/shard_map/all_to_all | solution.py:22
  67.9 0.5 reshape_reshape.7
  68.4 0.4 fusion.20
  68.9 2.4 %collective-permute-start = (bf16[40,128]{1,0:T(8,128)(2,1)S(1)}, bf16[40,128]{1,0:T(8,128)(2,1)S(1)}, u32[]{:S(2)}, u32[]{:S(2)}) collective-permute-start(bf16[40,128]{1,0:T(8,128)(2,1)S(1)} %get-tuple-element.124), channel_id=1, source_target_pairs={{0,1},{1,2},{2,3},{3,0},{4,5},{5,6},{6,7},{7,4},{8,9},{9,10},{10,1... | collective-permute-start | bytes 30728 | tf_op jit(solution)/shard_map/ppermute | solution.py:54
  71.3 4.3 %collective-permute-start.1 = (bf16[40,128]{1,0:T(8,128)(2,1)S(1)}, bf16[40,128]{1,0:T(8,128)(2,1)S(1)}, u32[]{:S(2)}, u32[]{:S(2)}) collective-permute-start(bf16[40,128]{1,0:T(8,128)(2,1)S(1)} %get-tuple-element.126), channel_id=1, source_target_pairs={{0,2},{1,3},{2,0},{3,1},{4,6},{5,7},{6,4},{7,5},{8,10},{9,11},{10,... | collective-permute-start | bytes 30728 | tf_op jit(solution)/shard_map/ppermute | solution.py:54
  75.6 1.9 collective-permute-start.2
  77.6 0.1 copy.35
  77.7 0.6 collective-permute-done.1
  78.4 4.0 %collective-permute-done.2 = bf16[40,128]{1,0:T(8,128)(2,1)S(1)} collective-permute-done((bf16[40,128]{1,0:T(8,128)(2,1)S(1)}, bf16[40,128]{1,0:T(8,128)(2,1)S(1)}, u32[]{:S(2)}, u32[]{:S(2)}) %collective-permute-start.2) | collective-permute-done | bytes 10272 | tf_op jit(solution)/shard_map/ppermute | solution.py:54
  82.4 0.1 copy.34
  82.6 1.0 gather_fusion
  83.6 0.1 add_convert_fusion
  83.8 0.1 copy.36
  83.9 1.8 all_gather.14
  85.7 29.6 %all_gather.15 = bf16[1280,128]{1,0:T(8,128)(2,1)S(1)} all-gather(bf16[80,128]{1,0:T(8,128)(2,1)S(1)} %all_gather.14), channel_id=1, replica_groups=mesh['y'=4,'z'=16,'c'=2,'mdl'=4] {'z'}, dimensions={0}, use_global_device_ids=true | all-gather | bytes 348160 | tf_op jit(solution)/shard_map/all_gather | solution.py:20
  115.4 1.2 broadcast_in_dim.75
  116.6 3.7 %all-to-all-start.1 = ((bf16[4,1280,128]{2,1,0:T(8,128)(2,1)}), bf16[4,1280,128]{2,1,0:T(8,128)(2,1)S(1)}, u32[]{:S(2)}, u32[]{:S(2)}) async-start(bf16[4,1280,128]{2,1,0:T(8,128)(2,1)} %broadcast_in_dim.75), calls=%async_computation.1 | async-start | bytes 2621440 | tf_op jit(solution)/shard_map/all_to_all | solution.py:22
  120.3 0.3 reshape.202
  120.6 2.4 %copy.37 = bf16[2,128,1,10,256]{4,0,3,1,2:T(2,128)(2,1)} copy(bf16[2,128,1,10,256]{4,1,3,2,0:T(8,128)(2,1)S(1)} %copy-done.3) | data formatting | bytes 2621440 | tf_op args[8]
  123.1 9.5 %all-to-all-done.1 = bf16[4,1280,128]{2,1,0:T(8,128)(2,1)S(1)} async-done(((bf16[4,1280,128]{2,1,0:T(8,128)(2,1)}), bf16[4,1280,128]{2,1,0:T(8,128)(2,1)S(1)}, u32[]{:S(2)}, u32[]{:S(2)}) %all-to-all-start.1) | async-done | bytes 1310752 | tf_op jit(solution)/shard_map/all_to_all | solution.py:22
  132.5 2.3 %reshape.207 = f32[128,10,512]{2,1,0:T(8,128)} reshape(bf16[4,1280,128]{2,1,0:T(8,128)(2,1)S(1)} %all-to-all-done.1) | data formatting | bytes 3932160 | tf_op jit(solution)/shard_map/convert_element_type | solution.py:156
  134.8 2.8 %fusion.11 = (bf16[512,128,10]{0,2,1:T(8,128)(2,1)S(1)}, f32[512]{0:T(512)S(1)}) fusion(f32[128,10,512]{2,1,0:T(8,128)} %reshape.207, f32[128,10]{1,0:T(8,128)S(1)} %bitcast.117), kind=kLoop, calls=%fused_computation.26 | loop fusion | flops 2620928 | bytes 3939328 | tf_op jit(solution)/shard_map/convert_element_type | solution.py:162
  137.6 1.3 convert_element_type.171
  138.9 0.3 copy-done.4
  139.2 2.2 %fusion.15 = bf16[512,2,256]{0,2,1:T(8,128)(2,1)S(1)} fusion(bf16[2,1280,256]{2,0,1:T(2,128)(2,1)S(1)} %bitcast.112, bf16[512,1280]{0,1:T(8,128)(2,1)} %convert_element_type.171), kind=kOutput, calls=%fused_computation.30 | convolution fusion | flops 671350784 | bytes 3145728 | tf_op jit(solution)/shard_map/rk,gkf->gfr/dot_general | solution.py:164
  141.4 0.8 pad_maximum_fusion
  142.3 2.5 %collective-permute-start.3 = (bf16[514,512]{1,0:T(8,128)(2,1)}, bf16[514,512]{1,0:T(8,128)(2,1)}, u32[]{:S(2)}, u32[]{:S(2)}) collective-permute-start(bf16[514,512]{1,0:T(8,128)(2,1)} %pad_maximum_fusion), channel_id=1, source_target_pairs={{0,1},{1,2},{2,3},{3,0},{4,5},{5,6},{6,7},{7,4},{8,9},{9,10},{10,1... | collective-permute-start | bytes 1579016 | tf_op jit(solution)/shard_map/ppermute | solution.py:40
  144.8 2.2 %collective-permute-start.4 = (bf16[514,512]{1,0:T(8,128)(2,1)}, bf16[514,512]{1,0:T(8,128)(2,1)}, u32[]{:S(2)}, u32[]{:S(2)}) collective-permute-start(bf16[514,512]{1,0:T(8,128)(2,1)} %pad_maximum_fusion), channel_id=1, source_target_pairs={{0,2},{1,3},{2,0},{3,1},{4,6},{5,7},{6,4},{7,5},{8,10},{9,11},{10,... | collective-permute-start | bytes 1579016 | tf_op jit(solution)/shard_map/ppermute | solution.py:40
  147.0 3.1 %collective-permute-start.5 = (bf16[514,512]{1,0:T(8,128)(2,1)}, bf16[514,512]{1,0:T(8,128)(2,1)}, u32[]{:S(2)}, u32[]{:S(2)}) collective-permute-start(bf16[514,512]{1,0:T(8,128)(2,1)} %pad_maximum_fusion), channel_id=1, source_target_pairs={{0,3},{1,0},{2,1},{3,2},{4,7},{5,4},{6,5},{7,6},{8,11},{9,8},{10,9... | collective-permute-start | bytes 1579016 | tf_op jit(solution)/shard_map/ppermute | solution.py:40
  150.1 1.0 copy.40
  151.1 0.2 reshape.205
  151.4 5.0 %collective-permute-done.3 = bf16[514,512]{1,0:T(8,128)(2,1)} collective-permute-done((bf16[514,512]{1,0:T(8,128)(2,1)}, bf16[514,512]{1,0:T(8,128)(2,1)}, u32[]{:S(2)}, u32[]{:S(2)}) %collective-permute-start.3) | collective-permute-done | bytes 526368 | tf_op jit(solution)/shard_map/ppermute | solution.py:40
  156.4 3.9 %collective-permute-done.4 = bf16[514,512]{1,0:T(8,128)(2,1)} collective-permute-done((bf16[514,512]{1,0:T(8,128)(2,1)}, bf16[514,512]{1,0:T(8,128)(2,1)}, u32[]{:S(2)}, u32[]{:S(2)}) %collective-permute-start.4) | collective-permute-done | bytes 526368 | tf_op jit(solution)/shard_map/ppermute | solution.py:40
  160.3 5.6 %collective-permute-done.5 = bf16[514,512]{1,0:T(8,128)(2,1)} collective-permute-done((bf16[514,512]{1,0:T(8,128)(2,1)}, bf16[514,512]{1,0:T(8,128)(2,1)}, u32[]{:S(2)}, u32[]{:S(2)}) %collective-permute-start.5) | collective-permute-done | bytes 526368 | tf_op jit(solution)/shard_map/ppermute | solution.py:40
  165.8 1.6 convert_add_fusion
  167.6 0.1 broadcast_multiply_fusion
  167.7 0.7 fusion.10
  168.4 0.7 copy.41
  169.0 0.8 convert_element_type.186
  169.9 0.1 copy.42
  170.0 4.8 %all_to_all.25 = bf16[4,16,2,40,128]{4,3,1,0,2:T(8,128)(2,1)S(1)} all-to-all(bf16[4,16,2,40,128]{4,3,1,0,2:T(8,128)(2,1)S(1)} %copy.42), channel_id=1, replica_groups=mesh['y'=4,'z'=16,'c'=2,'mdl'=4] {'c'}, dimensions={2} | all-to-all | bytes 2621440 | tf_op jit(solution)/shard_map/all_to_all | solution.py:28
  174.8 0.6 reduce_sum.55
  175.4 14.0 %all_to_all.26 = bf16[4,16,1,40,128]{4,3,1,2,0:T(8,128)(2,1)S(1)} all-to-all(bf16[4,16,1,40,128]{4,3,1,2,0:T(8,128)(2,1)S(1)} %bitcast.108), channel_id=1, replica_groups=mesh['y'=4,'z'=16,'c'=2,'mdl'=4] {'y'}, dimensions={0} | all-to-all | bytes 1310720 | tf_op jit(solution)/shard_map/all_to_all | solution.py:28
  189.4 0.1 reduce_sum.56
  189.5 23.4 %all_to_all.27 = bf16[1,16,1,40,128]{4,3,2,0,1:T(8,128)(2,1)S(1)} all-to-all(bf16[1,16,1,40,128]{4,3,2,0,1:T(8,128)(2,1)S(1)} %bitcast.114), channel_id=1, replica_groups=mesh['y'=4,'z'=16,'c'=2,'mdl'=4] {'z'}, dimensions={1} | all-to-all | bytes 327680 | tf_op jit(solution)/shard_map/all_to_all | solution.py:28
  213.0 0.1 copy.43
  213.2 0.7 copy.44
  (64 shorter events, 0.9 us)
Async XLA Ops:
  0.6 67.8 %copy-start = (bf16[1024,40]{0,1:T(8,128)(2,1)S(1)}, bf16[1024,40]{0,1:T(8,128)(2,1)}, u32[]{:S(2)}) copy-start(bf16[1024,40]{0,1:T(8,128)(2,1)} %param.18) | copy-start | bytes 245764
  0.6 0.7 copy-start.13
  0.7 7.9 %copy-start.10 = (bf16[2,4,256]{2,1,0:T(4,128)(2,1)S(1)}, bf16[2,4,256]{2,1,0:T(4,128)(2,1)}, u32[]{:S(2)}) copy-start(bf16[2,4,256]{2,1,0:T(4,128)(2,1)} %param.15) | copy-start | bytes 12292
  0.7 8.0 %copy-start.2 = (bf16[2,1024,256]{2,1,0:T(8,128)(2,1)S(1)}, bf16[2,1024,256]{2,1,0:T(8,128)(2,1)}, u32[]{:S(2)}) copy-start(bf16[2,1024,256]{2,1,0:T(8,128)(2,1)} %param.16) | copy-start | bytes 3145732
  8.8 1.0 copy-start.1
  8.9 1.0 copy-start.11
  53.4 3.7 %copy-start.12 = (s32[512]{0:T(512)S(1)}, s32[512]{0:T(512)}, u32[]{:S(2)}) copy-start(s32[512]{0:T(512)} %param.13) | copy-start | bytes 6148
  53.4 14.5 %all-to-all-start = ((bf16[4,1024,128]{2,1,0:T(8,128)(2,1)}), bf16[4,1024,128]{2,1,0:T(8,128)(2,1)S(1)}, u32[]{:S(2)}, u32[]{:S(2)}) async-start(bf16[4,1024,128]{2,1,0:T(8,128)(2,1)} %broadcast_in_dim.72), calls=%async_computation | async-start | bytes 2097152 | tf_op jit(solution)/shard_map/all_to_all | solution.py:22
  59.6 18.0 %copy-start.9 = (bf16[512,10]{0,1:T(8,128)(2,1)S(1)}, bf16[512,10]{0,1:T(8,128)(2,1)}, u32[]{:S(2)}) copy-start(bf16[512,10]{0,1:T(8,128)(2,1)} %param.17) | copy-start | bytes 30724
  68.9 8.8 %collective-permute-start = (bf16[40,128]{1,0:T(8,128)(2,1)S(1)}, bf16[40,128]{1,0:T(8,128)(2,1)S(1)}, u32[]{:S(2)}, u32[]{:S(2)}) collective-permute-start(bf16[40,128]{1,0:T(8,128)(2,1)S(1)} %get-tuple-element.124), channel_id=1, source_target_pairs={{0,1},{1,2},{2,3},{3,0},{4,5},{5,6},{6,7},{7,4},{8,9},{9,10},{10,1... | collective-permute-start | bytes 30728 | tf_op jit(solution)/shard_map/ppermute | solution.py:54
  71.3 7.1 %collective-permute-start.1 = (bf16[40,128]{1,0:T(8,128)(2,1)S(1)}, bf16[40,128]{1,0:T(8,128)(2,1)S(1)}, u32[]{:S(2)}, u32[]{:S(2)}) collective-permute-start(bf16[40,128]{1,0:T(8,128)(2,1)S(1)} %get-tuple-element.126), channel_id=1, source_target_pairs={{0,2},{1,3},{2,0},{3,1},{4,6},{5,7},{6,4},{7,5},{8,10},{9,11},{10,... | collective-permute-start | bytes 30728 | tf_op jit(solution)/shard_map/ppermute | solution.py:54
  75.6 6.8 %collective-permute-start.2 = (bf16[40,128]{1,0:T(8,128)(2,1)S(1)}, bf16[40,128]{1,0:T(8,128)(2,1)S(1)}, u32[]{:S(2)}, u32[]{:S(2)}) collective-permute-start(bf16[40,128]{1,0:T(8,128)(2,1)S(1)} %get-tuple-element.125), channel_id=1, source_target_pairs={{0,3},{1,0},{2,1},{3,2},{4,7},{5,4},{6,5},{7,6},{8,11},{9,8},{10,9... | collective-permute-start | bytes 30728 | tf_op jit(solution)/shard_map/ppermute | solution.py:54
  83.8 32.8 %copy-start.5 = (bf16[512,10]{1,0:T(8,128)(2,1)}, bf16[512,10]{1,0:T(8,128)(2,1)S(1)}, u32[]{:S(2)}) copy-start(bf16[512,10]{1,0:T(8,128)(2,1)S(1)} %add_convert_fusion) | copy-start | bytes 30724
  116.6 3.7 %copy-start.8 = (f32[5120]{0:T(1024)S(1)}, f32[5120]{0:T(1024)}, u32[]{:S(2)}) copy-start(f32[5120]{0:T(1024)} %param.19) | copy-start | bytes 61444
  116.6 4.0 %copy-start.3 = (bf16[2,128,1,10,256]{4,1,3,2,0:T(8,128)(2,1)S(1)}, bf16[2,128,1,10,256]{4,1,3,2,0:T(8,128)(2,1)}, u32[]{:S(2)}) copy-start(bf16[2,128,1,10,256]{4,1,3,2,0:T(8,128)(2,1)} %param.20) | copy-start | bytes 3932164
  116.6 15.9 %all-to-all-start.1 = ((bf16[4,1280,128]{2,1,0:T(8,128)(2,1)}), bf16[4,1280,128]{2,1,0:T(8,128)(2,1)S(1)}, u32[]{:S(2)}, u32[]{:S(2)}) async-start(bf16[4,1280,128]{2,1,0:T(8,128)(2,1)} %broadcast_in_dim.75), calls=%async_computation.1 | async-start | bytes 2621440 | tf_op jit(solution)/shard_map/all_to_all | solution.py:22
  137.6 1.6 copy-start.4
  141.4 8.6 %copy-start.7 = (bf16[256,128,1,10]{1,0,3,2:T(8,128)(2,1)S(1)}, bf16[256,128,1,10]{1,0,3,2:T(8,128)(2,1)}, u32[]{:S(2)}) copy-start(bf16[256,128,1,10]{1,0,3,2:T(8,128)(2,1)} %param.21) | copy-start | bytes 1966084
  142.3 14.1 %collective-permute-start.3 = (bf16[514,512]{1,0:T(8,128)(2,1)}, bf16[514,512]{1,0:T(8,128)(2,1)}, u32[]{:S(2)}, u32[]{:S(2)}) collective-permute-start(bf16[514,512]{1,0:T(8,128)(2,1)} %pad_maximum_fusion), channel_id=1, source_target_pairs={{0,1},{1,2},{2,3},{3,0},{4,5},{5,6},{6,7},{7,4},{8,9},{9,10},{10,1... | collective-permute-start | bytes 1579016 | tf_op jit(solution)/shard_map/ppermute | solution.py:40
  144.8 15.5 %collective-permute-start.4 = (bf16[514,512]{1,0:T(8,128)(2,1)}, bf16[514,512]{1,0:T(8,128)(2,1)}, u32[]{:S(2)}, u32[]{:S(2)}) collective-permute-start(bf16[514,512]{1,0:T(8,128)(2,1)} %pad_maximum_fusion), channel_id=1, source_target_pairs={{0,2},{1,3},{2,0},{3,1},{4,6},{5,7},{6,4},{7,5},{8,10},{9,11},{10,... | collective-permute-start | bytes 1579016 | tf_op jit(solution)/shard_map/ppermute | solution.py:40
  147.0 18.9 %collective-permute-start.5 = (bf16[514,512]{1,0:T(8,128)(2,1)}, bf16[514,512]{1,0:T(8,128)(2,1)}, u32[]{:S(2)}, u32[]{:S(2)}) collective-permute-start(bf16[514,512]{1,0:T(8,128)(2,1)} %pad_maximum_fusion), channel_id=1, source_target_pairs={{0,3},{1,0},{2,1},{3,2},{4,7},{5,4},{6,5},{7,6},{8,11},{9,8},{10,9... | collective-permute-start | bytes 1579016 | tf_op jit(solution)/shard_map/ppermute | solution.py:40
  175.4 37.7 %copy-start.6 = (bf16[512,10]{1,0:T(8,128)(2,1)S(1)}, bf16[512,10]{1,0:T(8,128)(2,1)}, u32[]{:S(2)}) copy-start(bf16[512,10]{1,0:T(8,128)(2,1)} %copy-done.5) | copy-start | bytes 30724

commit v4 on v3

--- a/solution.py
+++ b/solution.py
@@ -44,15 +44,10 @@
 
 def mdl_scatter_sum(value, wire):
     count = lax.axis_size("mdl")
-    me = lax.axis_index("mdl")
     height = value.shape[0] // count
     blocks = value.astype(wire).reshape((count, height * value.shape[1] // 128, 128))
-    total = lax.dynamic_index_in_dim(blocks, me, 0, keepdims=False).astype(jnp.float32)
-    for shift in range(1, count):
-        pairs = [(i, (i + shift) % count) for i in range(count)]
-        outgoing = lax.dynamic_index_in_dim(blocks, (me + shift) % count, 0, keepdims=False)
-        total = total + lax.ppermute(outgoing, "mdl", pairs).astype(jnp.float32)
-    return total.reshape(height, value.shape[1])
+    moved = lax.all_to_all(blocks, "mdl", 0, 0, tiled=True)
+    return moved.astype(jnp.float32).sum(0).reshape(height, value.shape[1])
 
 
 def slot_bounds(lengths):
@@ -163,17 +158,23 @@
     gate_up = gate_up_weight.reshape(2, col_groups * sub_width, gate_up_weight.shape[4])
     partial_value = jnp.einsum("rk,gkf->gfr", unscaled, gate_up, preferred_element_type=jnp.float32)
     units = partial_value.shape[1]
+    mdl_count = lax.axis_size("mdl")
+    quarter = units // mdl_count
     squares_high = own_squares.astype(jnp.bfloat16)
     squares_low = (own_squares - squares_high.astype(jnp.float32)).astype(jnp.bfloat16)
-    payload = jnp.concatenate(
-        [partial_value.reshape(2 * units, total_rows).astype(jnp.bfloat16), squares_high[None], squares_low[None]],
-        axis=0,
-    )
-    (summed_payload,) = mdl_sum((payload,), (jnp.bfloat16,))
-    square_sum = summed_payload[2 * units] + summed_payload[2 * units + 1]
+    squares_pair = jnp.broadcast_to(jnp.stack([squares_high, squares_low])[None], (mdl_count, 2, total_rows))
+    blocks = jnp.transpose(
+        partial_value.astype(jnp.bfloat16).reshape(2, mdl_count, quarter, total_rows), (1, 0, 2, 3)
+    ).reshape(mdl_count, 2 * quarter, total_rows)
+    payload = jnp.concatenate([blocks, squares_pair], axis=1)
+    summed_payload = lax.all_to_all(payload, "mdl", 0, 0, tiled=True).astype(jnp.float32).sum(0)
+    square_sum = summed_payload[2 * quarter] + summed_payload[2 * quarter + 1]
     scale = lax.rsqrt(square_sum / D + 1e-05)
-    gate_sums = summed_payload[: 2 * units].reshape(2, units, total_rows) * scale[None, None, :]
-    hidden = (jax.nn.silu(gate_sums[0]) * gate_sums[1]).astype(jnp.bfloat16)
+    gate_part = summed_payload[:quarter] * scale[None, :]
+    up_part = summed_payload[quarter : 2 * quarter] * scale[None, :]
+    hidden_part = (jax.nn.silu(gate_part) * up_part).astype(jnp.bfloat16)
+    hidden_copies = jnp.broadcast_to(hidden_part[None], (mdl_count,) + hidden_part.shape)
+    hidden = lax.all_to_all(hidden_copies, "mdl", 0, 0, tiled=True).reshape(units, total_rows)
     columns = down_weight.reshape(down_weight.shape[0], col_groups * sub_width)
     lowered = lax.dot_general(
         columns, hidden, (((0,), (0,)), ((), ())), preferred_element_type=jnp.float32

time: 215 us -> 206 us (0.958)
  waiting for transfers between devices: 36.9 us -> 24.5 us
  blocking collectives: 115 us -> 123 us
  starting transfers between devices: 23.7 us -> 19.1 us
    ppermute x6 -> x0, waiting for transfers between devices: 19.2 us -> none  [the longest x3 14.5 us: mdl_sum(): arrived = lax.ppermute(sent, 'mdl', pairs)]
    ppermute x6 -> x0, starting transfers between devices: 16.4 us -> none  [the longest x3 8.63 us: mdl_scatter_sum(): total = total + lax.ppermute(outgoing, 'mdl', pairs).astype(jnp.float32)]
    all_to_all x0 -> x1, blocking collectives: none -> 11.1 us  [body(): lax.all_to_all(payload, 'mdl', 0, 0, tiled=True).astype(jnp.float32).sum(0)]
    all_to_all x0 -> x2, starting transfers between devices: none -> 10.2 us  [the longest x1 5.45 us: body(): lax.all_to_all(hidden_copies, 'mdl', 0, 0, tiled=True)]
    all_to_all x0 -> x2, waiting for transfers between devices: none -> 6.61 us  [the longest x1 3.33 us: body(): lax.all_to_all(hidden_copies, 'mdl', 0, 0, tiled=True)]
  transfers between devices with their start and end apart: 8 -> 4, of which waited for: 7 -> 4; matrix products, arithmetic and copies ran while one was open for 3% -> 3% of each run, Pallas kernels for 0% -> 0%
where the time goes in v4:
time: 206 us; the launch traced here: 204 us
  blocking collectives  123 us (60%)
  waiting for transfers between devices  24.5 us (12%)
  local copies, waits for them, and re-layouts  21.3 us (10%)
  starting transfers between devices  19.1 us (9%)
  between operations  6.96 us (3%)
  other arithmetic  5.37 us (3%)
  matrix products  4.02 us (2%)
    all_gather x2, blocking collectives, gather_rows(): flat = lax.all_gather(flat, 'z', axis=0, tiled=True)  67.1 us
    all_to_all x3, blocking collectives, scatter_sum(): lax.all_to_all(parts.astype(jnp.bfloat16), name, position, position, tile...  40.9 us
    all_to_all x2, waiting for transfers between devices, gather_rows(): lax.all_to_all(copies, 'y', 0, 0, tiled=True).reshape((count,) + part.shape)  17.8 us
    all_to_all x1, blocking collectives, body(): lax.all_to_all(payload, 'mdl', 0, 0, tiled=True).astype(jnp.float32).sum(0)  11.1 us
    all_to_all x2, starting transfers between devices, gather_rows(): lax.all_to_all(copies, 'y', 0, 0, tiled=True).reshape((count,) + part.shape)  8.86 us
    unnamed x31, local copies, waits for them, and re-layouts  5.9 us
    all_to_all x1, starting transfers between devices, body(): lax.all_to_all(hidden_copies, 'mdl', 0, 0, tiled=True)  5.45 us
    all_to_all x1, starting transfers between devices, mdl_scatter_sum(): moved = lax.all_to_all(blocks, 'mdl', 0, 0, tiled=True)  4.77 us
  transfers between devices with their start and end apart: 4, of which 4 were waited for; matrix products, arithmetic and copies ran while one was open for 3% of the time, Pallas kernels for 0%

profile of v4, /device:TPU:6, one launch (start us, length us, event | category | flops | bytes accessed | tf_op | source)
XLA Modules:
  0.0 204.0 jit_solution(9678414586014294232)
XLA Ops:
  0.7 0.7 copy-done.13
  1.3 0.2 reduce-window.4
  1.5 0.6 reduce_max.18
  2.8 0.6 fusion.30
  8.9 0.1 reshape_squeeze.6
  9.0 0.7 copy-done.1
  9.7 0.1 reshape_squeeze.7
  10.0 1.7 while.14
  10.0 0.1 constant_dynamic-slice_fusion.4
  10.1 0.1 compare_and_fusion.3
  10.2 0.2 fusion.43
  10.4 0.2 fusion.44
  10.6 0.2 fusion.45
  10.9 0.1 constant_dynamic-slice_fusion.4
  11.0 0.1 compare_and_fusion.3
  11.1 0.2 fusion.43
  11.3 0.2 fusion.44
  11.5 0.2 fusion.45
  11.7 0.1 divide_convert_fusion
  11.8 1.8 all_gather.12
  13.6 39.4 %all_gather.13 = bf16[1024,128]{1,0:T(8,128)(2,1)S(1)} all-gather(bf16[64,128]{1,0:T(8,128)(2,1)S(1)} %all_gather.12), channel_id=1, replica_groups=mesh['y'=4,'z'=16,'c'=2,'mdl'=4] {'z'}, dimensions={0}, use_global_device_ids=true | all-gather | bytes 278528 | tf_op jit(solution)/shard_map/all_gather | solution.py:20
  53.0 1.1 broadcast_in_dim.83
  54.2 5.2 %all-to-all-start = ((bf16[4,1024,128]{2,1,0:T(8,128)(2,1)}), bf16[4,1024,128]{2,1,0:T(8,128)(2,1)S(1)}, u32[]{:S(2)}, u32[]{:S(2)}) async-start(bf16[4,1024,128]{2,1,0:T(8,128)(2,1)} %broadcast_in_dim.83), calls=%async_computation | async-start | bytes 2097152 | tf_op jit(solution)/shard_map/all_to_all | solution.py:22
  59.4 2.4 %scatter_custom_fusion = s32[512]{0:T(512)S(1)} fusion(s32[512]{0:T(512)S(1)} %compare_select_fusion.1, s32[512]{0:T(512)S(1)} %iota.8, s32[]{:T(128)} %constant.85.clone.1), kind=kCustom, calls=%fused_computation.54 | custom fusion | bytes 2052 | tf_op jit(solution)/shard_map/scatter | solution.py:142
  61.9 8.4 %all-to-all-done = bf16[4,1024,128]{2,1,0:T(8,128)(2,1)S(1)} async-done(((bf16[4,1024,128]{2,1,0:T(8,128)(2,1)}), bf16[4,1024,128]{2,1,0:T(8,128)(2,1)S(1)}, u32[]{:S(2)}, u32[]{:S(2)}) %all-to-all-start) | async-done | bytes 1048608 | tf_op jit(solution)/shard_map/all_to_all | solution.py:22
  70.3 0.5 reshape_reshape.7
  70.7 0.4 fusion.20
  71.2 0.6 reshape.184
  71.8 4.8 %all-to-all-start.1 = ((bf16[4,40,128]{2,1,0:T(8,128)(2,1)}), bf16[4,40,128]{2,1,0:T(8,128)(2,1)S(1)}, u32[]{:S(2)}, u32[]{:S(2)}) async-start(bf16[4,40,128]{2,1,0:T(8,128)(2,1)} %reshape.184), calls=%async_computation.1 | async-start | bytes 81920 | tf_op jit(solution)/shard_map/all_to_all | solution.py:49
  76.6 0.1 copy.36
  76.7 3.3 %all-to-all-done.1 = bf16[4,40,128]{2,1,0:T(8,128)(2,1)S(1)} async-done(((bf16[4,40,128]{2,1,0:T(8,128)(2,1)}), bf16[4,40,128]{2,1,0:T(8,128)(2,1)S(1)}, u32[]{:S(2)}, u32[]{:S(2)}) %all-to-all-start.1) | async-done | bytes 40992 | tf_op jit(solution)/shard_map/all_to_all | solution.py:49
  80.0 0.1 copy.35
  80.2 1.0 gather_fusion
  81.2 0.1 add_convert_fusion
  81.4 0.1 copy.37
  81.5 1.8 all_gather.14
  83.4 27.7 %all_gather.15 = bf16[1280,128]{1,0:T(8,128)(2,1)S(1)} all-gather(bf16[80,128]{1,0:T(8,128)(2,1)S(1)} %all_gather.14), channel_id=1, replica_groups=mesh['y'=4,'z'=16,'c'=2,'mdl'=4] {'z'}, dimensions={0}, use_global_device_ids=true | all-gather | bytes 348160 | tf_op jit(solution)/shard_map/all_gather | solution.py:20
  111.1 1.2 broadcast_in_dim.86
  112.3 3.7 %all-to-all-start.2 = ((bf16[4,1280,128]{2,1,0:T(8,128)(2,1)}), bf16[4,1280,128]{2,1,0:T(8,128)(2,1)S(1)}, u32[]{:S(2)}, u32[]{:S(2)}) async-start(bf16[4,1280,128]{2,1,0:T(8,128)(2,1)} %broadcast_in_dim.86), calls=%async_computation.2 | async-start | bytes 2621440 | tf_op jit(solution)/shard_map/all_to_all | solution.py:22
  116.0 0.3 reshape.187
  116.3 2.4 %copy.38 = bf16[2,128,1,10,256]{4,0,3,1,2:T(2,128)(2,1)} copy(bf16[2,128,1,10,256]{4,1,3,2,0:T(8,128)(2,1)S(1)} %copy-done.3) | data formatting | bytes 2621440 | tf_op args[8]
  118.8 9.5 %all-to-all-done.2 = bf16[4,1280,128]{2,1,0:T(8,128)(2,1)S(1)} async-done(((bf16[4,1280,128]{2,1,0:T(8,128)(2,1)}), bf16[4,1280,128]{2,1,0:T(8,128)(2,1)S(1)}, u32[]{:S(2)}, u32[]{:S(2)}) %all-to-all-start.2) | async-done | bytes 1310752 | tf_op jit(solution)/shard_map/all_to_all | solution.py:22
  128.3 2.2 %reshape.193 = f32[128,10,512]{2,1,0:T(8,128)} reshape(bf16[4,1280,128]{2,1,0:T(8,128)(2,1)S(1)} %all-to-all-done.2) | data formatting | bytes 3932160 | tf_op jit(solution)/shard_map/convert_element_type | solution.py:151
  130.5 2.8 %fusion.11 = (bf16[512,128,10]{0,2,1:T(8,128)(2,1)S(1)}, f32[512]{0:T(512)S(1)}) fusion(f32[128,10,512]{2,1,0:T(8,128)} %reshape.193, f32[128,10]{1,0:T(8,128)S(1)} %bitcast.109), kind=kLoop, calls=%fused_computation.26 | loop fusion | flops 2620928 | bytes 3939328 | tf_op jit(solution)/shard_map/convert_element_type | solution.py:157
  133.3 1.3 convert_element_type.140
  134.6 0.3 copy-done.4
  134.9 2.2 %fusion.15 = bf16[512,2,256]{0,2,1:T(8,128)(2,1)S(1)} fusion(bf16[2,1280,256]{2,0,1:T(2,128)(2,1)S(1)} %bitcast.102, bf16[512,1280]{0,1:T(8,128)(2,1)} %convert_element_type.140), kind=kOutput, calls=%fused_computation.30 | convolution fusion | flops 671350784 | bytes 3145728 | tf_op jit(solution)/shard_map/rk,gkf->gfr/dot_general | solution.py:159
  137.3 11.1 %all_to_all.40 = bf16[4,130,512]{2,1,0:T(8,128)(2,1)S(1)} all-to-all(bf16[4,130,512]{2,1,0:T(8,128)(2,1)S(1)} %pad_maximum_fusion), channel_id=1, replica_groups=mesh['y'=4,'z'=16,'c'=2,'mdl'=4] {'mdl'}, dimensions={0} | all-to-all | bytes 1064960 | tf_op jit(solution)/shard_map/all_to_all | solution.py:170
  148.5 0.7 broadcast_in_dim.88
  149.2 5.5 %all-to-all-start.4 = ((bf16[4,64,512]{2,1,0:T(8,128)(2,1)}), bf16[4,64,512]{2,1,0:T(8,128)(2,1)S(1)}, u32[]{:S(2)}, u32[]{:S(2)}) async-start(bf16[4,64,512]{2,1,0:T(8,128)(2,1)} %broadcast_in_dim.88), calls=%async_computation.4 | async-start | bytes 524288 | tf_op jit(solution)/shard_map/all_to_all | solution.py:177
  154.7 1.0 copy.42
  155.7 0.2 reshape.192
  156.0 3.3 %all-to-all-done.4 = bf16[4,64,512]{2,1,0:T(8,128)(2,1)S(1)} async-done(((bf16[4,64,512]{2,1,0:T(8,128)(2,1)}), bf16[4,64,512]{2,1,0:T(8,128)(2,1)S(1)}, u32[]{:S(2)}, u32[]{:S(2)}) %all-to-all-start.4) | async-done | bytes 262176 | tf_op jit(solution)/shard_map/all_to_all | solution.py:177
  159.3 0.6 fusion.10
  159.8 0.7 copy.43
  160.5 0.8 convert_element_type.150
  161.3 0.1 copy.44
  161.5 4.8 %all_to_all.41 = bf16[4,16,2,40,128]{4,3,1,0,2:T(8,128)(2,1)S(1)} all-to-all(bf16[4,16,2,40,128]{4,3,1,0,2:T(8,128)(2,1)S(1)} %copy.44), channel_id=1, replica_groups=mesh['y'=4,'z'=16,'c'=2,'mdl'=4] {'c'}, dimensions={2} | all-to-all | bytes 2621440 | tf_op jit(solution)/shard_map/all_to_all | solution.py:28
  166.3 0.6 reduce_sum.75
  166.9 14.0 %all_to_all.42 = bf16[4,16,1,40,128]{4,3,1,2,0:T(8,128)(2,1)S(1)} all-to-all(bf16[4,16,1,40,128]{4,3,1,2,0:T(8,128)(2,1)S(1)} %bitcast.99), channel_id=1, replica_groups=mesh['y'=4,'z'=16,'c'=2,'mdl'=4] {'y'}, dimensions={0} | all-to-all | bytes 1310720 | tf_op jit(solution)/shard_map/all_to_all | solution.py:28
  180.9 0.1 reduce_sum.76
  181.0 22.1 %all_to_all.43 = bf16[1,16,1,40,128]{4,3,2,0,1:T(8,128)(2,1)S(1)} all-to-all(bf16[1,16,1,40,128]{4,3,2,0,1:T(8,128)(2,1)S(1)} %bitcast.105), channel_id=1, replica_groups=mesh['y'=4,'z'=16,'c'=2,'mdl'=4] {'z'}, dimensions={1} | all-to-all | bytes 327680 | tf_op jit(solution)/shard_map/all_to_all | solution.py:28
  203.1 0.1 copy.45
  203.3 0.7 copy.46
  (68 shorter events, 0.8 us)
Async XLA Ops:
  0.6 70.1 %copy-start = (bf16[1024,40]{0,1:T(8,128)(2,1)S(1)}, bf16[1024,40]{0,1:T(8,128)(2,1)}, u32[]{:S(2)}) copy-start(bf16[1024,40]{0,1:T(8,128)(2,1)} %param.18) | copy-start | bytes 245764
  0.6 0.7 copy-start.13
  0.7 7.9 %copy-start.10 = (bf16[2,4,256]{2,1,0:T(4,128)(2,1)S(1)}, bf16[2,4,256]{2,1,0:T(4,128)(2,1)}, u32[]{:S(2)}) copy-start(bf16[2,4,256]{2,1,0:T(4,128)(2,1)} %param.15) | copy-start | bytes 12292
  0.7 7.9 %copy-start.2 = (bf16[2,1024,256]{2,1,0:T(8,128)(2,1)S(1)}, bf16[2,1024,256]{2,1,0:T(8,128)(2,1)}, u32[]{:S(2)}) copy-start(bf16[2,1024,256]{2,1,0:T(8,128)(2,1)} %param.16) | copy-start | bytes 3145732
  8.8 1.0 copy-start.1
  8.9 1.0 copy-start.11
  54.2 5.2 %copy-start.12 = (s32[512]{0:T(512)S(1)}, s32[512]{0:T(512)}, u32[]{:S(2)}) copy-start(s32[512]{0:T(512)} %param.13) | copy-start | bytes 6148
  54.2 16.1 %all-to-all-start = ((bf16[4,1024,128]{2,1,0:T(8,128)(2,1)}), bf16[4,1024,128]{2,1,0:T(8,128)(2,1)S(1)}, u32[]{:S(2)}, u32[]{:S(2)}) async-start(bf16[4,1024,128]{2,1,0:T(8,128)(2,1)} %broadcast_in_dim.83), calls=%async_computation | async-start | bytes 2097152 | tf_op jit(solution)/shard_map/all_to_all | solution.py:22
  61.8 14.8 %copy-start.9 = (bf16[512,10]{0,1:T(8,128)(2,1)S(1)}, bf16[512,10]{0,1:T(8,128)(2,1)}, u32[]{:S(2)}) copy-start(bf16[512,10]{0,1:T(8,128)(2,1)} %param.17) | copy-start | bytes 30724
  71.8 8.2 %all-to-all-start.1 = ((bf16[4,40,128]{2,1,0:T(8,128)(2,1)}), bf16[4,40,128]{2,1,0:T(8,128)(2,1)S(1)}, u32[]{:S(2)}, u32[]{:S(2)}) async-start(bf16[4,40,128]{2,1,0:T(8,128)(2,1)} %reshape.184), calls=%async_computation.1 | async-start | bytes 81920 | tf_op jit(solution)/shard_map/all_to_all | solution.py:49
  81.4 30.9 %copy-start.5 = (bf16[512,10]{1,0:T(8,128)(2,1)}, bf16[512,10]{1,0:T(8,128)(2,1)S(1)}, u32[]{:S(2)}) copy-start(bf16[512,10]{1,0:T(8,128)(2,1)S(1)} %add_convert_fusion) | copy-start | bytes 30724
  112.3 3.7 %copy-start.8 = (f32[5120]{0:T(1024)S(1)}, f32[5120]{0:T(1024)}, u32[]{:S(2)}) copy-start(f32[5120]{0:T(1024)} %param.19) | copy-start | bytes 61444
  112.3 4.0 %copy-start.3 = (bf16[2,128,1,10,256]{4,1,3,2,0:T(8,128)(2,1)S(1)}, bf16[2,128,1,10,256]{4,1,3,2,0:T(8,128)(2,1)}, u32[]{:S(2)}) copy-start(bf16[2,128,1,10,256]{4,1,3,2,0:T(8,128)(2,1)} %param.20) | copy-start | bytes 3932164
  112.3 15.9 %all-to-all-start.2 = ((bf16[4,1280,128]{2,1,0:T(8,128)(2,1)}), bf16[4,1280,128]{2,1,0:T(8,128)(2,1)S(1)}, u32[]{:S(2)}, u32[]{:S(2)}) async-start(bf16[4,1280,128]{2,1,0:T(8,128)(2,1)} %broadcast_in_dim.86), calls=%async_computation.2 | async-start | bytes 2621440 | tf_op jit(solution)/shard_map/all_to_all | solution.py:22
  133.3 1.6 copy-start.4
  137.3 17.4 %copy-start.7 = (bf16[256,128,1,10]{1,0,3,2:T(8,128)(2,1)S(1)}, bf16[256,128,1,10]{1,0,3,2:T(8,128)(2,1)}, u32[]{:S(2)}) copy-start(bf16[256,128,1,10]{1,0,3,2:T(8,128)(2,1)} %param.21) | copy-start | bytes 1966084
  149.2 10.1 %all-to-all-start.4 = ((bf16[4,64,512]{2,1,0:T(8,128)(2,1)}), bf16[4,64,512]{2,1,0:T(8,128)(2,1)S(1)}, u32[]{:S(2)}, u32[]{:S(2)}) async-start(bf16[4,64,512]{2,1,0:T(8,128)(2,1)} %broadcast_in_dim.88), calls=%async_computation.4 | async-start | bytes 524288 | tf_op jit(solution)/shard_map/all_to_all | solution.py:177
  166.9 36.4 %copy-start.6 = (bf16[512,10]{1,0:T(8,128)(2,1)S(1)}, bf16[512,10]{1,0:T(8,128)(2,1)}, u32[]{:S(2)}) copy-start(bf16[512,10]{1,0:T(8,128)(2,1)} %copy-done.5) | copy-start | bytes 30724

commit v5 on v4

--- a/solution.py
+++ b/solution.py
@@ -1,6 +1,8 @@
 import jax
 import jax.numpy as jnp
 from jax import lax
+from jax.experimental import pallas as pl
+from jax.experimental.pallas import tpu as pltpu
 from jax.sharding import Mesh, PartitionSpec as P
 
 D = 5120
@@ -48,6 +50,96 @@
     blocks = value.astype(wire).reshape((count, height * value.shape[1] // 128, 128))
     moved = lax.all_to_all(blocks, "mdl", 0, 0, tiled=True)
     return moved.astype(jnp.float32).sum(0).reshape(height, value.shape[1])
+
+
+CHUNK_ROWS = 256
+
+
+def attention_kernel(lengths_ref, query_ref, fresh_ref, cache_hbm, out_ref, keys, values, sems):
+    rows = keys.shape[0]
+    chunks = rows // CHUNK_ROWS
+    copies = []
+    for chunk in range(chunks):
+        window = pl.ds(chunk * CHUNK_ROWS, CHUNK_ROWS)
+        for which, target in ((0, keys), (1, values)):
+            copy = pltpu.make_async_copy(cache_hbm.at[which, window], target.at[window], sems.at[which, chunk])
+            copy.start()
+            copies.append(copy)
+    slot_count = lengths_ref.shape[0]
+    kv_heads, row_count, head_dim = query_ref.shape
+    group_width = row_count // slot_count
+    row_slot = lax.broadcasted_iota(jnp.int32, (row_count, 1), 0) // group_width
+    first = jnp.zeros((row_count, 1), jnp.int32)
+    end = jnp.zeros((row_count, 1), jnp.int32)
+    start = jnp.int32(0)
+    for slot in range(slot_count):
+        length = lengths_ref[slot]
+        first = jnp.where(row_slot == slot, start, first)
+        end = jnp.where(row_slot == slot, start + length, end)
+        start = start + length + 1
+    columns = lax.broadcasted_iota(jnp.int32, (row_count, rows), 1)
+    inside = (columns >= first) & (columns < end)
+    pick = (lax.broadcasted_iota(jnp.int32, (row_count, slot_count), 1) == row_slot)
+    for copy in copies:
+        copy.wait()
+    score_scale = head_dim ** (-0.5)
+    for head in range(kv_heads):
+        lanes = pl.ds(head * head_dim, head_dim)
+        query_rows = query_ref[head]
+        scores = lax.dot_general(
+            query_rows, keys[:, lanes], (((1,), (1,)), ((), ())), preferred_element_type=jnp.float32
+        ) * score_scale
+        fresh_scores = lax.dot_general(
+            query_rows, fresh_ref[0, head], (((1,), (1,)), ((), ())), preferred_element_type=jnp.float32
+        ) * score_scale
+        new_score = jnp.sum(jnp.where(pick, fresh_scores, 0.0), axis=1, keepdims=True)
+        scores = jnp.where(inside, scores, NEGATIVE_FILL)
+        top = jnp.maximum(jnp.max(scores, axis=1, keepdims=True), new_score)
+        weights = jnp.where(inside, jnp.exp(scores - top), 0.0)
+        new_weight = jnp.exp(new_score - top)
+        denominator = jnp.sum(weights, axis=1, keepdims=True) + new_weight
+        mixed = jnp.dot(weights.astype(jnp.bfloat16), values[:, lanes], preferred_element_type=jnp.float32)
+        fresh_values = jnp.dot(pick.astype(jnp.bfloat16), fresh_ref[1, head], preferred_element_type=jnp.float32)
+        mixed = mixed + new_weight.astype(jnp.bfloat16).astype(jnp.float32) * fresh_values
+        out_ref[head] = (mixed / denominator).astype(out_ref.dtype)
+
+
+def attend_kernel(lengths, query, key_value_fresh, kv_cache):
+    slot_count = lengths.shape[0]
+    kv_width = kv_cache.shape[2]
+    kv_heads = kv_width // HEAD_SIZE
+    group_width = QUERY_HEADS // KEY_VALUE_HEADS
+    rows = kv_cache.shape[1]
+    query_rows = jnp.transpose(
+        query.reshape(slot_count, kv_heads, group_width, HEAD_SIZE), (1, 0, 2, 3)
+    ).reshape(kv_heads, slot_count * group_width, HEAD_SIZE)
+    fresh = jnp.transpose(
+        key_value_fresh.reshape(2, slot_count, kv_heads, HEAD_SIZE), (0, 2, 1, 3)
+    )
+    out = pl.pallas_call(
+        attention_kernel,
+        out_shape=jax.ShapeDtypeStruct(query_rows.shape, jnp.bfloat16),
+        in_specs=[
+            pl.BlockSpec(memory_space=pltpu.SMEM),
+            pl.BlockSpec(memory_space=pltpu.VMEM),
+            pl.BlockSpec(memory_space=pltpu.VMEM),
+            pl.BlockSpec(memory_space=pl.ANY),
+        ],
+        out_specs=pl.BlockSpec(memory_space=pltpu.VMEM),
+        scratch_shapes=[
+            pltpu.VMEM((rows, kv_width), kv_cache.dtype),
+            pltpu.VMEM((rows, kv_width), kv_cache.dtype),
+            pltpu.SemaphoreType.DMA((2, rows // CHUNK_ROWS)),
+        ],
+        cost_estimate=pl.CostEstimate(
+            flops=4 * kv_heads * slot_count * group_width * rows * HEAD_SIZE,
+            transcendentals=kv_heads * slot_count * group_width * rows,
+            bytes_accessed=2 * rows * kv_width * 2,
+        ),
+    )(lengths, query_rows, fresh, kv_cache)
+    return jnp.transpose(
+        out.reshape(kv_heads, slot_count, group_width, HEAD_SIZE), (1, 0, 2, 3)
+    ).reshape(slot_count, kv_heads * group_width * HEAD_SIZE)
 
 
 def slot_bounds(lengths):
@@ -123,15 +215,7 @@
         )
     kv_heads = key_value_store.shape[2] // HEAD_SIZE
     group_width = QUERY_HEADS // KEY_VALUE_HEADS
-    query_rows = query.reshape(slot_count, kv_heads, group_width, HEAD_SIZE)
-    joint_max, denominator, accumulated = attend_rows(
-        query_rows, key_value_store, 0, first_rows, end_rows
-    )
-    attended = (
-        (accumulated / denominator[..., None])
-        .astype(jnp.bfloat16)
-        .reshape(slot_count, kv_heads * group_width * HEAD_SIZE)
-    )
+    attended = attend_kernel(lengths, query, key_value_fresh, kv_cache)
     all_attended = gather_rows(attended).reshape(-1, attended.shape[1])
     projected = jnp.dot(all_attended, out_weight, preferred_element_type=jnp.float32)
     head_share = mdl_scatter_sum(projected.T, jnp.bfloat16).T

time: 206 us -> 201 us (0.976)
  blocking collectives: 123 us -> 98.1 us
  starting transfers between devices: 19.1 us -> 26.2 us
  local copies, waits for them, and re-layouts: 21.3 us -> 28.1 us
  waiting for transfers between devices: 24.5 us -> 28.3 us
  Pallas kernels: 0 us -> 3.38 us
    all_to_all x3 -> x2, blocking collectives: 40.9 us -> 18.8 us  [scatter_sum(): lax.all_to_all(parts.astype(jnp.bfloat16), name, position, position, tile...]
    all_to_all x0 -> x1, starting transfers between devices: none -> 7.72 us  [scatter_sum(): lax.all_to_all(parts.astype(jnp.bfloat16), name, position, position, tile...]
    dynamic_update_slice x4, local copies, waits for them, and re-layouts: 0.15 us -> 5.27 us  [body(): lax.dynamic_update_slice(key_value_store, key_value_fresh[:, slot_index:s...]
    all_to_all x0 -> x1, waiting for transfers between devices: none -> 3.87 us  [scatter_sum(): lax.all_to_all(parts.astype(jnp.bfloat16), name, position, position, tile...]
    pallas_call x0 -> x1, Pallas kernels: none -> 3.38 us  [attend_kernel(): pl.pallas_call(attention_kernel, out_shape=jax.ShapeDtypeStruct(query_row...]
    all_gather x2, blocking collectives: 67.1 us -> 64.6 us  [gather_rows(): flat = lax.all_gather(flat, 'z', axis=0, tiled=True)]
    unnamed x31 -> x28, local copies, waits for them, and re-layouts: 5.9 us -> 6.81 us
  transfers between devices with their start and end apart: 4 -> 5, of which waited for: 4 -> 5; matrix products, arithmetic and copies ran while one was open for 3% -> 6% of each run, Pallas kernels for 0% -> 0%
where the time goes in v5:
time: 201 us; the launch traced here: 198 us
  blocking collectives  98.1 us (49%)
  waiting for transfers between devices  28.3 us (14%)
  local copies, waits for them, and re-layouts  28.1 us (14%)
  starting transfers between devices  26.2 us (13%)
  between operations  5.96 us (3%)
  other arithmetic  4.77 us (2%)
  Pallas kernels  3.38 us (2%)
  matrix products  3.18 us (2%)
    all_gather x2, blocking collectives, gather_rows(): flat = lax.all_gather(flat, 'z', axis=0, tiled=True)  64.6 us
    all_to_all x2, blocking collectives, scatter_sum(): lax.all_to_all(parts.astype(jnp.bfloat16), name, position, position, tile...  18.8 us
    all_to_all x2, waiting for transfers between devices, gather_rows(): lax.all_to_all(copies, 'y', 0, 0, tiled=True).reshape((count,) + part.shape)  17.8 us
    all_to_all x1, blocking collectives, body(): lax.all_to_all(payload, 'mdl', 0, 0, tiled=True).astype(jnp.float32).sum(0)  11.1 us
    all_to_all x2, starting transfers between devices, gather_rows(): lax.all_to_all(copies, 'y', 0, 0, tiled=True).reshape((count,) + part.shape)  8.27 us
    all_to_all x1, starting transfers between devices, scatter_sum(): lax.all_to_all(parts.astype(jnp.bfloat16), name, position, position, tile...  7.72 us
    unnamed x28, local copies, waits for them, and re-layouts  6.81 us
    all_to_all x1, starting transfers between devices, body(): lax.all_to_all(hidden_copies, 'mdl', 0, 0, tiled=True)  5.45 us
  transfers between devices with their start and end apart: 5, of which 5 were waited for; matrix products, arithmetic and copies ran while one was open for 6% of the time, Pallas kernels for 0%

profile of v5, /device:TPU:6, one launch (start us, length us, event | category | flops | bytes accessed | tf_op | source)
XLA Modules:
  0.0 198.0 jit_solution(17639234146183439431)
XLA Ops:
  0.6 0.0 copy-start
  0.7 2.3 %copy.53.cache_hbm = bf16[2,1024,256]{2,1,0:T(8,128)(2,1)} copy(bf16[2,1024,256]{2,1,0:T(8,128)(2,1)} %param.14) | data formatting | bytes 2097152
  3.0 0.6 copy.28
  3.6 3.4 %shard_map.113 = bf16[2,16,128]{2,1,0:T(8,128)(2,1)} custom-call(s32[4]{0:T(128)} %lengths_ref.1, bf16[2,16,128]{2,1,0:T(8,128)(2,1)} %bitcast.67, bf16[2,2,4,128]{3,2,1,0:T(4,128)(2,1)} %bitcast.66, bf16[2,1024,256]{2,1,0:T(8,128)(2,1)} %copy.53.cache_hbm), custom_call_target="tpu_custom_call" | custom-call | flops 16777216 | bytes 1048576 | tf_op jit(solution)/shard_map/pallas_call | solution.py:119
  7.0 0.7 copy.29
  7.7 1.8 all_gather.12
  9.5 36.8 %all_gather.13 = bf16[1024,128]{1,0:T(8,128)(2,1)S(1)} all-gather(bf16[64,128]{1,0:T(8,128)(2,1)S(1)} %all_gather.12), channel_id=1, replica_groups=mesh['y'=4,'z'=16,'c'=2,'mdl'=4] {'z'}, dimensions={0}, use_global_device_ids=true | all-gather | bytes 278528 | tf_op jit(solution)/shard_map/all_gather | solution.py:22
  46.2 1.1 broadcast_in_dim.24
  47.4 4.6 %all-to-all-start = ((bf16[4,1024,128]{2,1,0:T(8,128)(2,1)}), bf16[4,1024,128]{2,1,0:T(8,128)(2,1)S(1)}, u32[]{:S(2)}, u32[]{:S(2)}) async-start(bf16[4,1024,128]{2,1,0:T(8,128)(2,1)} %broadcast_in_dim.24), calls=%async_computation | async-start | bytes 2097152 | tf_op jit(solution)/shard_map/all_to_all | solution.py:24
  52.0 2.4 %scatter_custom_fusion = s32[512]{0:T(512)S(1)} fusion(s32[512]{0:T(512)S(1)} %compare_select_fusion.1, s32[512]{0:T(512)S(1)} %iota.3, s32[]{:T(128)} %constant.52.clone.1), kind=kCustom, calls=%fused_computation.33 | custom fusion | bytes 2052 | tf_op jit(solution)/shard_map/scatter | solution.py:226
  54.4 0.0 copy-start.8
  54.4 8.4 %all-to-all-done = bf16[4,1024,128]{2,1,0:T(8,128)(2,1)S(1)} async-done(((bf16[4,1024,128]{2,1,0:T(8,128)(2,1)}), bf16[4,1024,128]{2,1,0:T(8,128)(2,1)S(1)}, u32[]{:S(2)}, u32[]{:S(2)}) %all-to-all-start) | async-done | bytes 1048608 | tf_op jit(solution)/shard_map/all_to_all | solution.py:24
  62.8 0.5 reshape_reshape.7
  63.3 0.4 fusion.10
  63.8 0.6 reshape.141
  64.4 4.8 %all-to-all-start.1 = ((bf16[4,40,128]{2,1,0:T(8,128)(2,1)}), bf16[4,40,128]{2,1,0:T(8,128)(2,1)S(1)}, u32[]{:S(2)}, u32[]{:S(2)}) async-start(bf16[4,40,128]{2,1,0:T(8,128)(2,1)} %reshape.141), calls=%async_computation.1 | async-start | bytes 81920 | tf_op jit(solution)/shard_map/all_to_all | solution.py:51
  69.2 0.1 copy.31
  69.3 3.3 %all-to-all-done.1 = bf16[4,40,128]{2,1,0:T(8,128)(2,1)S(1)} async-done(((bf16[4,40,128]{2,1,0:T(8,128)(2,1)}), bf16[4,40,128]{2,1,0:T(8,128)(2,1)S(1)}, u32[]{:S(2)}, u32[]{:S(2)}) %all-to-all-start.1) | async-done | bytes 40992 | tf_op jit(solution)/shard_map/all_to_all | solution.py:51
  72.6 0.1 copy.30
  72.8 1.0 gather_fusion
  73.8 0.1 add_convert_fusion
  74.0 0.1 copy.32
  74.1 1.8 all_gather.14
  75.9 27.8 %all_gather.15 = bf16[1280,128]{1,0:T(8,128)(2,1)S(1)} all-gather(bf16[80,128]{1,0:T(8,128)(2,1)S(1)} %all_gather.14), channel_id=1, replica_groups=mesh['y'=4,'z'=16,'c'=2,'mdl'=4] {'z'}, dimensions={0}, use_global_device_ids=true | all-gather | bytes 348160 | tf_op jit(solution)/shard_map/all_gather | solution.py:22
  103.8 1.2 broadcast_in_dim.48
  105.0 3.7 %all-to-all-start.2 = ((bf16[4,1280,128]{2,1,0:T(8,128)(2,1)}), bf16[4,1280,128]{2,1,0:T(8,128)(2,1)S(1)}, u32[]{:S(2)}, u32[]{:S(2)}) async-start(bf16[4,1280,128]{2,1,0:T(8,128)(2,1)} %broadcast_in_dim.48), calls=%async_computation.2 | async-start | bytes 2621440 | tf_op jit(solution)/shard_map/all_to_all | solution.py:24
  108.7 0.3 reshape.144
  109.0 2.4 %copy.33 = bf16[2,128,1,10,256]{4,0,3,1,2:T(2,128)(2,1)} copy(bf16[2,128,1,10,256]{4,1,3,2,0:T(8,128)(2,1)S(1)} %copy-done.1) | data formatting | bytes 2621440 | tf_op args[8]
  111.4 0.1 constant_dynamic-slice_fusion
  111.5 9.4 %all-to-all-done.2 = bf16[4,1280,128]{2,1,0:T(8,128)(2,1)S(1)} async-done(((bf16[4,1280,128]{2,1,0:T(8,128)(2,1)}), bf16[4,1280,128]{2,1,0:T(8,128)(2,1)S(1)}, u32[]{:S(2)}, u32[]{:S(2)}) %all-to-all-start.2) | async-done | bytes 1310752 | tf_op jit(solution)/shard_map/all_to_all | solution.py:24
  121.0 2.3 %reshape.151 = f32[128,10,512]{2,1,0:T(8,128)} reshape(bf16[4,1280,128]{2,1,0:T(8,128)(2,1)S(1)} %all-to-all-done.2) | data formatting | bytes 3932160 | tf_op jit(solution)/shard_map/convert_element_type | solution.py:235
  123.2 2.8 %fusion.1 = (bf16[512,128,10]{0,2,1:T(8,128)(2,1)S(1)}, f32[512]{0:T(512)S(1)}) fusion(f32[128,10,512]{2,1,0:T(8,128)} %reshape.151, f32[128,10]{1,0:T(8,128)S(1)} %bitcast.65), kind=kLoop, calls=%fused_computation.6 | loop fusion | flops 2620928 | bytes 3939328 | tf_op jit(solution)/shard_map/convert_element_type | solution.py:241
  126.0 1.3 convert_element_type.133
  127.3 0.3 copy-done.2
  127.6 2.2 %fusion.5 = bf16[512,2,256]{0,2,1:T(8,128)(2,1)S(1)} fusion(bf16[2,1280,256]{2,0,1:T(2,128)(2,1)S(1)} %bitcast.61, bf16[512,1280]{0,1:T(8,128)(2,1)} %convert_element_type.133), kind=kOutput, calls=%fused_computation.10 | convolution fusion | flops 671350784 | bytes 3145728 | tf_op jit(solution)/shard_map/rk,gkf->gfr/dot_general | solution.py:243
  130.0 0.0 copy-start.5
  130.0 11.1 %all_to_all.40 = bf16[4,130,512]{2,1,0:T(8,128)(2,1)S(1)} all-to-all(bf16[4,130,512]{2,1,0:T(8,128)(2,1)S(1)} %pad_maximum_fusion), channel_id=1, replica_groups=mesh['y'=4,'z'=16,'c'=2,'mdl'=4] {'mdl'}, dimensions={0} | all-to-all | bytes 1064960 | tf_op jit(solution)/shard_map/all_to_all | solution.py:254
  141.1 0.1 convert_reduce_fusion
  141.2 0.1 fusion.13
  141.2 0.7 broadcast_in_dim.50
  141.9 5.5 %all-to-all-start.4 = ((bf16[4,64,512]{2,1,0:T(8,128)(2,1)}), bf16[4,64,512]{2,1,0:T(8,128)(2,1)S(1)}, u32[]{:S(2)}, u32[]{:S(2)}) async-start(bf16[4,64,512]{2,1,0:T(8,128)(2,1)} %broadcast_in_dim.50), calls=%async_computation.4 | async-start | bytes 524288 | tf_op jit(solution)/shard_map/all_to_all | solution.py:261
  147.4 1.0 copy.37
  148.4 0.2 reshape.149
  148.7 3.3 %all-to-all-done.4 = bf16[4,64,512]{2,1,0:T(8,128)(2,1)S(1)} async-done(((bf16[4,64,512]{2,1,0:T(8,128)(2,1)}), bf16[4,64,512]{2,1,0:T(8,128)(2,1)S(1)}, u32[]{:S(2)}, u32[]{:S(2)}) %all-to-all-start.4) | async-done | bytes 262176 | tf_op jit(solution)/shard_map/all_to_all | solution.py:261
  152.0 0.6 fusion
  152.5 0.7 copy.38
  153.2 0.8 convert_element_type.143
  154.0 0.1 copy.39
  154.2 4.8 %all_to_all.41 = bf16[4,16,2,40,128]{4,3,1,0,2:T(8,128)(2,1)S(1)} all-to-all(bf16[4,16,2,40,128]{4,3,1,0,2:T(8,128)(2,1)S(1)} %copy.39), channel_id=1, replica_groups=mesh['y'=4,'z'=16,'c'=2,'mdl'=4] {'c'}, dimensions={2} | all-to-all | bytes 2621440 | tf_op jit(solution)/shard_map/all_to_all | solution.py:30
  159.0 0.6 reduce_sum.66
  159.6 0.0 copy-start.11
  159.6 0.0 copy-start.6
  159.6 14.0 %all_to_all.42 = bf16[4,16,1,40,128]{4,3,1,2,0:T(8,128)(2,1)S(1)} all-to-all(bf16[4,16,1,40,128]{4,3,1,2,0:T(8,128)(2,1)S(1)} %bitcast.59), channel_id=1, replica_groups=mesh['y'=4,'z'=16,'c'=2,'mdl'=4] {'y'}, dimensions={0} | all-to-all | bytes 1310720 | tf_op jit(solution)/shard_map/all_to_all | solution.py:30
  173.6 0.8 reduce_sum.67
  174.4 7.7 %all-to-all-start.7 = ((bf16[1,16,1,40,128]{4,3,2,0,1:T(8,128)(2,1)}), bf16[1,16,1,40,128]{4,3,2,0,1:T(8,128)(2,1)S(1)}, u32[]{:S(2)}, u32[]{:S(2)}) async-start(bf16[1,16,1,40,128]{4,3,2,0,1:T(8,128)(2,1)} %bitcast.23), calls=%async_computation.7 | async-start | bytes 327680 | tf_op jit(solution)/shard_map/all_to_all | solution.py:30
  182.1 0.2 reduce-window.4
  182.3 0.6 fusion.18
  187.9 1.3 dynamic_update_slice.12
  189.2 1.3 dynamic_update_slice.13
  190.5 1.3 dynamic_update_slice.14
  191.8 1.3 dynamic_update_slice.15
  193.1 3.9 %all-to-all-done.7 = bf16[1,16,1,40,128]{4,3,2,0,1:T(8,128)(2,1)S(1)} async-done(((bf16[1,16,1,40,128]{4,3,2,0,1:T(8,128)(2,1)}), bf16[1,16,1,40,128]{4,3,2,0,1:T(8,128)(2,1)S(1)}, u32[]{:S(2)}, u32[]{:S(2)}) %all-to-all-start.7) | async-done | bytes 163872 | tf_op jit(solution)/shard_map/all_to_all | solution.py:30
  197.0 0.1 copy.40
  197.2 0.7 copy.41
  (39 shorter events, 0.3 us)
Async XLA Ops:
  0.6 62.7 %copy-start = (bf16[1024,40]{0,1:T(8,128)(2,1)S(1)}, bf16[1024,40]{0,1:T(8,128)(2,1)}, u32[]{:S(2)}) copy-start(bf16[1024,40]{0,1:T(8,128)(2,1)} %param.16) | copy-start | bytes 245764
  0.6 2.3 %copy-start.9 = (bf16[4,1024]{1,0:T(4,128)(2,1)S(1)}, bf16[4,1024]{1,0:T(4,128)(2,1)}, u32[]{:S(2)}) copy-start(bf16[4,1024]{1,0:T(4,128)(2,1)} %param.12) | copy-start | bytes 24580
  47.4 4.6 %copy-start.10 = (s32[512]{0:T(512)S(1)}, s32[512]{0:T(512)}, u32[]{:S(2)}) copy-start(s32[512]{0:T(512)} %param.11) | copy-start | bytes 6148
  47.4 15.5 %all-to-all-start = ((bf16[4,1024,128]{2,1,0:T(8,128)(2,1)}), bf16[4,1024,128]{2,1,0:T(8,128)(2,1)S(1)}, u32[]{:S(2)}, u32[]{:S(2)}) async-start(bf16[4,1024,128]{2,1,0:T(8,128)(2,1)} %broadcast_in_dim.24), calls=%async_computation | async-start | bytes 2097152 | tf_op jit(solution)/shard_map/all_to_all | solution.py:24
  54.4 14.8 %copy-start.8 = (bf16[512,10]{0,1:T(8,128)(2,1)S(1)}, bf16[512,10]{0,1:T(8,128)(2,1)}, u32[]{:S(2)}) copy-start(bf16[512,10]{0,1:T(8,128)(2,1)} %param.15) | copy-start | bytes 30724
  64.4 8.2 %all-to-all-start.1 = ((bf16[4,40,128]{2,1,0:T(8,128)(2,1)}), bf16[4,40,128]{2,1,0:T(8,128)(2,1)S(1)}, u32[]{:S(2)}, u32[]{:S(2)}) async-start(bf16[4,40,128]{2,1,0:T(8,128)(2,1)} %reshape.141), calls=%async_computation.1 | async-start | bytes 81920 | tf_op jit(solution)/shard_map/all_to_all | solution.py:51
  74.0 31.0 %copy-start.3 = (bf16[512,10]{1,0:T(8,128)(2,1)}, bf16[512,10]{1,0:T(8,128)(2,1)S(1)}, u32[]{:S(2)}) copy-start(bf16[512,10]{1,0:T(8,128)(2,1)S(1)} %add_convert_fusion) | copy-start | bytes 30724
  105.0 3.7 %copy-start.7 = (f32[5120]{0:T(1024)S(1)}, f32[5120]{0:T(1024)}, u32[]{:S(2)}) copy-start(f32[5120]{0:T(1024)} %param.17) | copy-start | bytes 61444
  105.0 4.0 %copy-start.1 = (bf16[2,128,1,10,256]{4,1,3,2,0:T(8,128)(2,1)S(1)}, bf16[2,128,1,10,256]{4,1,3,2,0:T(8,128)(2,1)}, u32[]{:S(2)}) copy-start(bf16[2,128,1,10,256]{4,1,3,2,0:T(8,128)(2,1)} %param.18) | copy-start | bytes 3932164
  105.0 15.9 %all-to-all-start.2 = ((bf16[4,1280,128]{2,1,0:T(8,128)(2,1)}), bf16[4,1280,128]{2,1,0:T(8,128)(2,1)S(1)}, u32[]{:S(2)}, u32[]{:S(2)}) async-start(bf16[4,1280,128]{2,1,0:T(8,128)(2,1)} %broadcast_in_dim.48), calls=%async_computation.2 | async-start | bytes 2621440 | tf_op jit(solution)/shard_map/all_to_all | solution.py:24
  126.0 1.6 copy-start.2
  130.0 17.4 %copy-start.5 = (bf16[256,128,1,10]{1,0,3,2:T(8,128)(2,1)S(1)}, bf16[256,128,1,10]{1,0,3,2:T(8,128)(2,1)}, u32[]{:S(2)}) copy-start(bf16[256,128,1,10]{1,0,3,2:T(8,128)(2,1)} %param.19) | copy-start | bytes 1966084
  141.9 10.1 %all-to-all-start.4 = ((bf16[4,64,512]{2,1,0:T(8,128)(2,1)}), bf16[4,64,512]{2,1,0:T(8,128)(2,1)S(1)}, u32[]{:S(2)}, u32[]{:S(2)}) async-start(bf16[4,64,512]{2,1,0:T(8,128)(2,1)} %broadcast_in_dim.50), calls=%async_computation.4 | async-start | bytes 524288 | tf_op jit(solution)/shard_map/all_to_all | solution.py:261
  159.6 22.5 %copy-start.11 = (s32[4]{0:T(128)S(1)}, s32[4]{0:T(128)}, u32[]{:S(2)}) copy-start(s32[4]{0:T(128)} %lengths_ref.1) | copy-start | bytes 52
  159.6 28.3 %copy-start.6 = (bf16[2,4,256]{2,1,0:T(4,128)(2,1)S(1)}, bf16[2,4,256]{2,1,0:T(4,128)(2,1)}, u32[]{:S(2)}) copy-start(bf16[2,4,256]{2,1,0:T(4,128)(2,1)} %param.13) | copy-start | bytes 12292
  159.6 37.6 %copy-start.4 = (bf16[512,10]{1,0:T(8,128)(2,1)S(1)}, bf16[512,10]{1,0:T(8,128)(2,1)}, u32[]{:S(2)}) copy-start(bf16[512,10]{1,0:T(8,128)(2,1)} %copy-done.3) | copy-start | bytes 30724
  174.4 22.6 %all-to-all-start.7 = ((bf16[1,16,1,40,128]{4,3,2,0,1:T(8,128)(2,1)}), bf16[1,16,1,40,128]{4,3,2,0,1:T(8,128)(2,1)S(1)}, u32[]{:S(2)}, u32[]{:S(2)}) async-start(bf16[1,16,1,40,128]{4,3,2,0,1:T(8,128)(2,1)} %bitcast.23), calls=%async_computation.7 | async-start | bytes 327680 | tf_op jit(solution)/shard_map/all_to_all | solution.py:30

commit v6 on v5

--- a/solution.py
+++ b/solution.py
@@ -216,9 +216,22 @@
     kv_heads = key_value_store.shape[2] // HEAD_SIZE
     group_width = QUERY_HEADS // KEY_VALUE_HEADS
     attended = attend_kernel(lengths, query, key_value_fresh, kv_cache)
-    all_attended = gather_rows(attended).reshape(-1, attended.shape[1])
-    projected = jnp.dot(all_attended, out_weight, preferred_element_type=jnp.float32)
-    head_share = mdl_scatter_sum(projected.T, jnp.bfloat16).T
+    y_count, mdl_count = lax.axis_size("y"), lax.axis_size("mdl")
+    weight_copies = jnp.broadcast_to(out_weight.T[None], (y_count,) + out_weight.T.shape)
+    row_weight = lax.all_to_all(weight_copies, "y", 0, 0, tiled=True).reshape(-1, out_weight.shape[0])
+    flat = attended.reshape(-1, 128)
+    flat = lax.all_gather(flat, "c", axis=0, tiled=True)
+    flat = lax.all_gather(flat, "z", axis=0, tiled=True)
+    row_attended = flat.reshape(-1, attended.shape[1])
+    row_slots = row_attended.shape[0]
+    sub_width = hidden_in.shape[1]
+    row_projected = lax.dot_general(
+        row_weight, row_attended, (((1,), (1,)), ((), ())), preferred_element_type=jnp.float32
+    )
+    outgoing = row_projected.astype(jnp.bfloat16).reshape(y_count * mdl_count, sub_width, row_slots)
+    arrived = lax.all_to_all(outgoing, ("y", "mdl"), 0, 0, tiled=True)
+    head_sum = arrived.astype(jnp.float32).reshape(y_count, mdl_count, sub_width, row_slots).sum(1)
+    head_share = jnp.transpose(head_sum, (1, 0, 2)).reshape(sub_width, y_count * row_slots).T
     total_rows = assignment.shape[0]
     inverse = (
         jnp.zeros((total_rows,), jnp.int32)

time: 201 us -> 196 us (0.975)
  waiting for transfers between devices: 28.3 us -> 22.1 us
  starting transfers between devices: 26.2 us -> 29.1 us
    all_gather x0 -> x2, blocking collectives: none -> 38.6 us  [the longest x1 36.8 us: body(): flat = lax.all_gather(flat, 'z', axis=0, tiled=True)]
    all_gather x2 -> x1, blocking collectives: 64.6 us -> 27.8 us  [gather_rows(): flat = lax.all_gather(flat, 'z', axis=0, tiled=True)]
    all_to_all x2 -> x1, waiting for transfers between devices: 17.8 us -> 9.45 us  [gather_rows(): lax.all_to_all(copies, 'y', 0, 0, tiled=True).reshape((count,) + part.shape)]
    all_to_all x1 -> x2, starting transfers between devices: 4.77 us -> 12.2 us  [the longest x1 7.75 us: body(): arrived = lax.all_to_all(outgoing, ('y', 'mdl'), 0, 0, tiled=True)]
    all_to_all x2 -> x1, starting transfers between devices: 8.27 us -> 3.67 us  [gather_rows(): lax.all_to_all(copies, 'y', 0, 0, tiled=True).reshape((count,) + part.shape)]
    all_to_all x1 -> x2, waiting for transfers between devices: 3.28 us -> 5.55 us  [the longest x1 5.55 us: body(): arrived = lax.all_to_all(outgoing, ('y', 'mdl'), 0, 0, tiled=True)]
    unnamed x28 -> x24, local copies, waits for them, and re-layouts: 6.81 us -> 6.79 us
  transfers between devices with their start and end apart: 5 -> 5, of which waited for: 5 -> 4; matrix products, arithmetic and copies ran while one was open for 6% -> 7% of each run, Pallas kernels for 0% -> 2%
where the time goes in v6:
time: 196 us; the launch traced here: 194 us
  blocking collectives  98 us (50%)
  starting transfers between devices  29.1 us (15%)
  local copies, waits for them, and re-layouts  27.3 us (14%)
  waiting for transfers between devices  22.1 us (11%)
  between operations  5.97 us (3%)
  other arithmetic  4.77 us (2%)
  Pallas kernels  3.46 us (2%)
  matrix products  3 us (2%)
    all_gather x1, blocking collectives, body(): flat = lax.all_gather(flat, 'z', axis=0, tiled=True)  36.8 us
    all_gather x1, blocking collectives, gather_rows(): flat = lax.all_gather(flat, 'z', axis=0, tiled=True)  27.8 us
    all_to_all x2, blocking collectives, scatter_sum(): lax.all_to_all(parts.astype(jnp.bfloat16), name, position, position, tile...  18.7 us
    all_to_all x1, blocking collectives, body(): lax.all_to_all(payload, 'mdl', 0, 0, tiled=True).astype(jnp.float32).sum(0)  11.1 us
    all_to_all x1, waiting for transfers between devices, gather_rows(): lax.all_to_all(copies, 'y', 0, 0, tiled=True).reshape((count,) + part.shape)  9.45 us
    all_to_all x1, starting transfers between devices, body(): arrived = lax.all_to_all(outgoing, ('y', 'mdl'), 0, 0, tiled=True)  7.75 us
    all_to_all x1, starting transfers between devices, scatter_sum(): lax.all_to_all(parts.astype(jnp.bfloat16), name, position, position, tile...  7.72 us
    unnamed x24, local copies, waits for them, and re-layouts  6.79 us
  transfers between devices with their start and end apart: 5, of which 4 were waited for; matrix products, arithmetic and copies ran while one was open for 7% of the time, Pallas kernels for 2%

profile of v6, /device:TPU:6, one launch (start us, length us, event | category | flops | bytes accessed | tf_op | source)
XLA Modules:
  0.0 193.7 jit_solution(16557633894900869645)
XLA Ops:
  0.7 2.3 %copy.52.cache_hbm = bf16[2,1024,256]{2,1,0:T(8,128)(2,1)} copy(bf16[2,1024,256]{2,1,0:T(8,128)(2,1)} %param.14) | data formatting | bytes 2097152
  2.9 0.0 copy-done.3
  3.0 0.7 broadcast_in_dim.24
  3.7 4.5 %all-to-all-start = ((bf16[4,40,1024]{2,1,0:T(8,128)(2,1)}), bf16[4,40,1024]{2,1,0:T(8,128)(2,1)S(1)}, u32[]{:S(2)}, u32[]{:S(2)}) async-start(bf16[4,40,1024]{2,1,0:T(8,128)(2,1)} %broadcast_in_dim.24), calls=%async_computation | async-start | bytes 655360 | tf_op jit(solution)/shard_map/all_to_all | solution.py:221
  8.2 0.6 copy.27
  8.8 3.5 %shard_map.113 = bf16[2,16,128]{2,1,0:T(8,128)(2,1)} custom-call(s32[4]{0:T(128)} %lengths_ref.1, bf16[2,16,128]{2,1,0:T(8,128)(2,1)} %bitcast.78, bf16[2,2,4,128]{3,2,1,0:T(4,128)(2,1)} %bitcast.77, bf16[2,1024,256]{2,1,0:T(8,128)(2,1)} %copy.52.cache_hbm), custom_call_target="tpu_custom_call" | custom-call | flops 16777216 | bytes 1048576 | tf_op jit(solution)/shard_map/pallas_call | solution.py:119
  12.2 0.7 copy.28
  13.0 1.8 all_gather.12
  14.8 2.4 %scatter_custom_fusion = s32[512]{0:T(512)S(1)} fusion(s32[512]{0:T(512)S(1)} %compare_select_fusion.1, s32[512]{0:T(512)S(1)} %iota.3, s32[]{:T(128)} %constant.52.clone.1), kind=kCustom, calls=%fused_computation.33 | custom fusion | bytes 2052 | tf_op jit(solution)/shard_map/scatter | solution.py:239
  17.2 36.8 %all_gather.13 = bf16[1024,128]{1,0:T(8,128)(2,1)S(1)} all-gather(bf16[64,128]{1,0:T(8,128)(2,1)S(1)} %all_gather.12), channel_id=1, replica_groups=mesh['y'=4,'z'=16,'c'=2,'mdl'=4] {'z'}, dimensions={0}, use_global_device_ids=true | all-gather | bytes 278528 | tf_op jit(solution)/shard_map/all_gather | solution.py:224
  54.0 0.1 reshape.153
  54.1 0.0 all-to-all-done
  54.2 0.2 fusion.10
  54.4 0.6 reshape.155
  55.0 7.8 %all-to-all-start.1 = ((bf16[16,10,128]{2,1,0:T(8,128)(2,1)}), bf16[16,10,128]{2,1,0:T(8,128)(2,1)S(1)}, u32[]{:S(2)}, u32[]{:S(2)}) async-start(bf16[16,10,128]{2,1,0:T(8,128)(2,1)} %reshape.155), calls=%async_computation.1 | async-start | bytes 131072 | tf_op jit(solution)/shard_map/all_to_all | solution.py:232
  62.8 0.1 copy.30
  63.0 5.5 %all-to-all-done.1 = bf16[16,10,128]{2,1,0:T(8,128)(2,1)S(1)} async-done(((bf16[16,10,128]{2,1,0:T(8,128)(2,1)}), bf16[16,10,128]{2,1,0:T(8,128)(2,1)S(1)}, u32[]{:S(2)}, u32[]{:S(2)}) %all-to-all-start.1) | async-done | bytes 40992 | tf_op jit(solution)/shard_map/all_to_all | solution.py:232
  68.5 0.1 copy.29
  68.7 1.0 gather_fusion
  69.7 0.1 add_convert_fusion
  69.9 0.1 copy.31
  70.0 1.8 all_gather.14
  71.8 27.8 %all_gather.15 = bf16[1280,128]{1,0:T(8,128)(2,1)S(1)} all-gather(bf16[80,128]{1,0:T(8,128)(2,1)S(1)} %all_gather.14), channel_id=1, replica_groups=mesh['y'=4,'z'=16,'c'=2,'mdl'=4] {'z'}, dimensions={0}, use_global_device_ids=true | all-gather | bytes 348160 | tf_op jit(solution)/shard_map/all_gather | solution.py:22
  99.6 1.2 broadcast_in_dim.48
  100.9 3.7 %all-to-all-start.2 = ((bf16[4,1280,128]{2,1,0:T(8,128)(2,1)}), bf16[4,1280,128]{2,1,0:T(8,128)(2,1)S(1)}, u32[]{:S(2)}, u32[]{:S(2)}) async-start(bf16[4,1280,128]{2,1,0:T(8,128)(2,1)} %broadcast_in_dim.48), calls=%async_computation.2 | async-start | bytes 2621440 | tf_op jit(solution)/shard_map/all_to_all | solution.py:24
  104.6 0.3 reshape.160
  104.9 2.4 %copy.32 = bf16[2,128,1,10,256]{4,0,3,1,2:T(2,128)(2,1)} copy(bf16[2,128,1,10,256]{4,1,3,2,0:T(8,128)(2,1)S(1)} %copy-done) | data formatting | bytes 2621440 | tf_op args[8]
  107.3 0.1 constant_dynamic-slice_fusion
  107.4 9.4 %all-to-all-done.2 = bf16[4,1280,128]{2,1,0:T(8,128)(2,1)S(1)} async-done(((bf16[4,1280,128]{2,1,0:T(8,128)(2,1)}), bf16[4,1280,128]{2,1,0:T(8,128)(2,1)S(1)}, u32[]{:S(2)}, u32[]{:S(2)}) %all-to-all-start.2) | async-done | bytes 1310752 | tf_op jit(solution)/shard_map/all_to_all | solution.py:24
  116.8 2.3 %reshape.169 = f32[128,10,512]{2,1,0:T(8,128)} reshape(bf16[4,1280,128]{2,1,0:T(8,128)(2,1)S(1)} %all-to-all-done.2) | data formatting | bytes 3932160 | tf_op jit(solution)/shard_map/convert_element_type | solution.py:248
  119.1 2.8 %fusion.1 = (bf16[512,128,10]{0,2,1:T(8,128)(2,1)S(1)}, f32[512]{0:T(512)S(1)}) fusion(f32[128,10,512]{2,1,0:T(8,128)} %reshape.169, f32[128,10]{1,0:T(8,128)S(1)} %bitcast.74), kind=kLoop, calls=%fused_computation.6 | loop fusion | flops 2620928 | bytes 3939328 | tf_op jit(solution)/shard_map/convert_element_type | solution.py:254
  121.9 0.0 copy-start.1
  121.9 1.3 convert_element_type.130
  123.2 0.3 copy-done.1
  123.5 2.2 %fusion.5 = bf16[512,2,256]{0,2,1:T(8,128)(2,1)S(1)} fusion(bf16[2,1280,256]{2,0,1:T(2,128)(2,1)S(1)} %bitcast.69, bf16[512,1280]{0,1:T(8,128)(2,1)} %convert_element_type.130), kind=kOutput, calls=%fused_computation.10 | convolution fusion | flops 671350784 | bytes 3145728 | tf_op jit(solution)/shard_map/rk,gkf->gfr/dot_general | solution.py:256
  125.9 0.0 copy-start.2
  125.9 11.1 %all_to_all.40 = bf16[4,130,512]{2,1,0:T(8,128)(2,1)S(1)} all-to-all(bf16[4,130,512]{2,1,0:T(8,128)(2,1)S(1)} %pad_maximum_fusion), channel_id=1, replica_groups=mesh['y'=4,'z'=16,'c'=2,'mdl'=4] {'mdl'}, dimensions={0} | all-to-all | bytes 1064960 | tf_op jit(solution)/shard_map/all_to_all | solution.py:267
  136.9 0.1 convert_reduce_fusion
  137.0 0.1 fusion.13
  137.1 0.7 broadcast_in_dim.50
  137.8 5.5 %all-to-all-start.4 = ((bf16[4,64,512]{2,1,0:T(8,128)(2,1)}), bf16[4,64,512]{2,1,0:T(8,128)(2,1)S(1)}, u32[]{:S(2)}, u32[]{:S(2)}) async-start(bf16[4,64,512]{2,1,0:T(8,128)(2,1)} %broadcast_in_dim.50), calls=%async_computation.4 | async-start | bytes 524288 | tf_op jit(solution)/shard_map/all_to_all | solution.py:274
  143.3 1.0 copy.36
  144.3 0.2 reshape.165
  144.6 3.3 %all-to-all-done.4 = bf16[4,64,512]{2,1,0:T(8,128)(2,1)S(1)} async-done(((bf16[4,64,512]{2,1,0:T(8,128)(2,1)}), bf16[4,64,512]{2,1,0:T(8,128)(2,1)S(1)}, u32[]{:S(2)}, u32[]{:S(2)}) %all-to-all-start.4) | async-done | bytes 262176 | tf_op jit(solution)/shard_map/all_to_all | solution.py:274
  147.9 0.6 fusion
  148.4 0.7 copy.37
  149.1 0.8 convert_element_type.140
  149.9 0.1 copy.38
  150.1 4.8 %all_to_all.41 = bf16[4,16,2,40,128]{4,3,1,0,2:T(8,128)(2,1)S(1)} all-to-all(bf16[4,16,2,40,128]{4,3,1,0,2:T(8,128)(2,1)S(1)} %copy.38), channel_id=1, replica_groups=mesh['y'=4,'z'=16,'c'=2,'mdl'=4] {'c'}, dimensions={2} | all-to-all | bytes 2621440 | tf_op jit(solution)/shard_map/all_to_all | solution.py:30
  154.9 0.6 reduce_sum.66
  155.5 0.0 copy-start.9
  155.5 0.0 copy-start.4
  155.5 13.9 %all_to_all.42 = bf16[4,16,1,40,128]{4,3,1,2,0:T(8,128)(2,1)S(1)} all-to-all(bf16[4,16,1,40,128]{4,3,1,2,0:T(8,128)(2,1)S(1)} %bitcast.67), channel_id=1, replica_groups=mesh['y'=4,'z'=16,'c'=2,'mdl'=4] {'y'}, dimensions={0} | all-to-all | bytes 1310720 | tf_op jit(solution)/shard_map/all_to_all | solution.py:30
  169.4 0.8 reduce_sum.67
  170.1 7.7 %all-to-all-start.7 = ((bf16[1,16,1,40,128]{4,3,2,0,1:T(8,128)(2,1)}), bf16[1,16,1,40,128]{4,3,2,0,1:T(8,128)(2,1)S(1)}, u32[]{:S(2)}, u32[]{:S(2)}) async-start(bf16[1,16,1,40,128]{4,3,2,0,1:T(8,128)(2,1)} %bitcast.28), calls=%async_computation.7 | async-start | bytes 327680 | tf_op jit(solution)/shard_map/all_to_all | solution.py:30
  177.9 0.2 reduce-window.4
  178.1 0.7 fusion.18
  183.7 1.3 dynamic_update_slice.12
  185.0 1.3 dynamic_update_slice.13
  186.3 1.3 dynamic_update_slice.14
  187.6 1.3 dynamic_update_slice.15
  188.9 3.8 %all-to-all-done.7 = bf16[1,16,1,40,128]{4,3,2,0,1:T(8,128)(2,1)S(1)} async-done(((bf16[1,16,1,40,128]{4,3,2,0,1:T(8,128)(2,1)}), bf16[1,16,1,40,128]{4,3,2,0,1:T(8,128)(2,1)S(1)}, u32[]{:S(2)}, u32[]{:S(2)}) %all-to-all-start.7) | async-done | bytes 163872 | tf_op jit(solution)/shard_map/all_to_all | solution.py:30
  192.8 0.1 copy.39
  193.0 0.7 copy.40
  (34 shorter events, 0.3 us)
Async XLA Ops:
  0.6 7.5 %copy-start.7 = (bf16[4,1024]{1,0:T(4,128)(2,1)S(1)}, bf16[4,1024]{1,0:T(4,128)(2,1)}, u32[]{:S(2)}) copy-start(bf16[4,1024]{1,0:T(4,128)(2,1)} %param.12) | copy-start | bytes 24580
  0.6 2.3 %copy-start.3 = (bf16[1024,40]{0,1:T(8,128)(2,1)S(1)}, bf16[1024,40]{0,1:T(8,128)(2,1)}, u32[]{:S(2)}) copy-start(bf16[1024,40]{0,1:T(8,128)(2,1)} %param.16) | copy-start | bytes 245764
  2.9 11.8 %copy-start.8 = (s32[512]{0:T(512)S(1)}, s32[512]{0:T(512)}, u32[]{:S(2)}) copy-start(s32[512]{0:T(512)} %param.11) | copy-start | bytes 6148
  3.7 50.4 %all-to-all-start = ((bf16[4,40,1024]{2,1,0:T(8,128)(2,1)}), bf16[4,40,1024]{2,1,0:T(8,128)(2,1)S(1)}, u32[]{:S(2)}, u32[]{:S(2)}) async-start(bf16[4,40,1024]{2,1,0:T(8,128)(2,1)} %broadcast_in_dim.24), calls=%async_computation | async-start | bytes 655360 | tf_op jit(solution)/shard_map/all_to_all | solution.py:221
  8.8 54.0 %copy-start.6 = (bf16[512,10]{0,1:T(8,128)(2,1)S(1)}, bf16[512,10]{0,1:T(8,128)(2,1)}, u32[]{:S(2)}) copy-start(bf16[512,10]{0,1:T(8,128)(2,1)} %param.15) | copy-start | bytes 30724
  55.0 13.5 %all-to-all-start.1 = ((bf16[16,10,128]{2,1,0:T(8,128)(2,1)}), bf16[16,10,128]{2,1,0:T(8,128)(2,1)S(1)}, u32[]{:S(2)}, u32[]{:S(2)}) async-start(bf16[16,10,128]{2,1,0:T(8,128)(2,1)} %reshape.155), calls=%async_computation.1 | async-start | bytes 131072 | tf_op jit(solution)/shard_map/all_to_all | solution.py:232
  100.9 3.7 %copy-start.5 = (f32[5120]{0:T(1024)S(1)}, f32[5120]{0:T(1024)}, u32[]{:S(2)}) copy-start(f32[5120]{0:T(1024)} %param.17) | copy-start | bytes 61444
  100.9 4.0 %copy-start = (bf16[2,128,1,10,256]{4,1,3,2,0:T(8,128)(2,1)S(1)}, bf16[2,128,1,10,256]{4,1,3,2,0:T(8,128)(2,1)}, u32[]{:S(2)}) copy-start(bf16[2,128,1,10,256]{4,1,3,2,0:T(8,128)(2,1)} %param.18) | copy-start | bytes 3932164
  100.9 15.9 %all-to-all-start.2 = ((bf16[4,1280,128]{2,1,0:T(8,128)(2,1)}), bf16[4,1280,128]{2,1,0:T(8,128)(2,1)S(1)}, u32[]{:S(2)}, u32[]{:S(2)}) async-start(bf16[4,1280,128]{2,1,0:T(8,128)(2,1)} %broadcast_in_dim.48), calls=%async_computation.2 | async-start | bytes 2621440 | tf_op jit(solution)/shard_map/all_to_all | solution.py:24
  121.9 1.6 copy-start.1
  125.9 17.4 %copy-start.2 = (bf16[256,128,1,10]{1,0,3,2:T(8,128)(2,1)S(1)}, bf16[256,128,1,10]{1,0,3,2:T(8,128)(2,1)}, u32[]{:S(2)}) copy-start(bf16[256,128,1,10]{1,0,3,2:T(8,128)(2,1)} %param.19) | copy-start | bytes 1966084
  137.8 10.1 %all-to-all-start.4 = ((bf16[4,64,512]{2,1,0:T(8,128)(2,1)}), bf16[4,64,512]{2,1,0:T(8,128)(2,1)S(1)}, u32[]{:S(2)}, u32[]{:S(2)}) async-start(bf16[4,64,512]{2,1,0:T(8,128)(2,1)} %broadcast_in_dim.50), calls=%async_computation.4 | async-start | bytes 524288 | tf_op jit(solution)/shard_map/all_to_all | solution.py:274
  155.5 22.4 %copy-start.9 = (s32[4]{0:T(128)S(1)}, s32[4]{0:T(128)}, u32[]{:S(2)}) copy-start(s32[4]{0:T(128)} %lengths_ref.1) | copy-start | bytes 52
  155.5 28.2 %copy-start.4 = (bf16[2,4,256]{2,1,0:T(4,128)(2,1)S(1)}, bf16[2,4,256]{2,1,0:T(4,128)(2,1)}, u32[]{:S(2)}) copy-start(bf16[2,4,256]{2,1,0:T(4,128)(2,1)} %param.13) | copy-start | bytes 12292
  170.1 22.6 %all-to-all-start.7 = ((bf16[1,16,1,40,128]{4,3,2,0,1:T(8,128)(2,1)}), bf16[1,16,1,40,128]{4,3,2,0,1:T(8,128)(2,1)S(1)}, u32[]{:S(2)}, u32[]{:S(2)}) async-start(bf16[1,16,1,40,128]{4,3,2,0,1:T(8,128)(2,1)} %bitcast.28), calls=%async_computation.7 | async-start | bytes 327680 | tf_op jit(solution)/shard_map/all_to_all | solution.py:30

commit v7 on v6

--- a/solution.py
+++ b/solution.py
@@ -55,7 +55,9 @@
 CHUNK_ROWS = 256
 
 
-def attention_kernel(lengths_ref, query_ref, fresh_ref, cache_hbm, out_ref, keys, values, sems):
+def attention_kernel(
+    lengths_ref, query_ref, fresh_ref, cache_hbm, fresh_rows, out_ref, store_hbm, keys, values, sems, write_sems
+):
     rows = keys.shape[0]
     chunks = rows // CHUNK_ROWS
     copies = []
@@ -82,6 +84,22 @@
     pick = (lax.broadcasted_iota(jnp.int32, (row_count, slot_count), 1) == row_slot)
     for copy in copies:
         copy.wait()
+    tile = 16
+    within = lax.broadcasted_iota(jnp.int32, (tile, keys.shape[1]), 0)
+    start = jnp.int32(0)
+    for slot in range(slot_count):
+        row = start + lengths_ref[slot]
+        base = pl.multiple_of((row // tile) * tile, tile)
+        for which, target in ((0, keys), (1, values)):
+            block = target[pl.ds(base, tile), :]
+            fresh_row = jnp.broadcast_to(fresh_rows[which, pl.ds(slot, 1), :], block.shape)
+            target[pl.ds(base, tile), :] = jnp.where(within == row - base, fresh_row, block)
+        start = row + 1
+    writes = []
+    for which, source in ((0, keys), (1, values)):
+        write = pltpu.make_async_copy(source, store_hbm.at[which], write_sems.at[which])
+        write.start()
+        writes.append(write)
     score_scale = head_dim ** (-0.5)
     for head in range(kv_heads):
         lanes = pl.ds(head * head_dim, head_dim)
@@ -102,6 +120,8 @@
         fresh_values = jnp.dot(pick.astype(jnp.bfloat16), fresh_ref[1, head], preferred_element_type=jnp.float32)
         mixed = mixed + new_weight.astype(jnp.bfloat16).astype(jnp.float32) * fresh_values
         out_ref[head] = (mixed / denominator).astype(out_ref.dtype)
+    for write in writes:
+        write.wait()
 
 
 def attend_kernel(lengths, query, key_value_fresh, kv_cache):
@@ -116,28 +136,33 @@
     fresh = jnp.transpose(
         key_value_fresh.reshape(2, slot_count, kv_heads, HEAD_SIZE), (0, 2, 1, 3)
     )
-    out = pl.pallas_call(
+    out, store = pl.pallas_call(
         attention_kernel,
-        out_shape=jax.ShapeDtypeStruct(query_rows.shape, jnp.bfloat16),
+        out_shape=(
+            jax.ShapeDtypeStruct(query_rows.shape, jnp.bfloat16),
+            jax.ShapeDtypeStruct(kv_cache.shape, kv_cache.dtype),
+        ),
         in_specs=[
             pl.BlockSpec(memory_space=pltpu.SMEM),
             pl.BlockSpec(memory_space=pltpu.VMEM),
             pl.BlockSpec(memory_space=pltpu.VMEM),
             pl.BlockSpec(memory_space=pl.ANY),
+            pl.BlockSpec(memory_space=pltpu.VMEM),
         ],
-        out_specs=pl.BlockSpec(memory_space=pltpu.VMEM),
+        out_specs=(pl.BlockSpec(memory_space=pltpu.VMEM), pl.BlockSpec(memory_space=pl.ANY)),
         scratch_shapes=[
             pltpu.VMEM((rows, kv_width), kv_cache.dtype),
             pltpu.VMEM((rows, kv_width), kv_cache.dtype),
             pltpu.SemaphoreType.DMA((2, rows // CHUNK_ROWS)),
+            pltpu.SemaphoreType.DMA((2,)),
         ],
         cost_estimate=pl.CostEstimate(
             flops=4 * kv_heads * slot_count * group_width * rows * HEAD_SIZE,
             transcendentals=kv_heads * slot_count * group_width * rows,
             bytes_accessed=2 * rows * kv_width * 2,
         ),
-    )(lengths, query_rows, fresh, kv_cache)
-    return jnp.transpose(
+    )(lengths, query_rows, fresh, kv_cache, key_value_fresh)
+    return store, jnp.transpose(
         out.reshape(kv_heads, slot_count, group_width, HEAD_SIZE), (1, 0, 2, 3)
     ).reshape(slot_count, kv_heads * group_width * HEAD_SIZE)
 
@@ -206,16 +231,7 @@
 ):
     slot_count = lengths.shape[0]
     first_rows, end_rows = slot_bounds(lengths)
-    key_value_store = kv_cache
-    for slot_index in range(slot_count):
-        key_value_store = lax.dynamic_update_slice(
-            key_value_store,
-            key_value_fresh[:, slot_index : slot_index + 1, :],
-            (jnp.int32(0), end_rows[slot_index] - 1, jnp.int32(0)),
-        )
-    kv_heads = key_value_store.shape[2] // HEAD_SIZE
-    group_width = QUERY_HEADS // KEY_VALUE_HEADS
-    attended = attend_kernel(lengths, query, key_value_fresh, kv_cache)
+    key_value_store, attended = attend_kernel(lengths, query, key_value_fresh, kv_cache)
     y_count, mdl_count = lax.axis_size("y"), lax.axis_size("mdl")
     weight_copies = jnp.broadcast_to(out_weight.T[None], (y_count,) + out_weight.T.shape)
     row_weight = lax.all_to_all(weight_copies, "y", 0, 0, tiled=True).reshape(-1, out_weight.shape[0])

time: 196 us -> 195 us (level)
  blocking collectives: 98 us -> 120 us
  starting transfers between devices: 29.1 us -> 21.3 us
  local copies, waits for them, and re-layouts: 27.3 us -> 20.7 us
  between operations: 5.97 us -> 0.96 us
  waiting for transfers between devices: 22.1 us -> 18.3 us
    all_to_all x2 -> x3, blocking collectives: 18.7 us -> 41.1 us  [scatter_sum(): lax.all_to_all(parts.astype(jnp.bfloat16), name, position, position, tile...]
    all_to_all x1 -> x0, starting transfers between devices: 7.72 us -> none  [scatter_sum(): lax.all_to_all(parts.astype(jnp.bfloat16), name, position, position, tile...]
    dynamic_update_slice x4 -> x0, local copies, waits for them, and re-layouts: 5.24 us -> none  [body(): lax.dynamic_update_slice(key_value_store, key_value_fresh[:, slot_index:s...]
    all_to_all x1 -> x0, waiting for transfers between devices: 3.82 us -> none  [scatter_sum(): lax.all_to_all(parts.astype(jnp.bfloat16), name, position, position, tile...]
    unnamed x24 -> x15, local copies, waits for them, and re-layouts: 6.79 us -> 4.46 us
  transfers between devices with their start and end apart: 5 -> 4, of which waited for: 4 -> 3; matrix products, arithmetic and copies ran while one was open for 7% -> 5% of each run, Pallas kernels for 2% -> 2%
where the time goes in v7:
time: 195 us; the launch traced here: 192 us
  blocking collectives  120 us (62%)
  starting transfers between devices  21.3 us (11%)
  local copies, waits for them, and re-layouts  20.7 us (11%)
  waiting for transfers between devices  18.3 us (9%)
  other arithmetic  3.91 us (2%)
  Pallas kernels  3.75 us (2%)
  matrix products  3 us (2%)
    all_to_all x3, blocking collectives, scatter_sum(): lax.all_to_all(parts.astype(jnp.bfloat16), name, position, position, tile...  41.1 us
    all_gather x1, blocking collectives, body(): flat = lax.all_gather(flat, 'z', axis=0, tiled=True)  36.8 us
    all_gather x1, blocking collectives, gather_rows(): flat = lax.all_gather(flat, 'z', axis=0, tiled=True)  27.8 us
    all_to_all x1, blocking collectives, body(): lax.all_to_all(payload, 'mdl', 0, 0, tiled=True).astype(jnp.float32).sum(0)  11.1 us
    all_to_all x1, waiting for transfers between devices, gather_rows(): lax.all_to_all(copies, 'y', 0, 0, tiled=True).reshape((count,) + part.shape)  9.45 us
    all_to_all x1, starting transfers between devices, body(): arrived = lax.all_to_all(outgoing, ('y', 'mdl'), 0, 0, tiled=True)  7.75 us
    all_to_all x1, waiting for transfers between devices, body(): arrived = lax.all_to_all(outgoing, ('y', 'mdl'), 0, 0, tiled=True)  5.55 us
    all_to_all x1, starting transfers between devices, body(): lax.all_to_all(hidden_copies, 'mdl', 0, 0, tiled=True)  5.45 us
  transfers between devices with their start and end apart: 4, of which 3 were waited for; matrix products, arithmetic and copies ran while one was open for 5% of the time, Pallas kernels for 2%

profile of v7, /device:TPU:6, one launch (start us, length us, event | category | flops | bytes accessed | tf_op | source)
XLA Modules:
  0.0 192.3 jit_solution(8763553800815342289)
XLA Ops:
  0.6 0.0 copy-start.5
  0.6 1.6 broadcast_in_dim.24
  2.3 4.5 %all-to-all-start = ((bf16[4,40,1024]{2,1,0:T(8,128)(2,1)}), bf16[4,40,1024]{2,1,0:T(8,128)(2,1)S(1)}, u32[]{:S(2)}, u32[]{:S(2)}) async-start(bf16[4,40,1024]{2,1,0:T(8,128)(2,1)} %broadcast_in_dim.24), calls=%async_computation | async-start | bytes 655360 | tf_op jit(solution)/shard_map/all_to_all | solution.py:237
  6.7 0.7 reshape.121
  7.4 0.6 copy.27
  8.1 0.0 copy-start.4
  8.1 3.7 %shard_map.113 = (bf16[2,16,128]{2,1,0:T(8,128)(2,1)}, bf16[2,1024,256]{2,1,0:T(8,128)(2,1)}) custom-call(s32[4]{0:T(128)} %lengths_ref.1, bf16[2,16,128]{2,1,0:T(8,128)(2,1)} %bitcast.68, bf16[2,2,4,128]{3,2,1,0:T(4,128)(2,1)} %bitcast.72, bf16[2,1024,256]{2,1,0:T(8,128)(2,1)} %cache_hbm.1, bf16[2,4,256]{2,1,0:T(4,128)(2,1)} %fresh_rows.1), custom_call_target="tpu_custom_call" | custom-call | flops 16777216 | bytes 1048576 | tf_op jit(solution)/shard_map/pallas_call | solution.py:139
  11.8 0.7 copy.28
  12.5 1.8 all_gather.12
  14.3 0.0 copy-done.5
  14.3 2.4 %scatter_custom_fusion = s32[512]{0:T(512)S(1)} fusion(s32[512]{0:T(512)S(1)} %compare_select_fusion.1, s32[512]{0:T(512)S(1)} %iota.3, s32[]{:T(128)} %constant.19.clone.1), kind=kCustom, calls=%fused_computation.33 | custom fusion | bytes 2052 | tf_op jit(solution)/shard_map/scatter | solution.py:255
  16.8 36.8 %all_gather.13 = bf16[1024,128]{1,0:T(8,128)(2,1)S(1)} all-gather(bf16[64,128]{1,0:T(8,128)(2,1)S(1)} %all_gather.12), channel_id=1, replica_groups=mesh['y'=4,'z'=16,'c'=2,'mdl'=4] {'z'}, dimensions={0}, use_global_device_ids=true | all-gather | bytes 278528 | tf_op jit(solution)/shard_map/all_gather | solution.py:240
  53.6 0.1 reshape.125
  53.7 0.0 all-to-all-done
  53.7 0.2 fusion.10
  54.0 0.6 reshape.127
  54.6 7.8 %all-to-all-start.1 = ((bf16[16,10,128]{2,1,0:T(8,128)(2,1)}), bf16[16,10,128]{2,1,0:T(8,128)(2,1)S(1)}, u32[]{:S(2)}, u32[]{:S(2)}) async-start(bf16[16,10,128]{2,1,0:T(8,128)(2,1)} %reshape.127), calls=%async_computation.1 | async-start | bytes 131072 | tf_op jit(solution)/shard_map/all_to_all | solution.py:248
  62.4 0.0 copy-done.4
  62.4 0.1 copy.30
  62.5 5.5 %all-to-all-done.1 = bf16[16,10,128]{2,1,0:T(8,128)(2,1)S(1)} async-done(((bf16[16,10,128]{2,1,0:T(8,128)(2,1)}), bf16[16,10,128]{2,1,0:T(8,128)(2,1)S(1)}, u32[]{:S(2)}, u32[]{:S(2)}) %all-to-all-start.1) | async-done | bytes 40992 | tf_op jit(solution)/shard_map/all_to_all | solution.py:248
  68.1 0.1 copy.29
  68.2 1.0 gather_fusion
  69.3 0.1 add_convert_fusion
  69.4 0.1 copy.31
  69.6 1.8 all_gather.14
  71.4 27.8 %all_gather.15 = bf16[1280,128]{1,0:T(8,128)(2,1)S(1)} all-gather(bf16[80,128]{1,0:T(8,128)(2,1)S(1)} %all_gather.14), channel_id=1, replica_groups=mesh['y'=4,'z'=16,'c'=2,'mdl'=4] {'z'}, dimensions={0}, use_global_device_ids=true | all-gather | bytes 348160 | tf_op jit(solution)/shard_map/all_gather | solution.py:22
  99.2 1.2 broadcast_in_dim.48
  100.4 0.0 copy-start.3
  100.4 0.0 copy-start
  100.5 3.7 %all-to-all-start.2 = ((bf16[4,1280,128]{2,1,0:T(8,128)(2,1)}), bf16[4,1280,128]{2,1,0:T(8,128)(2,1)S(1)}, u32[]{:S(2)}, u32[]{:S(2)}) async-start(bf16[4,1280,128]{2,1,0:T(8,128)(2,1)} %broadcast_in_dim.48), calls=%async_computation.2 | async-start | bytes 2621440 | tf_op jit(solution)/shard_map/all_to_all | solution.py:24
  104.1 0.0 copy-done.3
  104.1 0.3 reshape.132
  104.5 0.0 copy-done
  104.5 2.4 %copy.32 = bf16[2,128,1,10,256]{4,0,3,1,2:T(2,128)(2,1)} copy(bf16[2,128,1,10,256]{4,1,3,2,0:T(8,128)(2,1)S(1)} %copy-done) | data formatting | bytes 2621440 | tf_op args[8]
  106.9 0.1 constant_dynamic-slice_fusion
  106.9 9.5 %all-to-all-done.2 = bf16[4,1280,128]{2,1,0:T(8,128)(2,1)S(1)} async-done(((bf16[4,1280,128]{2,1,0:T(8,128)(2,1)}), bf16[4,1280,128]{2,1,0:T(8,128)(2,1)S(1)}, u32[]{:S(2)}, u32[]{:S(2)}) %all-to-all-start.2) | async-done | bytes 1310752 | tf_op jit(solution)/shard_map/all_to_all | solution.py:24
  116.4 2.2 %reshape.140 = f32[128,10,512]{2,1,0:T(8,128)} reshape(bf16[4,1280,128]{2,1,0:T(8,128)(2,1)S(1)} %all-to-all-done.2) | data formatting | bytes 3932160 | tf_op jit(solution)/shard_map/convert_element_type | solution.py:264
  118.6 2.8 %fusion.1 = (bf16[512,128,10]{0,2,1:T(8,128)(2,1)S(1)}, f32[512]{0:T(512)S(1)}) fusion(f32[128,10,512]{2,1,0:T(8,128)} %reshape.140, f32[128,10]{1,0:T(8,128)S(1)} %bitcast.65), kind=kLoop, calls=%fused_computation.6 | loop fusion | flops 2620928 | bytes 3939328 | tf_op jit(solution)/shard_map/convert_element_type | solution.py:270
  121.4 0.0 copy-start.1
  121.4 1.3 convert_element_type.130
  122.8 0.3 copy-done.1
  123.1 2.2 %fusion.5 = bf16[512,2,256]{0,2,1:T(8,128)(2,1)S(1)} fusion(bf16[2,1280,256]{2,0,1:T(2,128)(2,1)S(1)} %bitcast.59, bf16[512,1280]{0,1:T(8,128)(2,1)} %convert_element_type.130), kind=kOutput, calls=%fused_computation.10 | convolution fusion | flops 671350784 | bytes 3145728 | tf_op jit(solution)/shard_map/rk,gkf->gfr/dot_general | solution.py:272
  125.4 0.0 copy-start.2
  125.4 11.1 %all_to_all.40 = bf16[4,130,512]{2,1,0:T(8,128)(2,1)S(1)} all-to-all(bf16[4,130,512]{2,1,0:T(8,128)(2,1)S(1)} %pad_maximum_fusion), channel_id=1, replica_groups=mesh['y'=4,'z'=16,'c'=2,'mdl'=4] {'mdl'}, dimensions={0} | all-to-all | bytes 1064960 | tf_op jit(solution)/shard_map/all_to_all | solution.py:283
  136.5 0.1 convert_reduce_fusion
  136.6 0.1 fusion.13
  136.6 0.7 broadcast_in_dim.50
  137.4 5.4 %all-to-all-start.4 = ((bf16[4,64,512]{2,1,0:T(8,128)(2,1)}), bf16[4,64,512]{2,1,0:T(8,128)(2,1)S(1)}, u32[]{:S(2)}, u32[]{:S(2)}) async-start(bf16[4,64,512]{2,1,0:T(8,128)(2,1)} %broadcast_in_dim.50), calls=%async_computation.4 | async-start | bytes 524288 | tf_op jit(solution)/shard_map/all_to_all | solution.py:290
  142.8 0.0 copy-done.2
  142.8 1.0 copy.36
  143.9 0.2 reshape.137
  144.1 3.3 %all-to-all-done.4 = bf16[4,64,512]{2,1,0:T(8,128)(2,1)S(1)} async-done(((bf16[4,64,512]{2,1,0:T(8,128)(2,1)}), bf16[4,64,512]{2,1,0:T(8,128)(2,1)S(1)}, u32[]{:S(2)}, u32[]{:S(2)}) %all-to-all-start.4) | async-done | bytes 262176 | tf_op jit(solution)/shard_map/all_to_all | solution.py:290
  147.4 0.6 fusion
  148.0 0.7 copy.37
  148.6 0.8 convert_element_type.140
  149.5 0.1 copy.38
  149.6 4.8 %all_to_all.41 = bf16[4,16,2,40,128]{4,3,1,0,2:T(8,128)(2,1)S(1)} all-to-all(bf16[4,16,2,40,128]{4,3,1,0,2:T(8,128)(2,1)S(1)} %copy.38), channel_id=1, replica_groups=mesh['y'=4,'z'=16,'c'=2,'mdl'=4] {'c'}, dimensions={2} | all-to-all | bytes 2621440 | tf_op jit(solution)/shard_map/all_to_all | solution.py:30
  154.4 0.6 reduce_sum.66
  155.0 13.9 %all_to_all.42 = bf16[4,16,1,40,128]{4,3,1,2,0:T(8,128)(2,1)S(1)} all-to-all(bf16[4,16,1,40,128]{4,3,1,2,0:T(8,128)(2,1)S(1)} %bitcast.57), channel_id=1, replica_groups=mesh['y'=4,'z'=16,'c'=2,'mdl'=4] {'y'}, dimensions={0} | all-to-all | bytes 1310720 | tf_op jit(solution)/shard_map/all_to_all | solution.py:30
  168.9 0.1 reduce_sum.67
  169.0 22.4 %all_to_all.43 = bf16[1,16,1,40,128]{4,3,2,0,1:T(8,128)(2,1)S(1)} all-to-all(bf16[1,16,1,40,128]{4,3,2,0,1:T(8,128)(2,1)S(1)} %bitcast.63), channel_id=1, replica_groups=mesh['y'=4,'z'=16,'c'=2,'mdl'=4] {'z'}, dimensions={1} | all-to-all | bytes 327680 | tf_op jit(solution)/shard_map/all_to_all | solution.py:30
  191.4 0.1 copy.39
  191.6 0.7 copy.40
  (17 shorter events, 0.3 us)
Async XLA Ops:
  0.6 13.7 %copy-start.5 = (s32[512]{0:T(512)S(1)}, s32[512]{0:T(512)}, u32[]{:S(2)}) copy-start(s32[512]{0:T(512)} %param.11) | copy-start | bytes 6148
  2.3 51.4 %all-to-all-start = ((bf16[4,40,1024]{2,1,0:T(8,128)(2,1)}), bf16[4,40,1024]{2,1,0:T(8,128)(2,1)S(1)}, u32[]{:S(2)}, u32[]{:S(2)}) async-start(bf16[4,40,1024]{2,1,0:T(8,128)(2,1)} %broadcast_in_dim.24), calls=%async_computation | async-start | bytes 655360 | tf_op jit(solution)/shard_map/all_to_all | solution.py:237
  8.1 54.3 %copy-start.4 = (bf16[512,10]{0,1:T(8,128)(2,1)S(1)}, bf16[512,10]{0,1:T(8,128)(2,1)}, u32[]{:S(2)}) copy-start(bf16[512,10]{0,1:T(8,128)(2,1)} %param.15) | copy-start | bytes 30724
  54.6 13.5 %all-to-all-start.1 = ((bf16[16,10,128]{2,1,0:T(8,128)(2,1)}), bf16[16,10,128]{2,1,0:T(8,128)(2,1)S(1)}, u32[]{:S(2)}, u32[]{:S(2)}) async-start(bf16[16,10,128]{2,1,0:T(8,128)(2,1)} %reshape.127), calls=%async_computation.1 | async-start | bytes 131072 | tf_op jit(solution)/shard_map/all_to_all | solution.py:248
  100.4 3.7 %copy-start.3 = (f32[5120]{0:T(1024)S(1)}, f32[5120]{0:T(1024)}, u32[]{:S(2)}) copy-start(f32[5120]{0:T(1024)} %param.17) | copy-start | bytes 61444
  100.4 4.0 %copy-start = (bf16[2,128,1,10,256]{4,1,3,2,0:T(8,128)(2,1)S(1)}, bf16[2,128,1,10,256]{4,1,3,2,0:T(8,128)(2,1)}, u32[]{:S(2)}) copy-start(bf16[2,128,1,10,256]{4,1,3,2,0:T(8,128)(2,1)} %param.18) | copy-start | bytes 3932164
  100.5 15.9 %all-to-all-start.2 = ((bf16[4,1280,128]{2,1,0:T(8,128)(2,1)}), bf16[4,1280,128]{2,1,0:T(8,128)(2,1)S(1)}, u32[]{:S(2)}, u32[]{:S(2)}) async-start(bf16[4,1280,128]{2,1,0:T(8,128)(2,1)} %broadcast_in_dim.48), calls=%async_computation.2 | async-start | bytes 2621440 | tf_op jit(solution)/shard_map/all_to_all | solution.py:24
  121.4 1.6 copy-start.1
  125.4 17.4 %copy-start.2 = (bf16[256,128,1,10]{1,0,3,2:T(8,128)(2,1)S(1)}, bf16[256,128,1,10]{1,0,3,2:T(8,128)(2,1)}, u32[]{:S(2)}) copy-start(bf16[256,128,1,10]{1,0,3,2:T(8,128)(2,1)} %param.19) | copy-start | bytes 1966084
  137.4 10.1 %all-to-all-start.4 = ((bf16[4,64,512]{2,1,0:T(8,128)(2,1)}), bf16[4,64,512]{2,1,0:T(8,128)(2,1)S(1)}, u32[]{:S(2)}, u32[]{:S(2)}) async-start(bf16[4,64,512]{2,1,0:T(8,128)(2,1)} %broadcast_in_dim.50), calls=%async_computation.4 | async-start | bytes 524288 | tf_op jit(solution)/shard_map/all_to_all | solution.py:290

commit v8 on v7

--- a/solution.py
+++ b/solution.py
@@ -249,12 +249,16 @@
     head_sum = arrived.astype(jnp.float32).reshape(y_count, mdl_count, sub_width, row_slots).sum(1)
     head_share = jnp.transpose(head_sum, (1, 0, 2)).reshape(sub_width, y_count * row_slots).T
     total_rows = assignment.shape[0]
-    inverse = (
-        jnp.zeros((total_rows,), jnp.int32)
-        .at[assignment]
-        .set(jnp.arange(total_rows, dtype=jnp.int32))
-    )
-    placed = jnp.take(head_share, inverse, axis=0)
+    selection = (
+        assignment[:, None] == lax.broadcasted_iota(jnp.int32, (total_rows, total_rows), 1)
+    ).astype(jnp.float32)
+    placed = lax.dot_general(
+        selection,
+        head_share,
+        (((0,), (0,)), ((), ())),
+        precision=lax.Precision.HIGHEST,
+        preferred_element_type=jnp.float32,
+    )
     residual_wide = hidden_in.astype(jnp.float32) + placed
     residual = residual_wide.astype(jnp.bfloat16)
     local_wide = residual.astype(jnp.float32)

time: 195 us -> 190 us (0.974)
  blocking collectives: 120 us -> 134 us
  starting transfers between devices: 21.3 us -> 13.6 us
  waiting for transfers between devices: 18.3 us -> 12.8 us
  local copies, waits for them, and re-layouts: 20.7 us -> 15.4 us
    all_to_all x0 -> x1, blocking collectives: none -> 13.2 us  [body(): arrived = lax.all_to_all(outgoing, ('y', 'mdl'), 0, 0, tiled=True)]
    all_to_all x1 -> x0, starting transfers between devices: 7.75 us -> none  [body(): arrived = lax.all_to_all(outgoing, ('y', 'mdl'), 0, 0, tiled=True)]
    all_to_all x1 -> x0, waiting for transfers between devices: 5.55 us -> none  [body(): arrived = lax.all_to_all(outgoing, ('y', 'mdl'), 0, 0, tiled=True)]
    scatter x1 -> x0, local copies, waits for them, and re-layouts: 2.44 us -> none  [body(): inverse = jnp.zeros((total_rows,), jnp.int32).at[assignment].set(jnp.aran...]
    unnamed x15 -> x16, local copies, waits for them, and re-layouts: 4.46 us -> 3.76 us
  transfers between devices with their start and end apart: 4 -> 3, of which waited for: 3 -> 2; matrix products, arithmetic and copies ran while one was open for 5% -> 3% of each run, Pallas kernels for 2% -> 2%
where the time goes in v8:
time: 190 us; the launch traced here: 188 us
  blocking collectives  134 us (71%)
  local copies, waits for them, and re-layouts  15.4 us (8%)
  starting transfers between devices  13.6 us (7%)
  waiting for transfers between devices  12.8 us (7%)
  other arithmetic  4.34 us (2%)
  Pallas kernels  3.75 us (2%)
  matrix products  3.49 us (2%)
    all_to_all x3, blocking collectives, scatter_sum(): lax.all_to_all(parts.astype(jnp.bfloat16), name, position, position, tile...  41.1 us
    all_gather x1, blocking collectives, body(): flat = lax.all_gather(flat, 'z', axis=0, tiled=True)  36.8 us
    all_gather x1, blocking collectives, gather_rows(): flat = lax.all_gather(flat, 'z', axis=0, tiled=True)  27.8 us
    all_to_all x1, blocking collectives, body(): arrived = lax.all_to_all(outgoing, ('y', 'mdl'), 0, 0, tiled=True)  13.2 us
    all_to_all x1, blocking collectives, body(): lax.all_to_all(payload, 'mdl', 0, 0, tiled=True).astype(jnp.float32).sum(0)  11.1 us
    all_to_all x1, waiting for transfers between devices, gather_rows(): lax.all_to_all(copies, 'y', 0, 0, tiled=True).reshape((count,) + part.shape)  9.45 us
    all_to_all x1, starting transfers between devices, body(): lax.all_to_all(hidden_copies, 'mdl', 0, 0, tiled=True)  5.45 us
    all_to_all x1, starting transfers between devices, body(): lax.all_to_all(weight_copies, 'y', 0, 0, tiled=True)  4.46 us
  transfers between devices with their start and end apart: 3, of which 2 were waited for; matrix products, arithmetic and copies ran while one was open for 3% of the time, Pallas kernels for 2%

profile of v8, /device:TPU:6, one launch (start us, length us, event | category | flops | bytes accessed | tf_op | source)
XLA Modules:
  0.0 187.8 jit_solution(13350594444728017111)
XLA Ops:
  0.6 1.6 broadcast_in_dim.8
  2.3 4.5 %all-to-all-start = ((bf16[4,40,1024]{2,1,0:T(8,128)(2,1)}), bf16[4,40,1024]{2,1,0:T(8,128)(2,1)S(1)}, u32[]{:S(2)}, u32[]{:S(2)}) async-start(bf16[4,40,1024]{2,1,0:T(8,128)(2,1)} %broadcast_in_dim.8), calls=%async_computation | async-start | bytes 655360 | tf_op jit(solution)/shard_map/all_to_all | solution.py:237
  6.7 0.7 reshape.117
  7.4 0.6 copy.21
  8.0 0.0 copy-start.4
  8.0 0.0 copy-start.5
  8.0 3.7 %shard_map.113 = (bf16[2,16,128]{2,1,0:T(8,128)(2,1)}, bf16[2,1024,256]{2,1,0:T(8,128)(2,1)}) custom-call(s32[4]{0:T(128)} %lengths_ref.1, bf16[2,16,128]{2,1,0:T(8,128)(2,1)} %bitcast.69, bf16[2,2,4,128]{3,2,1,0:T(4,128)(2,1)} %bitcast.74, bf16[2,1024,256]{2,1,0:T(8,128)(2,1)} %cache_hbm.1, bf16[2,4,256]{2,1,0:T(4,128)(2,1)} %fresh_rows.1), custom_call_target="tpu_custom_call" | custom-call | flops 16777216 | bytes 1048576 | tf_op jit(solution)/shard_map/pallas_call | solution.py:139
  11.8 0.7 copy.22
  12.5 1.8 all_gather.12
  14.3 36.8 %all_gather.13 = bf16[1024,128]{1,0:T(8,128)(2,1)S(1)} all-gather(bf16[64,128]{1,0:T(8,128)(2,1)S(1)} %all_gather.12), channel_id=1, replica_groups=mesh['y'=4,'z'=16,'c'=2,'mdl'=4] {'z'}, dimensions={0}, use_global_device_ids=true | all-gather | bytes 278528 | tf_op jit(solution)/shard_map/all_gather | solution.py:240
  51.1 0.1 reshape.121
  51.2 0.0 all-to-all-done
  51.2 0.2 fusion.10
  51.5 13.2 %all_to_all.40 = bf16[16,10,128]{2,1,0:T(8,128)(2,1)S(1)} all-to-all(bf16[16,10,128]{2,1,0:T(8,128)(2,1)S(1)} %reshape.123), channel_id=1, replica_groups=mesh['y'=4,'z'=16,'c'=2,'mdl'=4] {'y','mdl'}, dimensions={0} | all-to-all | bytes 81920 | tf_op jit(solution)/shard_map/all_to_all | solution.py:248
  64.8 0.0 copy-done.4
  64.8 0.0 copy-done.5
  64.8 0.5 fusion.11
  65.3 1.8 all_gather.14
  67.2 27.8 %all_gather.15 = bf16[1280,128]{1,0:T(8,128)(2,1)S(1)} all-gather(bf16[80,128]{1,0:T(8,128)(2,1)S(1)} %all_gather.14), channel_id=1, replica_groups=mesh['y'=4,'z'=16,'c'=2,'mdl'=4] {'z'}, dimensions={0}, use_global_device_ids=true | all-gather | bytes 348160 | tf_op jit(solution)/shard_map/all_gather | solution.py:22
  95.0 1.2 broadcast_in_dim.9
  96.2 0.0 copy-start.3
  96.2 0.0 copy-start
  96.2 3.7 %all-to-all-start.2 = ((bf16[4,1280,128]{2,1,0:T(8,128)(2,1)}), bf16[4,1280,128]{2,1,0:T(8,128)(2,1)S(1)}, u32[]{:S(2)}, u32[]{:S(2)}) async-start(bf16[4,1280,128]{2,1,0:T(8,128)(2,1)} %broadcast_in_dim.9), calls=%async_computation.2 | async-start | bytes 2621440 | tf_op jit(solution)/shard_map/all_to_all | solution.py:24
  99.9 0.0 copy-done.3
  99.9 0.3 reshape.128
  100.3 0.0 copy-done
  100.3 2.4 %copy.24 = bf16[2,128,1,10,256]{4,0,3,1,2:T(2,128)(2,1)} copy(bf16[2,128,1,10,256]{4,1,3,2,0:T(8,128)(2,1)S(1)} %copy-done) | data formatting | bytes 2621440 | tf_op args[8]
  102.7 0.1 constant_dynamic-slice_fusion
  102.7 9.5 %all-to-all-done.2 = bf16[4,1280,128]{2,1,0:T(8,128)(2,1)S(1)} async-done(((bf16[4,1280,128]{2,1,0:T(8,128)(2,1)}), bf16[4,1280,128]{2,1,0:T(8,128)(2,1)S(1)}, u32[]{:S(2)}, u32[]{:S(2)}) %all-to-all-start.2) | async-done | bytes 1310752 | tf_op jit(solution)/shard_map/all_to_all | solution.py:24
  112.2 2.2 %reshape.136 = f32[128,10,512]{2,1,0:T(8,128)} reshape(bf16[4,1280,128]{2,1,0:T(8,128)(2,1)S(1)} %all-to-all-done.2) | data formatting | bytes 3932160 | tf_op jit(solution)/shard_map/convert_element_type | solution.py:268
  114.4 2.8 %fusion.1 = (bf16[512,128,10]{0,2,1:T(8,128)(2,1)S(1)}, f32[512]{0:T(512)S(1)}) fusion(f32[128,10,512]{2,1,0:T(8,128)} %reshape.136, f32[128,10]{1,0:T(8,128)S(1)} %bitcast.64), kind=kLoop, calls=%fused_computation.4 | loop fusion | flops 2620928 | bytes 3939328 | tf_op jit(solution)/shard_map/convert_element_type | solution.py:274
  117.2 0.0 copy-start.1
  117.2 1.3 convert_element_type.131
  118.6 0.3 copy-done.1
  118.9 2.2 %fusion.5 = bf16[512,2,256]{0,2,1:T(8,128)(2,1)S(1)} fusion(bf16[2,1280,256]{2,0,1:T(2,128)(2,1)S(1)} %bitcast.59, bf16[512,1280]{0,1:T(8,128)(2,1)} %convert_element_type.131), kind=kOutput, calls=%fused_computation.8 | convolution fusion | flops 671350784 | bytes 3145728 | tf_op jit(solution)/shard_map/rk,gkf->gfr/dot_general | solution.py:276
  121.2 0.0 copy-start.2
  121.2 11.1 %all_to_all.41 = bf16[4,130,512]{2,1,0:T(8,128)(2,1)S(1)} all-to-all(bf16[4,130,512]{2,1,0:T(8,128)(2,1)S(1)} %pad_maximum_fusion), channel_id=1, replica_groups=mesh['y'=4,'z'=16,'c'=2,'mdl'=4] {'mdl'}, dimensions={0} | all-to-all | bytes 1064960 | tf_op jit(solution)/shard_map/all_to_all | solution.py:287
  132.3 0.1 convert_reduce_fusion
  132.4 0.1 fusion.14
  132.4 0.7 broadcast_in_dim.11
  133.2 5.4 %all-to-all-start.4 = ((bf16[4,64,512]{2,1,0:T(8,128)(2,1)}), bf16[4,64,512]{2,1,0:T(8,128)(2,1)S(1)}, u32[]{:S(2)}, u32[]{:S(2)}) async-start(bf16[4,64,512]{2,1,0:T(8,128)(2,1)} %broadcast_in_dim.11), calls=%async_computation.4 | async-start | bytes 524288 | tf_op jit(solution)/shard_map/all_to_all | solution.py:294
  138.6 0.0 copy-done.2
  138.6 1.0 copy.28
  139.6 0.2 reshape.133
  139.9 3.3 %all-to-all-done.4 = bf16[4,64,512]{2,1,0:T(8,128)(2,1)S(1)} async-done(((bf16[4,64,512]{2,1,0:T(8,128)(2,1)}), bf16[4,64,512]{2,1,0:T(8,128)(2,1)S(1)}, u32[]{:S(2)}, u32[]{:S(2)}) %all-to-all-start.4) | async-done | bytes 262176 | tf_op jit(solution)/shard_map/all_to_all | solution.py:294
  143.2 0.6 fusion
  143.8 0.7 copy.29
  144.4 0.8 convert_element_type.141
  145.3 0.1 copy.30
  145.4 4.8 %all_to_all.42 = bf16[4,16,2,40,128]{4,3,1,0,2:T(8,128)(2,1)S(1)} all-to-all(bf16[4,16,2,40,128]{4,3,1,0,2:T(8,128)(2,1)S(1)} %copy.30), channel_id=1, replica_groups=mesh['y'=4,'z'=16,'c'=2,'mdl'=4] {'c'}, dimensions={2} | all-to-all | bytes 2621440 | tf_op jit(solution)/shard_map/all_to_all | solution.py:30
  150.2 0.6 reduce_sum.66
  150.8 13.9 %all_to_all.43 = bf16[4,16,1,40,128]{4,3,1,2,0:T(8,128)(2,1)S(1)} all-to-all(bf16[4,16,1,40,128]{4,3,1,2,0:T(8,128)(2,1)S(1)} %bitcast.57), channel_id=1, replica_groups=mesh['y'=4,'z'=16,'c'=2,'mdl'=4] {'y'}, dimensions={0} | all-to-all | bytes 1310720 | tf_op jit(solution)/shard_map/all_to_all | solution.py:30
  164.7 0.1 reduce_sum.67
  164.8 22.4 %all_to_all.44 = bf16[1,16,1,40,128]{4,3,2,0,1:T(8,128)(2,1)S(1)} all-to-all(bf16[1,16,1,40,128]{4,3,2,0,1:T(8,128)(2,1)S(1)} %bitcast.62), channel_id=1, replica_groups=mesh['y'=4,'z'=16,'c'=2,'mdl'=4] {'z'}, dimensions={1} | all-to-all | bytes 327680 | tf_op jit(solution)/shard_map/all_to_all | solution.py:30
  187.2 0.6 fusion.15
  (15 shorter events, 0.2 us)
Async XLA Ops:
  2.3 48.9 %all-to-all-start = ((bf16[4,40,1024]{2,1,0:T(8,128)(2,1)}), bf16[4,40,1024]{2,1,0:T(8,128)(2,1)S(1)}, u32[]{:S(2)}, u32[]{:S(2)}) async-start(bf16[4,40,1024]{2,1,0:T(8,128)(2,1)} %broadcast_in_dim.8), calls=%async_computation | async-start | bytes 655360 | tf_op jit(solution)/shard_map/all_to_all | solution.py:237
  8.0 56.8 %copy-start.4 = (bf16[512,10]{0,1:T(8,128)(2,1)S(1)}, bf16[512,10]{0,1:T(8,128)(2,1)}, u32[]{:S(2)}) copy-start(bf16[512,10]{0,1:T(8,128)(2,1)} %param.15) | copy-start | bytes 30724
  8.0 56.8 %copy-start.5 = (s32[512]{0:T(512)S(1)}, s32[512]{0:T(512)}, u32[]{:S(2)}) copy-start(s32[512]{0:T(512)} %param.11) | copy-start | bytes 6148
  96.2 3.7 %copy-start.3 = (f32[5120]{0:T(1024)S(1)}, f32[5120]{0:T(1024)}, u32[]{:S(2)}) copy-start(f32[5120]{0:T(1024)} %param.17) | copy-start | bytes 61444
  96.2 4.0 %copy-start = (bf16[2,128,1,10,256]{4,1,3,2,0:T(8,128)(2,1)S(1)}, bf16[2,128,1,10,256]{4,1,3,2,0:T(8,128)(2,1)}, u32[]{:S(2)}) copy-start(bf16[2,128,1,10,256]{4,1,3,2,0:T(8,128)(2,1)} %param.18) | copy-start | bytes 3932164
  96.2 15.9 %all-to-all-start.2 = ((bf16[4,1280,128]{2,1,0:T(8,128)(2,1)}), bf16[4,1280,128]{2,1,0:T(8,128)(2,1)S(1)}, u32[]{:S(2)}, u32[]{:S(2)}) async-start(bf16[4,1280,128]{2,1,0:T(8,128)(2,1)} %broadcast_in_dim.9), calls=%async_computation.2 | async-start | bytes 2621440 | tf_op jit(solution)/shard_map/all_to_all | solution.py:24
  117.2 1.6 copy-start.1
  121.2 17.4 %copy-start.2 = (bf16[256,128,1,10]{1,0,3,2:T(8,128)(2,1)S(1)}, bf16[256,128,1,10]{1,0,3,2:T(8,128)(2,1)}, u32[]{:S(2)}) copy-start(bf16[256,128,1,10]{1,0,3,2:T(8,128)(2,1)} %param.19) | copy-start | bytes 1966084
  133.2 10.1 %all-to-all-start.4 = ((bf16[4,64,512]{2,1,0:T(8,128)(2,1)}), bf16[4,64,512]{2,1,0:T(8,128)(2,1)S(1)}, u32[]{:S(2)}, u32[]{:S(2)}) async-start(bf16[4,64,512]{2,1,0:T(8,128)(2,1)} %broadcast_in_dim.11), calls=%async_computation.4 | async-start | bytes 524288 | tf_op jit(solution)/shard_map/all_to_all | solution.py:294

commit v9 on v8

--- a/solution.py
+++ b/solution.py
@@ -264,16 +264,16 @@
     local_wide = residual.astype(jnp.float32)
     col_groups = gate_up_weight.shape[1]
     sub_width = hidden_in.shape[1]
-    gathered = jnp.transpose(gather_rows(residual.T), (2, 0, 1)).reshape(total_rows, col_groups * sub_width)
+    gathered = gather_rows(residual.T).reshape(col_groups * sub_width, total_rows)
     widened = gathered.astype(jnp.float32)
-    own_squares = jnp.sum(widened * widened, axis=1)
+    own_squares = jnp.sum(widened * widened, axis=0)
     gain_table = norm_gain.reshape(col_groups, lax.axis_size("mdl"), sub_width)
     gain_cols = lax.dynamic_index_in_dim(
         gain_table, lax.axis_index("mdl"), 1, keepdims=False
     ).reshape(col_groups * sub_width)
-    unscaled = (widened * gain_cols).astype(jnp.bfloat16)
+    unscaled = (widened * gain_cols[:, None]).astype(jnp.bfloat16)
     gate_up = gate_up_weight.reshape(2, col_groups * sub_width, gate_up_weight.shape[4])
-    partial_value = jnp.einsum("rk,gkf->gfr", unscaled, gate_up, preferred_element_type=jnp.float32)
+    partial_value = jnp.einsum("kr,gkf->gfr", unscaled, gate_up, preferred_element_type=jnp.float32)
     units = partial_value.shape[1]
     mdl_count = lax.axis_size("mdl")
     quarter = units // mdl_count

time: 190 us -> 193 us (1.016)
  other arithmetic: 4.34 us -> 6.42 us
    mul x0 -> x4, local copies, waits for them, and re-layouts: none -> 2.4 us  [the longest x1 1.7 us: body(): own_squares = jnp.sum(widened * widened, axis=0)]
    reduce_sum x0 -> x1, other arithmetic: none -> 2.07 us  [body(): own_squares = jnp.sum(widened * widened, axis=0)]
  transfers between devices with their start and end apart: 3 -> 3, of which waited for: 2 -> 2; matrix products, arithmetic and copies ran while one was open for 3% -> 4% of each run, Pallas kernels for 2% -> 2%
where the time goes in v9:
time: 193 us; the launch traced here: 190 us
  blocking collectives  134 us (69%)
  local copies, waits for them, and re-layouts  15.8 us (8%)
  starting transfers between devices  14.3 us (7%)
  waiting for transfers between devices  11.9 us (6%)
  other arithmetic  6.42 us (3%)
  Pallas kernels  3.75 us (2%)
  matrix products  3.49 us (2%)
    all_to_all x3, blocking collectives, scatter_sum(): lax.all_to_all(parts.astype(jnp.bfloat16), name, position, position, tile...  41.1 us
    all_gather x1, blocking collectives, body(): flat = lax.all_gather(flat, 'z', axis=0, tiled=True)  36.8 us
    all_gather x1, blocking collectives, gather_rows(): flat = lax.all_gather(flat, 'z', axis=0, tiled=True)  27.8 us
    all_to_all x1, blocking collectives, body(): arrived = lax.all_to_all(outgoing, ('y', 'mdl'), 0, 0, tiled=True)  13.2 us
    all_to_all x1, blocking collectives, body(): lax.all_to_all(payload, 'mdl', 0, 0, tiled=True).astype(jnp.float32).sum(0)  11.1 us
    all_to_all x1, waiting for transfers between devices, gather_rows(): lax.all_to_all(copies, 'y', 0, 0, tiled=True).reshape((count,) + part.shape)  8.6 us
    all_to_all x1, starting transfers between devices, body(): lax.all_to_all(hidden_copies, 'mdl', 0, 0, tiled=True)  5.45 us
    all_to_all x1, starting transfers between devices, body(): lax.all_to_all(weight_copies, 'y', 0, 0, tiled=True)  4.46 us
  transfers between devices with their start and end apart: 3, of which 2 were waited for; matrix products, arithmetic and copies ran while one was open for 4% of the time, Pallas kernels for 2%

profile of v9, /device:TPU:6, one launch (start us, length us, event | category | flops | bytes accessed | tf_op | source)
XLA Modules:
  0.0 190.3 jit_solution(10022919908265100801)
XLA Ops:
  0.6 1.6 broadcast_in_dim.8
  2.3 4.5 %all-to-all-start = ((bf16[4,40,1024]{2,1,0:T(8,128)(2,1)}), bf16[4,40,1024]{2,1,0:T(8,128)(2,1)S(1)}, u32[]{:S(2)}, u32[]{:S(2)}) async-start(bf16[4,40,1024]{2,1,0:T(8,128)(2,1)} %broadcast_in_dim.8), calls=%async_computation | async-start | bytes 655360 | tf_op jit(solution)/shard_map/all_to_all | solution.py:237
  6.7 0.7 reshape.113
  7.4 0.6 copy.20
  8.0 0.0 copy-start.5
  8.0 0.0 copy-start.6
  8.0 3.7 %shard_map.113 = (bf16[2,16,128]{2,1,0:T(8,128)(2,1)}, bf16[2,1024,256]{2,1,0:T(8,128)(2,1)}) custom-call(s32[4]{0:T(128)} %lengths_ref.1, bf16[2,16,128]{2,1,0:T(8,128)(2,1)} %bitcast.59, bf16[2,2,4,128]{3,2,1,0:T(4,128)(2,1)} %bitcast.64, bf16[2,1024,256]{2,1,0:T(8,128)(2,1)} %cache_hbm.1, bf16[2,4,256]{2,1,0:T(4,128)(2,1)} %fresh_rows.1), custom_call_target="tpu_custom_call" | custom-call | flops 16777216 | bytes 1048576 | tf_op jit(solution)/shard_map/pallas_call | solution.py:139
  11.8 0.7 copy.21
  12.5 1.8 all_gather.12
  14.3 36.8 %all_gather.13 = bf16[1024,128]{1,0:T(8,128)(2,1)S(1)} all-gather(bf16[64,128]{1,0:T(8,128)(2,1)S(1)} %all_gather.12), channel_id=1, replica_groups=mesh['y'=4,'z'=16,'c'=2,'mdl'=4] {'z'}, dimensions={0}, use_global_device_ids=true | all-gather | bytes 278528 | tf_op jit(solution)/shard_map/all_gather | solution.py:240
  51.1 0.1 reshape.117
  51.2 0.0 all-to-all-done
  51.2 0.2 fusion.7
  51.5 13.2 %all_to_all.40 = bf16[16,10,128]{2,1,0:T(8,128)(2,1)S(1)} all-to-all(bf16[16,10,128]{2,1,0:T(8,128)(2,1)S(1)} %reshape.119), channel_id=1, replica_groups=mesh['y'=4,'z'=16,'c'=2,'mdl'=4] {'y','mdl'}, dimensions={0} | all-to-all | bytes 81920 | tf_op jit(solution)/shard_map/all_to_all | solution.py:248
  64.8 0.0 copy-done.5
  64.8 0.0 copy-done.6
  64.8 0.5 fusion.8
  65.3 1.8 all_gather.14
  67.2 27.8 %all_gather.15 = bf16[1280,128]{1,0:T(8,128)(2,1)S(1)} all-gather(bf16[80,128]{1,0:T(8,128)(2,1)S(1)} %all_gather.14), channel_id=1, replica_groups=mesh['y'=4,'z'=16,'c'=2,'mdl'=4] {'z'}, dimensions={0}, use_global_device_ids=true | all-gather | bytes 348160 | tf_op jit(solution)/shard_map/all_gather | solution.py:22
  95.0 1.2 broadcast_in_dim.9
  96.3 0.0 copy-start.4
  96.3 4.4 %all-to-all-start.2 = ((bf16[4,1280,128]{2,1,0:T(8,128)(2,1)}), bf16[4,1280,128]{2,1,0:T(8,128)(2,1)}, u32[]{:S(2)}, u32[]{:S(2)}) async-start(bf16[4,1280,128]{2,1,0:T(8,128)(2,1)} %broadcast_in_dim.9), calls=%async_computation.2 | async-start | bytes 2621440 | tf_op jit(solution)/shard_map/all_to_all | solution.py:24
  100.7 0.0 copy-start.1
  100.7 0.0 copy-done.4
  100.7 0.3 reshape.124
  101.0 0.2 dynamic-slice_reduce_fusion
  101.2 0.1 mul.44
  101.3 0.2 mul.45
  101.6 0.4 mul.46
  101.9 0.1 copy-done.1
  102.0 2.4 %copy.23 = bf16[2,128,1,10,256]{4,0,3,1,2:T(2,128)(2,1)} copy(bf16[2,128,1,10,256]{4,1,3,2,0:T(8,128)(2,1)S(1)} %copy-done.1) | data formatting | bytes 2621440 | tf_op args[8]
  104.4 8.6 %all-to-all-done.2 = bf16[4,1280,128]{2,1,0:T(8,128)(2,1)} async-done(((bf16[4,1280,128]{2,1,0:T(8,128)(2,1)}), bf16[4,1280,128]{2,1,0:T(8,128)(2,1)}, u32[]{:S(2)}, u32[]{:S(2)}) %all-to-all-start.2) | async-done | bytes 1310752 | tf_op jit(solution)/shard_map/all_to_all | solution.py:24
  113.0 2.8 %fusion.1 = (bf16[4,1280,128]{2,1,0:T(8,128)(2,1)}, f32[4,1280,128]{2,1,0:T(8,128)S(1)}) fusion(bf16[4,1280,128]{2,1,0:T(8,128)(2,1)} %all-to-all-done.2, f32[4,1280]{1,0:T(4,128)S(1)} %mul.46), kind=kLoop, calls=%fused_computation.4 | loop fusion | flops 2621440 | bytes 5263360 | tf_op jit(solution)/shard_map/convert_element_type | solution.py:274
  115.8 1.7 mul.50
  117.5 0.0 copy-start
  117.5 2.1 %reduce_sum.63 = f32[512]{0:T(512)S(1)} reduce(f32[1280,512]{1,0:T(8,128)} %mul.50, f32[]{:T(128)} %constant.9.clone.1), dimensions={0}, to_apply=%region_1.0 | reduce | flops 654848 | bytes 2623492 | tf_op jit(solution)/shard_map/reduce_sum | solution.py:269
  119.6 0.0 copy-done
  119.6 0.0 copy-start.2
  119.6 1.7 reshape.132
  121.3 0.0 copy-done.2
  121.3 2.2 %fusion.4 = bf16[512,2,256]{0,2,1:T(8,128)(2,1)S(1)} fusion(bf16[1280,512,1]{1,0,2:T(8,128)(2,1)} %reshape.132, bf16[2,1280,256]{2,0,1:T(2,128)(2,1)S(1)} %bitcast.50), kind=kOutput, calls=%fused_computation.7 | convolution fusion | flops 671350784 | bytes 3145728 | tf_op jit(solution)/shard_map/kr,gkf->gfr/dot_general | solution.py:276
  123.6 0.0 copy-start.3
  123.7 11.1 %all_to_all.41 = bf16[4,130,512]{2,1,0:T(8,128)(2,1)S(1)} all-to-all(bf16[4,130,512]{2,1,0:T(8,128)(2,1)S(1)} %pad_maximum_fusion), channel_id=1, replica_groups=mesh['y'=4,'z'=16,'c'=2,'mdl'=4] {'mdl'}, dimensions={0} | all-to-all | bytes 1064960 | tf_op jit(solution)/shard_map/all_to_all | solution.py:287
  134.7 0.1 convert_reduce_fusion
  134.8 0.1 fusion.11
  134.9 0.7 broadcast_in_dim.11
  135.6 5.4 %all-to-all-start.4 = ((bf16[4,64,512]{2,1,0:T(8,128)(2,1)}), bf16[4,64,512]{2,1,0:T(8,128)(2,1)S(1)}, u32[]{:S(2)}, u32[]{:S(2)}) async-start(bf16[4,64,512]{2,1,0:T(8,128)(2,1)} %broadcast_in_dim.11), calls=%async_computation.4 | async-start | bytes 524288 | tf_op jit(solution)/shard_map/all_to_all | solution.py:294
  141.1 0.0 copy-done.3
  141.1 1.0 copy.26
  142.1 0.2 reshape.129
  142.3 3.3 %all-to-all-done.4 = bf16[4,64,512]{2,1,0:T(8,128)(2,1)S(1)} async-done(((bf16[4,64,512]{2,1,0:T(8,128)(2,1)}), bf16[4,64,512]{2,1,0:T(8,128)(2,1)S(1)}, u32[]{:S(2)}, u32[]{:S(2)}) %all-to-all-start.4) | async-done | bytes 262176 | tf_op jit(solution)/shard_map/all_to_all | solution.py:294
  145.7 0.6 fusion
  146.2 0.7 copy.27
  146.9 0.8 convert_element_type.132
  147.7 0.1 copy.28
  147.8 4.8 %all_to_all.42 = bf16[4,16,2,40,128]{4,3,1,0,2:T(8,128)(2,1)S(1)} all-to-all(bf16[4,16,2,40,128]{4,3,1,0,2:T(8,128)(2,1)S(1)} %copy.28), channel_id=1, replica_groups=mesh['y'=4,'z'=16,'c'=2,'mdl'=4] {'c'}, dimensions={2} | all-to-all | bytes 2621440 | tf_op jit(solution)/shard_map/all_to_all | solution.py:30
  152.6 0.6 reduce_sum.66
  153.2 13.9 %all_to_all.43 = bf16[4,16,1,40,128]{4,3,1,2,0:T(8,128)(2,1)S(1)} all-to-all(bf16[4,16,1,40,128]{4,3,1,2,0:T(8,128)(2,1)S(1)} %bitcast.48), channel_id=1, replica_groups=mesh['y'=4,'z'=16,'c'=2,'mdl'=4] {'y'}, dimensions={0} | all-to-all | bytes 1310720 | tf_op jit(solution)/shard_map/all_to_all | solution.py:30
  167.1 0.1 reduce_sum.67
  167.2 22.4 %all_to_all.44 = bf16[1,16,1,40,128]{4,3,2,0,1:T(8,128)(2,1)S(1)} all-to-all(bf16[1,16,1,40,128]{4,3,2,0,1:T(8,128)(2,1)S(1)} %bitcast.53), channel_id=1, replica_groups=mesh['y'=4,'z'=16,'c'=2,'mdl'=4] {'z'}, dimensions={1} | all-to-all | bytes 327680 | tf_op jit(solution)/shard_map/all_to_all | solution.py:30
  189.7 0.6 fusion.12
  (15 shorter events, 0.2 us)
Async XLA Ops:
  2.3 48.9 %all-to-all-start = ((bf16[4,40,1024]{2,1,0:T(8,128)(2,1)}), bf16[4,40,1024]{2,1,0:T(8,128)(2,1)S(1)}, u32[]{:S(2)}, u32[]{:S(2)}) async-start(bf16[4,40,1024]{2,1,0:T(8,128)(2,1)} %broadcast_in_dim.8), calls=%async_computation | async-start | bytes 655360 | tf_op jit(solution)/shard_map/all_to_all | solution.py:237
  8.0 56.8 %copy-start.5 = (bf16[512,10]{0,1:T(8,128)(2,1)S(1)}, bf16[512,10]{0,1:T(8,128)(2,1)}, u32[]{:S(2)}) copy-start(bf16[512,10]{0,1:T(8,128)(2,1)} %param.15) | copy-start | bytes 30724
  8.0 56.8 %copy-start.6 = (s32[512]{0:T(512)S(1)}, s32[512]{0:T(512)}, u32[]{:S(2)}) copy-start(s32[512]{0:T(512)} %param.11) | copy-start | bytes 6148
  96.3 4.4 %copy-start.4 = (f32[5120]{0:T(1024)S(1)}, f32[5120]{0:T(1024)}, u32[]{:S(2)}) copy-start(f32[5120]{0:T(1024)} %param.17) | copy-start | bytes 61444
  96.3 16.8 %all-to-all-start.2 = ((bf16[4,1280,128]{2,1,0:T(8,128)(2,1)}), bf16[4,1280,128]{2,1,0:T(8,128)(2,1)}, u32[]{:S(2)}, u32[]{:S(2)}) async-start(bf16[4,1280,128]{2,1,0:T(8,128)(2,1)} %broadcast_in_dim.9), calls=%async_computation.2 | async-start | bytes 2621440 | tf_op jit(solution)/shard_map/all_to_all | solution.py:24
  100.7 1.3 copy-start.1
  117.5 2.1 %copy-start = (bf16[4,1280,128]{2,1,0:T(8,128)(2,1)S(1)}, bf16[4,1280,128]{2,1,0:T(8,128)(2,1)}, u32[]{:S(2)}) copy-start(bf16[4,1280,128]{2,1,0:T(8,128)(2,1)} %get-tuple-element.6) | copy-start | bytes 3932164
  119.6 1.7 copy-start.2
  123.6 17.4 %copy-start.3 = (bf16[256,128,1,10]{1,0,3,2:T(8,128)(2,1)S(1)}, bf16[256,128,1,10]{1,0,3,2:T(8,128)(2,1)}, u32[]{:S(2)}) copy-start(bf16[256,128,1,10]{1,0,3,2:T(8,128)(2,1)} %param.19) | copy-start | bytes 1966084
  135.6 10.1 %all-to-all-start.4 = ((bf16[4,64,512]{2,1,0:T(8,128)(2,1)}), bf16[4,64,512]{2,1,0:T(8,128)(2,1)S(1)}, u32[]{:S(2)}, u32[]{:S(2)}) async-start(bf16[4,64,512]{2,1,0:T(8,128)(2,1)} %broadcast_in_dim.11), calls=%async_computation.4 | async-start | bytes 524288 | tf_op jit(solution)/shard_map/all_to_all | solution.py:294

commit v10 on v8

--- a/solution.py
+++ b/solution.py
@@ -26,7 +26,7 @@
 
 def scatter_sum(parts):
     wide = None
-    for position, name in ((2, "c"), (0, "y"), (1, "z")):
+    for position, name in ((2, "c"), (1, "z"), (0, "y")):
         moved = lax.all_to_all(parts.astype(jnp.bfloat16), name, position, position, tiled=True)
         wide = moved.astype(jnp.float32).sum(position, keepdims=True)
         parts = wide

time: 190 us -> 206 us (1.084)
  blocking collectives: 134 us -> 150 us
    all_to_all x3, blocking collectives: 41.1 us -> 57 us  [scatter_sum(): lax.all_to_all(parts.astype(jnp.bfloat16), name, position, position, tile...]
where the time goes in v10:
time: 206 us; the launch traced here: 204 us
  blocking collectives  150 us (73%)
  local copies, waits for them, and re-layouts  15.4 us (7%)
  starting transfers between devices  13.6 us (7%)
  waiting for transfers between devices  12.8 us (6%)
  other arithmetic  4.31 us (2%)
  Pallas kernels  3.75 us (2%)
  matrix products  3.49 us (2%)
    all_to_all x3, blocking collectives, scatter_sum(): lax.all_to_all(parts.astype(jnp.bfloat16), name, position, position, tile...  57 us
    all_gather x1, blocking collectives, body(): flat = lax.all_gather(flat, 'z', axis=0, tiled=True)  36.8 us
    all_gather x1, blocking collectives, gather_rows(): flat = lax.all_gather(flat, 'z', axis=0, tiled=True)  27.8 us
    all_to_all x1, blocking collectives, body(): arrived = lax.all_to_all(outgoing, ('y', 'mdl'), 0, 0, tiled=True)  13.2 us
    all_to_all x1, blocking collectives, body(): lax.all_to_all(payload, 'mdl', 0, 0, tiled=True).astype(jnp.float32).sum(0)  11.1 us
    all_to_all x1, waiting for transfers between devices, gather_rows(): lax.all_to_all(copies, 'y', 0, 0, tiled=True).reshape((count,) + part.shape)  9.45 us
    all_to_all x1, starting transfers between devices, body(): lax.all_to_all(hidden_copies, 'mdl', 0, 0, tiled=True)  5.45 us
    all_to_all x1, starting transfers between devices, body(): lax.all_to_all(weight_copies, 'y', 0, 0, tiled=True)  4.46 us
  transfers between devices with their start and end apart: 3, of which 2 were waited for; matrix products, arithmetic and copies ran while one was open for 3% of the time, Pallas kernels for 2%

profile of v10, /device:TPU:6, one launch (start us, length us, event | category | flops | bytes accessed | tf_op | source)
XLA Modules:
  0.0 203.8 jit_solution(9707147337633744783)
XLA Ops:
  0.6 1.6 broadcast_in_dim.8
  2.3 4.5 %all-to-all-start = ((bf16[4,40,1024]{2,1,0:T(8,128)(2,1)}), bf16[4,40,1024]{2,1,0:T(8,128)(2,1)S(1)}, u32[]{:S(2)}, u32[]{:S(2)}) async-start(bf16[4,40,1024]{2,1,0:T(8,128)(2,1)} %broadcast_in_dim.8), calls=%async_computation | async-start | bytes 655360 | tf_op jit(solution)/shard_map/all_to_all | solution.py:237
  6.7 0.7 reshape.117
  7.4 0.6 copy.31
  8.0 0.0 copy-start.4
  8.0 0.0 copy-start.5
  8.0 3.7 %shard_map.113 = (bf16[2,16,128]{2,1,0:T(8,128)(2,1)}, bf16[2,1024,256]{2,1,0:T(8,128)(2,1)}) custom-call(s32[4]{0:T(128)} %lengths_ref.1, bf16[2,16,128]{2,1,0:T(8,128)(2,1)} %bitcast.69, bf16[2,2,4,128]{3,2,1,0:T(4,128)(2,1)} %bitcast.74, bf16[2,1024,256]{2,1,0:T(8,128)(2,1)} %cache_hbm.1, bf16[2,4,256]{2,1,0:T(4,128)(2,1)} %fresh_rows.1), custom_call_target="tpu_custom_call" | custom-call | flops 16777216 | bytes 1048576 | tf_op jit(solution)/shard_map/pallas_call | solution.py:139
  11.8 0.7 copy.32
  12.5 1.8 all_gather.12
  14.3 36.8 %all_gather.13 = bf16[1024,128]{1,0:T(8,128)(2,1)S(1)} all-gather(bf16[64,128]{1,0:T(8,128)(2,1)S(1)} %all_gather.12), channel_id=1, replica_groups=mesh['y'=4,'z'=16,'c'=2,'mdl'=4] {'z'}, dimensions={0}, use_global_device_ids=true | all-gather | bytes 278528 | tf_op jit(solution)/shard_map/all_gather | solution.py:240
  51.1 0.1 reshape.121
  51.2 0.0 all-to-all-done
  51.2 0.2 fusion.10
  51.5 13.2 %all_to_all.40 = bf16[16,10,128]{2,1,0:T(8,128)(2,1)S(1)} all-to-all(bf16[16,10,128]{2,1,0:T(8,128)(2,1)S(1)} %reshape.123), channel_id=1, replica_groups=mesh['y'=4,'z'=16,'c'=2,'mdl'=4] {'y','mdl'}, dimensions={0} | all-to-all | bytes 81920 | tf_op jit(solution)/shard_map/all_to_all | solution.py:248
  64.8 0.0 copy-done.4
  64.8 0.0 copy-done.5
  64.8 0.5 fusion.11
  65.3 1.8 all_gather.14
  67.2 27.8 %all_gather.15 = bf16[1280,128]{1,0:T(8,128)(2,1)S(1)} all-gather(bf16[80,128]{1,0:T(8,128)(2,1)S(1)} %all_gather.14), channel_id=1, replica_groups=mesh['y'=4,'z'=16,'c'=2,'mdl'=4] {'z'}, dimensions={0}, use_global_device_ids=true | all-gather | bytes 348160 | tf_op jit(solution)/shard_map/all_gather | solution.py:22
  95.0 1.2 broadcast_in_dim.9
  96.2 0.0 copy-start.3
  96.2 0.0 copy-start
  96.2 3.7 %all-to-all-start.2 = ((bf16[4,1280,128]{2,1,0:T(8,128)(2,1)}), bf16[4,1280,128]{2,1,0:T(8,128)(2,1)S(1)}, u32[]{:S(2)}, u32[]{:S(2)}) async-start(bf16[4,1280,128]{2,1,0:T(8,128)(2,1)} %broadcast_in_dim.9), calls=%async_computation.2 | async-start | bytes 2621440 | tf_op jit(solution)/shard_map/all_to_all | solution.py:24
  99.9 0.0 copy-done.3
  99.9 0.3 reshape.128
  100.3 0.0 copy-done
  100.3 2.4 %copy.34 = bf16[2,128,1,10,256]{4,0,3,1,2:T(2,128)(2,1)} copy(bf16[2,128,1,10,256]{4,1,3,2,0:T(8,128)(2,1)S(1)} %copy-done) | data formatting | bytes 2621440 | tf_op args[8]
  102.7 0.1 constant_dynamic-slice_fusion
  102.7 9.5 %all-to-all-done.2 = bf16[4,1280,128]{2,1,0:T(8,128)(2,1)S(1)} async-done(((bf16[4,1280,128]{2,1,0:T(8,128)(2,1)}), bf16[4,1280,128]{2,1,0:T(8,128)(2,1)S(1)}, u32[]{:S(2)}, u32[]{:S(2)}) %all-to-all-start.2) | async-done | bytes 1310752 | tf_op jit(solution)/shard_map/all_to_all | solution.py:24
  112.2 2.2 %reshape.136 = f32[128,10,512]{2,1,0:T(8,128)} reshape(bf16[4,1280,128]{2,1,0:T(8,128)(2,1)S(1)} %all-to-all-done.2) | data formatting | bytes 3932160 | tf_op jit(solution)/shard_map/convert_element_type | solution.py:268
  114.4 2.8 %fusion.1 = (bf16[512,128,10]{0,2,1:T(8,128)(2,1)S(1)}, f32[512]{0:T(512)S(1)}) fusion(f32[128,10,512]{2,1,0:T(8,128)} %reshape.136, f32[128,10]{1,0:T(8,128)S(1)} %bitcast.63), kind=kLoop, calls=%fused_computation.4 | loop fusion | flops 2620928 | bytes 3939328 | tf_op jit(solution)/shard_map/convert_element_type | solution.py:274
  117.2 0.0 copy-start.1
  117.2 1.3 convert_element_type.131
  118.6 0.3 copy-done.1
  118.9 2.2 %fusion.5 = bf16[512,2,256]{0,2,1:T(8,128)(2,1)S(1)} fusion(bf16[2,1280,256]{2,0,1:T(2,128)(2,1)S(1)} %bitcast.59, bf16[512,1280]{0,1:T(8,128)(2,1)} %convert_element_type.131), kind=kOutput, calls=%fused_computation.8 | convolution fusion | flops 671350784 | bytes 3145728 | tf_op jit(solution)/shard_map/rk,gkf->gfr/dot_general | solution.py:276
  121.2 0.0 copy-start.2
  121.2 11.1 %all_to_all.41 = bf16[4,130,512]{2,1,0:T(8,128)(2,1)S(1)} all-to-all(bf16[4,130,512]{2,1,0:T(8,128)(2,1)S(1)} %pad_maximum_fusion), channel_id=1, replica_groups=mesh['y'=4,'z'=16,'c'=2,'mdl'=4] {'mdl'}, dimensions={0} | all-to-all | bytes 1064960 | tf_op jit(solution)/shard_map/all_to_all | solution.py:287
  132.3 0.1 convert_reduce_fusion
  132.4 0.1 fusion.14
  132.4 0.7 broadcast_in_dim.11
  133.2 5.4 %all-to-all-start.4 = ((bf16[4,64,512]{2,1,0:T(8,128)(2,1)}), bf16[4,64,512]{2,1,0:T(8,128)(2,1)S(1)}, u32[]{:S(2)}, u32[]{:S(2)}) async-start(bf16[4,64,512]{2,1,0:T(8,128)(2,1)} %broadcast_in_dim.11), calls=%async_computation.4 | async-start | bytes 524288 | tf_op jit(solution)/shard_map/all_to_all | solution.py:294
  138.6 0.0 copy-done.2
  138.6 1.0 copy.38
  139.6 0.2 reshape.133
  139.9 3.3 %all-to-all-done.4 = bf16[4,64,512]{2,1,0:T(8,128)(2,1)S(1)} async-done(((bf16[4,64,512]{2,1,0:T(8,128)(2,1)}), bf16[4,64,512]{2,1,0:T(8,128)(2,1)S(1)}, u32[]{:S(2)}, u32[]{:S(2)}) %all-to-all-start.4) | async-done | bytes 262176 | tf_op jit(solution)/shard_map/all_to_all | solution.py:294
  143.2 0.6 fusion
  143.8 0.7 copy.39
  144.4 0.8 convert_element_type.141
  145.3 0.1 copy.40
  145.4 4.8 %all_to_all.42 = bf16[4,16,2,40,128]{4,3,1,0,2:T(8,128)(2,1)S(1)} all-to-all(bf16[4,16,2,40,128]{4,3,1,0,2:T(8,128)(2,1)S(1)} %copy.40), channel_id=1, replica_groups=mesh['y'=4,'z'=16,'c'=2,'mdl'=4] {'c'}, dimensions={2} | all-to-all | bytes 2621440 | tf_op jit(solution)/shard_map/all_to_all | solution.py:30
  150.2 0.6 reduce_sum.66
  150.8 0.1 copy.41
  150.9 44.4 %all_to_all.43 = bf16[4,16,1,40,128]{4,3,0,2,1:T(8,128)(2,1)S(1)} all-to-all(bf16[4,16,1,40,128]{4,3,0,2,1:T(8,128)(2,1)S(1)} %copy.41), channel_id=1, replica_groups=mesh['y'=4,'z'=16,'c'=2,'mdl'=4] {'z'}, dimensions={1} | all-to-all | bytes 1310720 | tf_op jit(solution)/shard_map/all_to_all | solution.py:30
  195.3 0.1 reduce_sum.67
  195.4 7.8 %all_to_all.44 = bf16[4,1,1,40,128]{4,3,2,1,0:T(8,128)(2,1)S(1)} all-to-all(bf16[4,1,1,40,128]{4,3,2,1,0:T(8,128)(2,1)S(1)} %bitcast.64), channel_id=1, replica_groups=mesh['y'=4,'z'=16,'c'=2,'mdl'=4] {'y'}, dimensions={0} | all-to-all | bytes 81920 | tf_op jit(solution)/shard_map/all_to_all | solution.py:30
  203.2 0.6 fusion.15
  (15 shorter events, 0.2 us)
Async XLA Ops:
  2.3 48.9 %all-to-all-start = ((bf16[4,40,1024]{2,1,0:T(8,128)(2,1)}), bf16[4,40,1024]{2,1,0:T(8,128)(2,1)S(1)}, u32[]{:S(2)}, u32[]{:S(2)}) async-start(bf16[4,40,1024]{2,1,0:T(8,128)(2,1)} %broadcast_in_dim.8), calls=%async_computation | async-start | bytes 655360 | tf_op jit(solution)/shard_map/all_to_all | solution.py:237
  8.0 56.8 %copy-start.4 = (bf16[512,10]{0,1:T(8,128)(2,1)S(1)}, bf16[512,10]{0,1:T(8,128)(2,1)}, u32[]{:S(2)}) copy-start(bf16[512,10]{0,1:T(8,128)(2,1)} %param.15) | copy-start | bytes 30724
  8.0 56.8 %copy-start.5 = (s32[512]{0:T(512)S(1)}, s32[512]{0:T(512)}, u32[]{:S(2)}) copy-start(s32[512]{0:T(512)} %param.11) | copy-start | bytes 6148
  96.2 3.7 %copy-start.3 = (f32[5120]{0:T(1024)S(1)}, f32[5120]{0:T(1024)}, u32[]{:S(2)}) copy-start(f32[5120]{0:T(1024)} %param.17) | copy-start | bytes 61444
  96.2 4.0 %copy-start = (bf16[2,128,1,10,256]{4,1,3,2,0:T(8,128)(2,1)S(1)}, bf16[2,128,1,10,256]{4,1,3,2,0:T(8,128)(2,1)}, u32[]{:S(2)}) copy-start(bf16[2,128,1,10,256]{4,1,3,2,0:T(8,128)(2,1)} %param.18) | copy-start | bytes 3932164
  96.2 15.9 %all-to-all-start.2 = ((bf16[4,1280,128]{2,1,0:T(8,128)(2,1)}), bf16[4,1280,128]{2,1,0:T(8,128)(2,1)S(1)}, u32[]{:S(2)}, u32[]{:S(2)}) async-start(bf16[4,1280,128]{2,1,0:T(8,128)(2,1)} %broadcast_in_dim.9), calls=%async_computation.2 | async-start | bytes 2621440 | tf_op jit(solution)/shard_map/all_to_all | solution.py:24
  117.2 1.6 copy-start.1
  121.2 17.4 %copy-start.2 = (bf16[256,128,1,10]{1,0,3,2:T(8,128)(2,1)S(1)}, bf16[256,128,1,10]{1,0,3,2:T(8,128)(2,1)}, u32[]{:S(2)}) copy-start(bf16[256,128,1,10]{1,0,3,2:T(8,128)(2,1)} %param.19) | copy-start | bytes 1966084
  133.2 10.1 %all-to-all-start.4 = ((bf16[4,64,512]{2,1,0:T(8,128)(2,1)}), bf16[4,64,512]{2,1,0:T(8,128)(2,1)S(1)}, u32[]{:S(2)}, u32[]{:S(2)}) async-start(bf16[4,64,512]{2,1,0:T(8,128)(2,1)} %broadcast_in_dim.11), calls=%async_computation.4 | async-start | bytes 524288 | tf_op jit(solution)/shard_map/all_to_all | solution.py:294

commit v11 on v8

--- a/solution.py
+++ b/solution.py
@@ -264,9 +264,14 @@
     local_wide = residual.astype(jnp.float32)
     col_groups = gate_up_weight.shape[1]
     sub_width = hidden_in.shape[1]
-    gathered = jnp.transpose(gather_rows(residual.T), (2, 0, 1)).reshape(total_rows, col_groups * sub_width)
+    local_squares = jnp.sum(local_wide * local_wide, axis=1)
+    local_high = local_squares.astype(jnp.bfloat16)
+    local_low = (local_squares - local_high.astype(jnp.float32)).astype(jnp.bfloat16)
+    sent = jnp.concatenate([residual.T, local_high[None], local_low[None]], axis=0)
+    arrived = gather_rows(sent)
+    own_squares = jnp.sum(arrived[:, sub_width:].astype(jnp.float32), axis=(0, 1))
+    gathered = jnp.transpose(arrived[:, :sub_width], (2, 0, 1)).reshape(total_rows, col_groups * sub_width)
     widened = gathered.astype(jnp.float32)
-    own_squares = jnp.sum(widened * widened, axis=1)
     gain_table = norm_gain.reshape(col_groups, lax.axis_size("mdl"), sub_width)
     gain_cols = lax.dynamic_index_in_dim(
         gain_table, lax.axis_index("mdl"), 1, keepdims=False

time: 190 us -> 194 us (1.021)
  waiting for transfers between devices: 12.8 us -> 16.1 us
    all_to_all x1, waiting for transfers between devices: 9.45 us -> 12.7 us  [gather_rows(): lax.all_to_all(copies, 'y', 0, 0, tiled=True).reshape((count,) + part.shape)]
    reshape x0 -> x1, local copies, waits for them, and re-layouts: none -> 2.77 us  [gather_rows(): lax.all_to_all(copies, 'y', 0, 0, tiled=True).reshape((count,) + part.shape)]
    convert_element_type x1 -> x0, local copies, waits for them, and re-layouts: 2.25 us -> none  [body(): widened = gathered.astype(jnp.float32)]
where the time goes in v11:
time: 194 us; the launch traced here: 191 us
  blocking collectives  134 us (69%)
  waiting for transfers between devices  16.1 us (8%)
  local copies, waits for them, and re-layouts  15.9 us (8%)
  starting transfers between devices  14.4 us (7%)
  other arithmetic  3.82 us (2%)
  Pallas kernels  3.75 us (2%)
  matrix products  2.2 us (1%)
    all_to_all x3, blocking collectives, scatter_sum(): lax.all_to_all(parts.astype(jnp.bfloat16), name, position, position, tile...  41.1 us
    all_gather x1, blocking collectives, body(): flat = lax.all_gather(flat, 'z', axis=0, tiled=True)  36.8 us
    all_gather x1, blocking collectives, gather_rows(): flat = lax.all_gather(flat, 'z', axis=0, tiled=True)  28.3 us
    all_to_all x1, blocking collectives, body(): arrived = lax.all_to_all(outgoing, ('y', 'mdl'), 0, 0, tiled=True)  13.2 us
    all_to_all x1, waiting for transfers between devices, gather_rows(): lax.all_to_all(copies, 'y', 0, 0, tiled=True).reshape((count,) + part.shape)  12.7 us
    all_to_all x1, blocking collectives, body(): lax.all_to_all(payload, 'mdl', 0, 0, tiled=True).astype(jnp.float32).sum(0)  11.2 us
    all_to_all x1, starting transfers between devices, body(): lax.all_to_all(hidden_copies, 'mdl', 0, 0, tiled=True)  5.45 us
    all_to_all x1, starting transfers between devices, gather_rows(): lax.all_to_all(copies, 'y', 0, 0, tiled=True).reshape((count,) + part.shape)  4.47 us
  transfers between devices with their start and end apart: 3, of which 2 were waited for; matrix products, arithmetic and copies ran while one was open for 3% of the time, Pallas kernels for 2%

profile of v11, /device:TPU:6, one launch (start us, length us, event | category | flops | bytes accessed | tf_op | source)
XLA Modules:
  0.0 191.3 jit_solution(1311226018853614863)
XLA Ops:
  0.6 1.6 broadcast_in_dim.8
  2.3 4.5 %all-to-all-start = ((bf16[4,40,1024]{2,1,0:T(8,128)(2,1)}), bf16[4,40,1024]{2,1,0:T(8,128)(2,1)S(1)}, u32[]{:S(2)}, u32[]{:S(2)}) async-start(bf16[4,40,1024]{2,1,0:T(8,128)(2,1)} %broadcast_in_dim.8), calls=%async_computation | async-start | bytes 655360 | tf_op jit(solution)/shard_map/all_to_all | solution.py:237
  6.7 0.7 reshape.137
  7.4 0.6 copy.21
  8.0 0.0 copy-start.3
  8.0 0.0 copy-start.4
  8.0 3.7 %shard_map.113 = (bf16[2,16,128]{2,1,0:T(8,128)(2,1)}, bf16[2,1024,256]{2,1,0:T(8,128)(2,1)}) custom-call(s32[4]{0:T(128)} %lengths_ref.1, bf16[2,16,128]{2,1,0:T(8,128)(2,1)} %bitcast.68, bf16[2,2,4,128]{3,2,1,0:T(4,128)(2,1)} %bitcast.73, bf16[2,1024,256]{2,1,0:T(8,128)(2,1)} %cache_hbm.1, bf16[2,4,256]{2,1,0:T(4,128)(2,1)} %fresh_rows.1), custom_call_target="tpu_custom_call" | custom-call | flops 16777216 | bytes 1048576 | tf_op jit(solution)/shard_map/pallas_call | solution.py:139
  11.8 0.7 copy.22
  12.5 1.8 all_gather.12
  14.3 36.8 %all_gather.13 = bf16[1024,128]{1,0:T(8,128)(2,1)S(1)} all-gather(bf16[64,128]{1,0:T(8,128)(2,1)S(1)} %all_gather.12), channel_id=1, replica_groups=mesh['y'=4,'z'=16,'c'=2,'mdl'=4] {'z'}, dimensions={0}, use_global_device_ids=true | all-gather | bytes 278528 | tf_op jit(solution)/shard_map/all_gather | solution.py:240
  51.1 0.1 reshape.141
  51.2 0.0 all-to-all-done
  51.2 0.2 fusion.10
  51.5 13.2 %all_to_all.40 = bf16[16,10,128]{2,1,0:T(8,128)(2,1)S(1)} all-to-all(bf16[16,10,128]{2,1,0:T(8,128)(2,1)S(1)} %reshape.143), channel_id=1, replica_groups=mesh['y'=4,'z'=16,'c'=2,'mdl'=4] {'y','mdl'}, dimensions={0} | all-to-all | bytes 81920 | tf_op jit(solution)/shard_map/all_to_all | solution.py:248
  64.8 0.0 copy-done.3
  64.8 0.0 copy-done.4
  64.8 0.5 fusion.15
  65.4 1.8 all_gather.14
  67.2 28.3 %all_gather.15 = bf16[1536,128]{1,0:T(8,128)(2,1)S(1)} all-gather(bf16[96,128]{1,0:T(8,128)(2,1)S(1)} %all_gather.14), channel_id=1, replica_groups=mesh['y'=4,'z'=16,'c'=2,'mdl'=4] {'z'}, dimensions={0}, use_global_device_ids=true | all-gather | bytes 417792 | tf_op jit(solution)/shard_map/all_gather | solution.py:22
  95.6 1.3 broadcast_in_dim.9
  96.9 0.0 copy-start.2
  96.9 0.0 copy-start
  96.9 4.5 %all-to-all-start.2 = ((bf16[4,1536,128]{2,1,0:T(8,128)(2,1)}), bf16[4,1536,128]{2,1,0:T(8,128)(2,1)}, u32[]{:S(2)}, u32[]{:S(2)}) async-start(bf16[4,1536,128]{2,1,0:T(8,128)(2,1)} %broadcast_in_dim.9), calls=%async_computation.2 | async-start | bytes 3145728 | tf_op jit(solution)/shard_map/all_to_all | solution.py:24
  101.4 0.0 copy-done.2
  101.4 0.3 reshape.149
  101.7 0.0 copy-done
  101.7 1.3 copy.24
  103.1 0.1 constant_dynamic-slice_fusion
  103.2 12.7 %all-to-all-done.2 = bf16[4,1536,128]{2,1,0:T(8,128)(2,1)} async-done(((bf16[4,1536,128]{2,1,0:T(8,128)(2,1)}), bf16[4,1536,128]{2,1,0:T(8,128)(2,1)}, u32[]{:S(2)}, u32[]{:S(2)}) %all-to-all-start.2) | async-done | bytes 1572896 | tf_op jit(solution)/shard_map/all_to_all | solution.py:24
  115.9 2.8 %reshape.148 = bf16[128,12,512]{2,1,0:T(8,128)(2,1)S(1)} reshape(bf16[4,1536,128]{2,1,0:T(8,128)(2,1)} %all-to-all-done.2) | data formatting | bytes 3145728 | tf_op jit(solution)/shard_map/reshape | solution.py:24
  118.7 0.4 convert_reduce_fusion.1
  119.1 1.8 fusion.1
  120.9 2.6 %convert_element_type.166 = bf16[512,1280]{0,1:T(8,128)(2,1)S(1)} reshape(bf16[512,128,10]{0,2,1:T(8,128)(2,1)} %fusion.1) | data formatting | bytes 2621440 | tf_op jit(solution)/shard_map/convert_element_type | solution.py:279
  123.5 0.9 fusion.5
  124.5 0.0 copy-start.1
  124.5 11.2 %all_to_all.41 = bf16[4,130,512]{2,1,0:T(8,128)(2,1)S(1)} all-to-all(bf16[4,130,512]{2,1,0:T(8,128)(2,1)S(1)} %pad_maximum_fusion), channel_id=1, replica_groups=mesh['y'=4,'z'=16,'c'=2,'mdl'=4] {'mdl'}, dimensions={0} | all-to-all | bytes 1064960 | tf_op jit(solution)/shard_map/all_to_all | solution.py:292
  135.8 0.1 convert_reduce_fusion
  135.9 0.1 fusion.14
  135.9 0.7 broadcast_in_dim.11
  136.6 5.4 %all-to-all-start.4 = ((bf16[4,64,512]{2,1,0:T(8,128)(2,1)}), bf16[4,64,512]{2,1,0:T(8,128)(2,1)S(1)}, u32[]{:S(2)}, u32[]{:S(2)}) async-start(bf16[4,64,512]{2,1,0:T(8,128)(2,1)} %broadcast_in_dim.11), calls=%async_computation.4 | async-start | bytes 524288 | tf_op jit(solution)/shard_map/all_to_all | solution.py:299
  142.1 0.0 copy-done.1
  142.1 1.0 copy.28
  143.1 0.2 reshape.154
  143.4 3.3 %all-to-all-done.4 = bf16[4,64,512]{2,1,0:T(8,128)(2,1)S(1)} async-done(((bf16[4,64,512]{2,1,0:T(8,128)(2,1)}), bf16[4,64,512]{2,1,0:T(8,128)(2,1)S(1)}, u32[]{:S(2)}, u32[]{:S(2)}) %all-to-all-start.4) | async-done | bytes 262176 | tf_op jit(solution)/shard_map/all_to_all | solution.py:299
  146.7 0.6 fusion
  147.2 0.7 copy.29
  147.9 0.8 convert_element_type.177
  148.7 0.1 copy.30
  148.9 4.8 %all_to_all.42 = bf16[4,16,2,40,128]{4,3,1,0,2:T(8,128)(2,1)S(1)} all-to-all(bf16[4,16,2,40,128]{4,3,1,0,2:T(8,128)(2,1)S(1)} %copy.30), channel_id=1, replica_groups=mesh['y'=4,'z'=16,'c'=2,'mdl'=4] {'c'}, dimensions={2} | all-to-all | bytes 2621440 | tf_op jit(solution)/shard_map/all_to_all | solution.py:30
  153.7 0.6 reduce_sum.79
  154.3 13.9 %all_to_all.43 = bf16[4,16,1,40,128]{4,3,1,2,0:T(8,128)(2,1)S(1)} all-to-all(bf16[4,16,1,40,128]{4,3,1,2,0:T(8,128)(2,1)S(1)} %bitcast.56), channel_id=1, replica_groups=mesh['y'=4,'z'=16,'c'=2,'mdl'=4] {'y'}, dimensions={0} | all-to-all | bytes 1310720 | tf_op jit(solution)/shard_map/all_to_all | solution.py:30
  168.1 0.1 reduce_sum.80
  168.2 22.4 %all_to_all.44 = bf16[1,16,1,40,128]{4,3,2,0,1:T(8,128)(2,1)S(1)} all-to-all(bf16[1,16,1,40,128]{4,3,2,0,1:T(8,128)(2,1)S(1)} %bitcast.61), channel_id=1, replica_groups=mesh['y'=4,'z'=16,'c'=2,'mdl'=4] {'z'}, dimensions={1} | all-to-all | bytes 327680 | tf_op jit(solution)/shard_map/all_to_all | solution.py:30
  190.7 0.6 fusion.16
  (18 shorter events, 0.3 us)
Async XLA Ops:
  2.3 48.9 %all-to-all-start = ((bf16[4,40,1024]{2,1,0:T(8,128)(2,1)}), bf16[4,40,1024]{2,1,0:T(8,128)(2,1)S(1)}, u32[]{:S(2)}, u32[]{:S(2)}) async-start(bf16[4,40,1024]{2,1,0:T(8,128)(2,1)} %broadcast_in_dim.8), calls=%async_computation | async-start | bytes 655360 | tf_op jit(solution)/shard_map/all_to_all | solution.py:237
  8.0 56.8 %copy-start.3 = (bf16[512,10]{0,1:T(8,128)(2,1)S(1)}, bf16[512,10]{0,1:T(8,128)(2,1)}, u32[]{:S(2)}) copy-start(bf16[512,10]{0,1:T(8,128)(2,1)} %param.15) | copy-start | bytes 30724
  8.0 56.8 %copy-start.4 = (s32[512]{0:T(512)S(1)}, s32[512]{0:T(512)}, u32[]{:S(2)}) copy-start(s32[512]{0:T(512)} %param.11) | copy-start | bytes 6148
  96.9 4.5 %copy-start.2 = (f32[5120]{0:T(1024)S(1)}, f32[5120]{0:T(1024)}, u32[]{:S(2)}) copy-start(f32[5120]{0:T(1024)} %param.17) | copy-start | bytes 61444
  96.9 4.8 %copy-start = (bf16[2,128,1,10,256]{4,1,3,2,0:T(8,128)(2,1)S(1)}, bf16[2,128,1,10,256]{4,1,3,2,0:T(8,128)(2,1)}, u32[]{:S(2)}) copy-start(bf16[2,128,1,10,256]{4,1,3,2,0:T(8,128)(2,1)} %param.18) | copy-start | bytes 3932164
  96.9 19.0 %all-to-all-start.2 = ((bf16[4,1536,128]{2,1,0:T(8,128)(2,1)}), bf16[4,1536,128]{2,1,0:T(8,128)(2,1)}, u32[]{:S(2)}, u32[]{:S(2)}) async-start(bf16[4,1536,128]{2,1,0:T(8,128)(2,1)} %broadcast_in_dim.9), calls=%async_computation.2 | async-start | bytes 3145728 | tf_op jit(solution)/shard_map/all_to_all | solution.py:24
  124.5 17.6 %copy-start.1 = (bf16[256,128,1,10]{1,0,3,2:T(8,128)(2,1)S(1)}, bf16[256,128,1,10]{1,0,3,2:T(8,128)(2,1)}, u32[]{:S(2)}) copy-start(bf16[256,128,1,10]{1,0,3,2:T(8,128)(2,1)} %param.19) | copy-start | bytes 1966084
  136.6 10.1 %all-to-all-start.4 = ((bf16[4,64,512]{2,1,0:T(8,128)(2,1)}), bf16[4,64,512]{2,1,0:T(8,128)(2,1)S(1)}, u32[]{:S(2)}, u32[]{:S(2)}) async-start(bf16[4,64,512]{2,1,0:T(8,128)(2,1)} %broadcast_in_dim.11), calls=%async_computation.4 | async-start | bytes 524288 | tf_op jit(solution)/shard_map/all_to_all | solution.py:299

commit v12 on v8

--- a/solution.py
+++ b/solution.py
@@ -101,6 +101,7 @@
         write.start()
         writes.append(write)
     score_scale = head_dim ** (-0.5)
+    results = []
     for head in range(kv_heads):
         lanes = pl.ds(head * head_dim, head_dim)
         query_rows = query_ref[head]
@@ -119,7 +120,13 @@
         mixed = jnp.dot(weights.astype(jnp.bfloat16), values[:, lanes], preferred_element_type=jnp.float32)
         fresh_values = jnp.dot(pick.astype(jnp.bfloat16), fresh_ref[1, head], preferred_element_type=jnp.float32)
         mixed = mixed + new_weight.astype(jnp.bfloat16).astype(jnp.float32) * fresh_values
-        out_ref[head] = (mixed / denominator).astype(out_ref.dtype)
+        results.append(mixed / denominator)
+    pieces = [
+        results[head][slot * group_width : (slot + 1) * group_width]
+        for slot in range(slot_count)
+        for head in range(kv_heads)
+    ]
+    out_ref[...] = jnp.concatenate(pieces, axis=0).astype(out_ref.dtype)
     for write in writes:
         write.wait()
 
@@ -139,7 +146,7 @@
     out, store = pl.pallas_call(
         attention_kernel,
         out_shape=(
-            jax.ShapeDtypeStruct(query_rows.shape, jnp.bfloat16),
+            jax.ShapeDtypeStruct((slot_count * kv_heads * group_width, HEAD_SIZE), jnp.bfloat16),
             jax.ShapeDtypeStruct(kv_cache.shape, kv_cache.dtype),
         ),
         in_specs=[
@@ -162,9 +169,7 @@
             bytes_accessed=2 * rows * kv_width * 2,
         ),
     )(lengths, query_rows, fresh, kv_cache, key_value_fresh)
-    return store, jnp.transpose(
-        out.reshape(kv_heads, slot_count, group_width, HEAD_SIZE), (1, 0, 2, 3)
-    ).reshape(slot_count, kv_heads * group_width * HEAD_SIZE)
+    return store, out.reshape(slot_count, kv_heads * group_width * HEAD_SIZE)
 
 
 def slot_bounds(lengths):

time: 190 us -> 190 us (level)
  no operation moved by 1% of the time
where the time goes in v12:
time: 190 us; the launch traced here: 187 us
  blocking collectives  134 us (71%)
  local copies, waits for them, and re-layouts  14.6 us (8%)
  starting transfers between devices  13.6 us (7%)
  waiting for transfers between devices  12.8 us (7%)
  other arithmetic  4.34 us (2%)
  Pallas kernels  3.75 us (2%)
  matrix products  3.49 us (2%)
    all_to_all x3, blocking collectives, scatter_sum(): lax.all_to_all(parts.astype(jnp.bfloat16), name, position, position, tile...  41.1 us
    all_gather x1, blocking collectives, body(): flat = lax.all_gather(flat, 'z', axis=0, tiled=True)  36.8 us
    all_gather x1, blocking collectives, gather_rows(): flat = lax.all_gather(flat, 'z', axis=0, tiled=True)  27.8 us
    all_to_all x1, blocking collectives, body(): arrived = lax.all_to_all(outgoing, ('y', 'mdl'), 0, 0, tiled=True)  13.2 us
    all_to_all x1, blocking collectives, body(): lax.all_to_all(payload, 'mdl', 0, 0, tiled=True).astype(jnp.float32).sum(0)  11.1 us
    all_to_all x1, waiting for transfers between devices, gather_rows(): lax.all_to_all(copies, 'y', 0, 0, tiled=True).reshape((count,) + part.shape)  9.45 us
    all_to_all x1, starting transfers between devices, body(): lax.all_to_all(hidden_copies, 'mdl', 0, 0, tiled=True)  5.45 us
    all_to_all x1, starting transfers between devices, body(): lax.all_to_all(weight_copies, 'y', 0, 0, tiled=True)  4.46 us
  transfers between devices with their start and end apart: 3, of which 2 were waited for; matrix products, arithmetic and copies ran while one was open for 3% of the time, Pallas kernels for 2%

profile of v12, /device:TPU:6, one launch (start us, length us, event | category | flops | bytes accessed | tf_op | source)
XLA Modules:
  0.0 187.4 jit_solution(13724065697478867096)
XLA Ops:
  0.6 1.6 broadcast_in_dim.8
  2.3 4.5 %all-to-all-start = ((bf16[4,40,1024]{2,1,0:T(8,128)(2,1)}), bf16[4,40,1024]{2,1,0:T(8,128)(2,1)S(1)}, u32[]{:S(2)}, u32[]{:S(2)}) async-start(bf16[4,40,1024]{2,1,0:T(8,128)(2,1)} %broadcast_in_dim.8), calls=%async_computation | async-start | bytes 655360 | tf_op jit(solution)/shard_map/all_to_all | solution.py:242
  6.7 0.7 reshape.114
  7.4 0.6 copy.20
  8.0 0.0 copy-start.4
  8.0 0.0 copy-start.5
  8.0 3.7 %shard_map.113 = (bf16[32,128]{1,0:T(8,128)(2,1)}, bf16[2,1024,256]{2,1,0:T(8,128)(2,1)}) custom-call(s32[4]{0:T(128)} %lengths_ref.1, bf16[2,16,128]{2,1,0:T(8,128)(2,1)} %bitcast.65, bf16[2,2,4,128]{3,2,1,0:T(4,128)(2,1)} %bitcast.69, bf16[2,1024,256]{2,1,0:T(8,128)(2,1)} %cache_hbm.1, bf16[2,4,256]{2,1,0:T(4,128)(2,1)} %fresh_rows.1), custom_call_target="tpu_custom_call" | custom-call | flops 16777216 | bytes 1048576 | tf_op jit(solution)/shard_map/pallas_call | solution.py:146
  11.8 2.0 %all_gather.12 = bf16[64,128]{1,0:T(8,128)(2,1)S(1)} all-gather(bf16[32,128]{1,0:T(8,128)(2,1)} %get-tuple-element.4), channel_id=1, replica_groups=mesh['y'=4,'z'=16,'c'=2,'mdl'=4] {'c'}, dimensions={0}, use_global_device_ids=true | all-gather | bytes 24576 | tf_op jit(solution)/shard_map/all_gather | solution.py:244
  13.8 36.8 %all_gather.13 = bf16[1024,128]{1,0:T(8,128)(2,1)S(1)} all-gather(bf16[64,128]{1,0:T(8,128)(2,1)S(1)} %all_gather.12), channel_id=1, replica_groups=mesh['y'=4,'z'=16,'c'=2,'mdl'=4] {'z'}, dimensions={0}, use_global_device_ids=true | all-gather | bytes 278528 | tf_op jit(solution)/shard_map/all_gather | solution.py:245
  50.6 0.1 reshape.117
  50.7 0.0 all-to-all-done
  50.7 0.2 fusion.10
  51.0 13.2 %all_to_all.40 = bf16[16,10,128]{2,1,0:T(8,128)(2,1)S(1)} all-to-all(bf16[16,10,128]{2,1,0:T(8,128)(2,1)S(1)} %reshape.119), channel_id=1, replica_groups=mesh['y'=4,'z'=16,'c'=2,'mdl'=4] {'y','mdl'}, dimensions={0} | all-to-all | bytes 81920 | tf_op jit(solution)/shard_map/all_to_all | solution.py:253
  64.3 0.0 copy-done.4
  64.3 0.0 copy-done.5
  64.3 0.5 fusion.11
  64.9 1.8 all_gather.14
  66.7 27.8 %all_gather.15 = bf16[1280,128]{1,0:T(8,128)(2,1)S(1)} all-gather(bf16[80,128]{1,0:T(8,128)(2,1)S(1)} %all_gather.14), channel_id=1, replica_groups=mesh['y'=4,'z'=16,'c'=2,'mdl'=4] {'z'}, dimensions={0}, use_global_device_ids=true | all-gather | bytes 348160 | tf_op jit(solution)/shard_map/all_gather | solution.py:22
  94.5 1.2 broadcast_in_dim.9
  95.8 0.0 copy-start.3
  95.8 0.0 copy-start
  95.8 3.7 %all-to-all-start.2 = ((bf16[4,1280,128]{2,1,0:T(8,128)(2,1)}), bf16[4,1280,128]{2,1,0:T(8,128)(2,1)S(1)}, u32[]{:S(2)}, u32[]{:S(2)}) async-start(bf16[4,1280,128]{2,1,0:T(8,128)(2,1)} %broadcast_in_dim.9), calls=%async_computation.2 | async-start | bytes 2621440 | tf_op jit(solution)/shard_map/all_to_all | solution.py:24
  99.4 0.0 copy-done.3
  99.5 0.3 reshape.124
  99.8 0.0 copy-done
  99.8 2.4 %copy.22 = bf16[2,128,1,10,256]{4,0,3,1,2:T(2,128)(2,1)} copy(bf16[2,128,1,10,256]{4,1,3,2,0:T(8,128)(2,1)S(1)} %copy-done) | data formatting | bytes 2621440 | tf_op args[8]
  102.2 0.1 constant_dynamic-slice_fusion
  102.3 9.5 %all-to-all-done.2 = bf16[4,1280,128]{2,1,0:T(8,128)(2,1)S(1)} async-done(((bf16[4,1280,128]{2,1,0:T(8,128)(2,1)}), bf16[4,1280,128]{2,1,0:T(8,128)(2,1)S(1)}, u32[]{:S(2)}, u32[]{:S(2)}) %all-to-all-start.2) | async-done | bytes 1310752 | tf_op jit(solution)/shard_map/all_to_all | solution.py:24
  111.7 2.2 %reshape.132 = f32[128,10,512]{2,1,0:T(8,128)} reshape(bf16[4,1280,128]{2,1,0:T(8,128)(2,1)S(1)} %all-to-all-done.2) | data formatting | bytes 3932160 | tf_op jit(solution)/shard_map/convert_element_type | solution.py:273
  114.0 2.8 %fusion.1 = (bf16[512,128,10]{0,2,1:T(8,128)(2,1)S(1)}, f32[512]{0:T(512)S(1)}) fusion(f32[128,10,512]{2,1,0:T(8,128)} %reshape.132, f32[128,10]{1,0:T(8,128)S(1)} %bitcast.60), kind=kLoop, calls=%fused_computation.4 | loop fusion | flops 2620928 | bytes 3939328 | tf_op jit(solution)/shard_map/convert_element_type | solution.py:279
  116.7 0.0 copy-start.1
  116.8 1.3 convert_element_type.131
  118.1 0.3 copy-done.1
  118.4 2.2 %fusion.5 = bf16[512,2,256]{0,2,1:T(8,128)(2,1)S(1)} fusion(bf16[2,1280,256]{2,0,1:T(2,128)(2,1)S(1)} %bitcast.55, bf16[512,1280]{0,1:T(8,128)(2,1)} %convert_element_type.131), kind=kOutput, calls=%fused_computation.8 | convolution fusion | flops 671350784 | bytes 3145728 | tf_op jit(solution)/shard_map/rk,gkf->gfr/dot_general | solution.py:281
  120.7 0.0 copy-start.2
  120.7 11.1 %all_to_all.41 = bf16[4,130,512]{2,1,0:T(8,128)(2,1)S(1)} all-to-all(bf16[4,130,512]{2,1,0:T(8,128)(2,1)S(1)} %pad_maximum_fusion), channel_id=1, replica_groups=mesh['y'=4,'z'=16,'c'=2,'mdl'=4] {'mdl'}, dimensions={0} | all-to-all | bytes 1064960 | tf_op jit(solution)/shard_map/all_to_all | solution.py:292
  131.8 0.1 convert_reduce_fusion
  131.9 0.1 fusion.14
  132.0 0.7 broadcast_in_dim.11
  132.7 5.4 %all-to-all-start.4 = ((bf16[4,64,512]{2,1,0:T(8,128)(2,1)}), bf16[4,64,512]{2,1,0:T(8,128)(2,1)S(1)}, u32[]{:S(2)}, u32[]{:S(2)}) async-start(bf16[4,64,512]{2,1,0:T(8,128)(2,1)} %broadcast_in_dim.11), calls=%async_computation.4 | async-start | bytes 524288 | tf_op jit(solution)/shard_map/all_to_all | solution.py:299
  138.1 0.0 copy-done.2
  138.1 1.0 copy.26
  139.2 0.2 reshape.129
  139.4 3.3 %all-to-all-done.4 = bf16[4,64,512]{2,1,0:T(8,128)(2,1)S(1)} async-done(((bf16[4,64,512]{2,1,0:T(8,128)(2,1)}), bf16[4,64,512]{2,1,0:T(8,128)(2,1)S(1)}, u32[]{:S(2)}, u32[]{:S(2)}) %all-to-all-start.4) | async-done | bytes 262176 | tf_op jit(solution)/shard_map/all_to_all | solution.py:299
  142.7 0.6 fusion
  143.3 0.7 copy.27
  144.0 0.8 convert_element_type.141
  144.8 0.1 copy.28
  144.9 4.8 %all_to_all.42 = bf16[4,16,2,40,128]{4,3,1,0,2:T(8,128)(2,1)S(1)} all-to-all(bf16[4,16,2,40,128]{4,3,1,0,2:T(8,128)(2,1)S(1)} %copy.28), channel_id=1, replica_groups=mesh['y'=4,'z'=16,'c'=2,'mdl'=4] {'c'}, dimensions={2} | all-to-all | bytes 2621440 | tf_op jit(solution)/shard_map/all_to_all | solution.py:30
  149.7 0.6 reduce_sum.66
  150.3 13.9 %all_to_all.43 = bf16[4,16,1,40,128]{4,3,1,2,0:T(8,128)(2,1)S(1)} all-to-all(bf16[4,16,1,40,128]{4,3,1,2,0:T(8,128)(2,1)S(1)} %bitcast.53), channel_id=1, replica_groups=mesh['y'=4,'z'=16,'c'=2,'mdl'=4] {'y'}, dimensions={0} | all-to-all | bytes 1310720 | tf_op jit(solution)/shard_map/all_to_all | solution.py:30
  164.2 0.1 reduce_sum.67
  164.3 22.4 %all_to_all.44 = bf16[1,16,1,40,128]{4,3,2,0,1:T(8,128)(2,1)S(1)} all-to-all(bf16[1,16,1,40,128]{4,3,2,0,1:T(8,128)(2,1)S(1)} %bitcast.58), channel_id=1, replica_groups=mesh['y'=4,'z'=16,'c'=2,'mdl'=4] {'z'}, dimensions={1} | all-to-all | bytes 327680 | tf_op jit(solution)/shard_map/all_to_all | solution.py:30
  186.7 0.6 fusion.15
  (15 shorter events, 0.2 us)
Async XLA Ops:
  2.3 48.5 %all-to-all-start = ((bf16[4,40,1024]{2,1,0:T(8,128)(2,1)}), bf16[4,40,1024]{2,1,0:T(8,128)(2,1)S(1)}, u32[]{:S(2)}, u32[]{:S(2)}) async-start(bf16[4,40,1024]{2,1,0:T(8,128)(2,1)} %broadcast_in_dim.8), calls=%async_computation | async-start | bytes 655360 | tf_op jit(solution)/shard_map/all_to_all | solution.py:242
  8.0 56.3 %copy-start.4 = (bf16[512,10]{0,1:T(8,128)(2,1)S(1)}, bf16[512,10]{0,1:T(8,128)(2,1)}, u32[]{:S(2)}) copy-start(bf16[512,10]{0,1:T(8,128)(2,1)} %param.15) | copy-start | bytes 30724
  8.0 56.3 %copy-start.5 = (s32[512]{0:T(512)S(1)}, s32[512]{0:T(512)}, u32[]{:S(2)}) copy-start(s32[512]{0:T(512)} %param.11) | copy-start | bytes 6148
  95.8 3.7 %copy-start.3 = (f32[5120]{0:T(1024)S(1)}, f32[5120]{0:T(1024)}, u32[]{:S(2)}) copy-start(f32[5120]{0:T(1024)} %param.17) | copy-start | bytes 61444
  95.8 4.0 %copy-start = (bf16[2,128,1,10,256]{4,1,3,2,0:T(8,128)(2,1)S(1)}, bf16[2,128,1,10,256]{4,1,3,2,0:T(8,128)(2,1)}, u32[]{:S(2)}) copy-start(bf16[2,128,1,10,256]{4,1,3,2,0:T(8,128)(2,1)} %param.18) | copy-start | bytes 3932164
  95.8 15.9 %all-to-all-start.2 = ((bf16[4,1280,128]{2,1,0:T(8,128)(2,1)}), bf16[4,1280,128]{2,1,0:T(8,128)(2,1)S(1)}, u32[]{:S(2)}, u32[]{:S(2)}) async-start(bf16[4,1280,128]{2,1,0:T(8,128)(2,1)} %broadcast_in_dim.9), calls=%async_computation.2 | async-start | bytes 2621440 | tf_op jit(solution)/shard_map/all_to_all | solution.py:24
  116.7 1.6 copy-start.1
  120.7 17.4 %copy-start.2 = (bf16[256,128,1,10]{1,0,3,2:T(8,128)(2,1)S(1)}, bf16[256,128,1,10]{1,0,3,2:T(8,128)(2,1)}, u32[]{:S(2)}) copy-start(bf16[256,128,1,10]{1,0,3,2:T(8,128)(2,1)} %param.19) | copy-start | bytes 1966084
  132.7 10.1 %all-to-all-start.4 = ((bf16[4,64,512]{2,1,0:T(8,128)(2,1)}), bf16[4,64,512]{2,1,0:T(8,128)(2,1)S(1)}, u32[]{:S(2)}, u32[]{:S(2)}) async-start(bf16[4,64,512]{2,1,0:T(8,128)(2,1)} %broadcast_in_dim.11), calls=%async_computation.4 | async-start | bytes 524288 | tf_op jit(solution)/shard_map/all_to_all | solution.py:299

commit v13 on v12

--- a/solution.py
+++ b/solution.py
@@ -56,7 +56,7 @@
 
 
 def attention_kernel(
-    lengths_ref, query_ref, fresh_ref, cache_hbm, fresh_rows, out_ref, store_hbm, keys, values, sems, write_sems
+    lengths_ref, query_ref, cache_hbm, fresh_rows, out_ref, store_hbm, keys, values, sems, write_sems
 ):
     rows = keys.shape[0]
     chunks = rows // CHUNK_ROWS
@@ -109,7 +109,7 @@
             query_rows, keys[:, lanes], (((1,), (1,)), ((), ())), preferred_element_type=jnp.float32
         ) * score_scale
         fresh_scores = lax.dot_general(
-            query_rows, fresh_ref[0, head], (((1,), (1,)), ((), ())), preferred_element_type=jnp.float32
+            query_rows, fresh_rows[0, :, lanes], (((1,), (1,)), ((), ())), preferred_element_type=jnp.float32
         ) * score_scale
         new_score = jnp.sum(jnp.where(pick, fresh_scores, 0.0), axis=1, keepdims=True)
         scores = jnp.where(inside, scores, NEGATIVE_FILL)
@@ -118,7 +118,7 @@
         new_weight = jnp.exp(new_score - top)
         denominator = jnp.sum(weights, axis=1, keepdims=True) + new_weight
         mixed = jnp.dot(weights.astype(jnp.bfloat16), values[:, lanes], preferred_element_type=jnp.float32)
-        fresh_values = jnp.dot(pick.astype(jnp.bfloat16), fresh_ref[1, head], preferred_element_type=jnp.float32)
+        fresh_values = jnp.dot(pick.astype(jnp.bfloat16), fresh_rows[1, :, lanes], preferred_element_type=jnp.float32)
         mixed = mixed + new_weight.astype(jnp.bfloat16).astype(jnp.float32) * fresh_values
         results.append(mixed / denominator)
     pieces = [
@@ -140,9 +140,6 @@
     query_rows = jnp.transpose(
         query.reshape(slot_count, kv_heads, group_width, HEAD_SIZE), (1, 0, 2, 3)
     ).reshape(kv_heads, slot_count * group_width, HEAD_SIZE)
-    fresh = jnp.transpose(
-        key_value_fresh.reshape(2, slot_count, kv_heads, HEAD_SIZE), (0, 2, 1, 3)
-    )
     out, store = pl.pallas_call(
         attention_kernel,
         out_shape=(
@@ -151,7 +148,6 @@
         ),
         in_specs=[
             pl.BlockSpec(memory_space=pltpu.SMEM),
-            pl.BlockSpec(memory_space=pltpu.VMEM),
             pl.BlockSpec(memory_space=pltpu.VMEM),
             pl.BlockSpec(memory_space=pl.ANY),
             pl.BlockSpec(memory_space=pltpu.VMEM),
@@ -168,7 +164,7 @@
             transcendentals=kv_heads * slot_count * group_width * rows,
             bytes_accessed=2 * rows * kv_width * 2,
         ),
-    )(lengths, query_rows, fresh, kv_cache, key_value_fresh)
+    )(lengths, query_rows, kv_cache, key_value_fresh)
     return store, out.reshape(slot_count, kv_heads * group_width * HEAD_SIZE)
 
 

time: 190 us -> 190 us (level)
  no operation moved by 1% of the time
where the time goes in v13:
time: 190 us; the launch traced here: 187 us
  blocking collectives  134 us (71%)
  local copies, waits for them, and re-layouts  14.6 us (8%)
  starting transfers between devices  13.6 us (7%)
  waiting for transfers between devices  12.8 us (7%)
  other arithmetic  4.34 us (2%)
  Pallas kernels  3.75 us (2%)
  matrix products  3.49 us (2%)
    all_to_all x3, blocking collectives, scatter_sum(): lax.all_to_all(parts.astype(jnp.bfloat16), name, position, position, tile...  41.1 us
    all_gather x1, blocking collectives, body(): flat = lax.all_gather(flat, 'z', axis=0, tiled=True)  36.8 us
    all_gather x1, blocking collectives, gather_rows(): flat = lax.all_gather(flat, 'z', axis=0, tiled=True)  27.8 us
    all_to_all x1, blocking collectives, body(): arrived = lax.all_to_all(outgoing, ('y', 'mdl'), 0, 0, tiled=True)  13.2 us
    all_to_all x1, blocking collectives, body(): lax.all_to_all(payload, 'mdl', 0, 0, tiled=True).astype(jnp.float32).sum(0)  11.1 us
    all_to_all x1, waiting for transfers between devices, gather_rows(): lax.all_to_all(copies, 'y', 0, 0, tiled=True).reshape((count,) + part.shape)  9.45 us
    all_to_all x1, starting transfers between devices, body(): lax.all_to_all(hidden_copies, 'mdl', 0, 0, tiled=True)  5.45 us
    all_to_all x1, starting transfers between devices, body(): lax.all_to_all(weight_copies, 'y', 0, 0, tiled=True)  4.46 us
  transfers between devices with their start and end apart: 3, of which 2 were waited for; matrix products, arithmetic and copies ran while one was open for 3% of the time, Pallas kernels for 2%

profile of v13, /device:TPU:6, one launch (start us, length us, event | category | flops | bytes accessed | tf_op | source)
XLA Modules:
  0.0 187.4 jit_solution(9980369708633022271)
XLA Ops:
  0.6 1.6 broadcast_in_dim.8
  2.3 4.5 %all-to-all-start = ((bf16[4,40,1024]{2,1,0:T(8,128)(2,1)}), bf16[4,40,1024]{2,1,0:T(8,128)(2,1)S(1)}, u32[]{:S(2)}, u32[]{:S(2)}) async-start(bf16[4,40,1024]{2,1,0:T(8,128)(2,1)} %broadcast_in_dim.8), calls=%async_computation | async-start | bytes 655360 | tf_op jit(solution)/shard_map/all_to_all | solution.py:238
  6.7 0.7 reshape.111
  7.4 0.6 copy.20
  8.0 0.0 copy-start.4
  8.0 0.0 copy-start.5
  8.0 3.7 %shard_map.113 = (bf16[32,128]{1,0:T(8,128)(2,1)}, bf16[2,1024,256]{2,1,0:T(8,128)(2,1)}) custom-call(s32[4]{0:T(128)} %lengths_ref.1, bf16[2,16,128]{2,1,0:T(8,128)(2,1)} %bitcast.62, bf16[2,1024,256]{2,1,0:T(8,128)(2,1)} %cache_hbm.1, bf16[2,4,256]{2,1,0:T(4,128)(2,1)} %fresh_rows.1), custom_call_target="tpu_custom_call" | custom-call | flops 16777216 | bytes 1048576 | tf_op jit(solution)/shard_map/pallas_call | solution.py:143
  11.8 2.0 %all_gather.12 = bf16[64,128]{1,0:T(8,128)(2,1)S(1)} all-gather(bf16[32,128]{1,0:T(8,128)(2,1)} %get-tuple-element.4), channel_id=1, replica_groups=mesh['y'=4,'z'=16,'c'=2,'mdl'=4] {'c'}, dimensions={0}, use_global_device_ids=true | all-gather | bytes 24576 | tf_op jit(solution)/shard_map/all_gather | solution.py:240
  13.8 36.8 %all_gather.13 = bf16[1024,128]{1,0:T(8,128)(2,1)S(1)} all-gather(bf16[64,128]{1,0:T(8,128)(2,1)S(1)} %all_gather.12), channel_id=1, replica_groups=mesh['y'=4,'z'=16,'c'=2,'mdl'=4] {'z'}, dimensions={0}, use_global_device_ids=true | all-gather | bytes 278528 | tf_op jit(solution)/shard_map/all_gather | solution.py:241
  50.6 0.1 reshape.113
  50.7 0.0 all-to-all-done
  50.7 0.2 fusion.10
  51.0 13.2 %all_to_all.40 = bf16[16,10,128]{2,1,0:T(8,128)(2,1)S(1)} all-to-all(bf16[16,10,128]{2,1,0:T(8,128)(2,1)S(1)} %reshape.115), channel_id=1, replica_groups=mesh['y'=4,'z'=16,'c'=2,'mdl'=4] {'y','mdl'}, dimensions={0} | all-to-all | bytes 81920 | tf_op jit(solution)/shard_map/all_to_all | solution.py:249
  64.3 0.0 copy-done.4
  64.3 0.0 copy-done.5
  64.3 0.5 fusion.11
  64.9 1.8 all_gather.14
  66.7 27.8 %all_gather.15 = bf16[1280,128]{1,0:T(8,128)(2,1)S(1)} all-gather(bf16[80,128]{1,0:T(8,128)(2,1)S(1)} %all_gather.14), channel_id=1, replica_groups=mesh['y'=4,'z'=16,'c'=2,'mdl'=4] {'z'}, dimensions={0}, use_global_device_ids=true | all-gather | bytes 348160 | tf_op jit(solution)/shard_map/all_gather | solution.py:22
  94.5 1.2 broadcast_in_dim.9
  95.8 0.0 copy-start.3
  95.8 0.0 copy-start
  95.8 3.7 %all-to-all-start.2 = ((bf16[4,1280,128]{2,1,0:T(8,128)(2,1)}), bf16[4,1280,128]{2,1,0:T(8,128)(2,1)S(1)}, u32[]{:S(2)}, u32[]{:S(2)}) async-start(bf16[4,1280,128]{2,1,0:T(8,128)(2,1)} %broadcast_in_dim.9), calls=%async_computation.2 | async-start | bytes 2621440 | tf_op jit(solution)/shard_map/all_to_all | solution.py:24
  99.4 0.0 copy-done.3
  99.5 0.3 reshape.120
  99.8 0.0 copy-done
  99.8 2.4 %copy.22 = bf16[2,128,1,10,256]{4,0,3,1,2:T(2,128)(2,1)} copy(bf16[2,128,1,10,256]{4,1,3,2,0:T(8,128)(2,1)S(1)} %copy-done) | data formatting | bytes 2621440 | tf_op args[8]
  102.2 0.1 constant_dynamic-slice_fusion
  102.3 9.5 %all-to-all-done.2 = bf16[4,1280,128]{2,1,0:T(8,128)(2,1)S(1)} async-done(((bf16[4,1280,128]{2,1,0:T(8,128)(2,1)}), bf16[4,1280,128]{2,1,0:T(8,128)(2,1)S(1)}, u32[]{:S(2)}, u32[]{:S(2)}) %all-to-all-start.2) | async-done | bytes 1310752 | tf_op jit(solution)/shard_map/all_to_all | solution.py:24
  111.7 2.2 %reshape.128 = f32[128,10,512]{2,1,0:T(8,128)} reshape(bf16[4,1280,128]{2,1,0:T(8,128)(2,1)S(1)} %all-to-all-done.2) | data formatting | bytes 3932160 | tf_op jit(solution)/shard_map/convert_element_type | solution.py:269
  114.0 2.8 %fusion.1 = (bf16[512,128,10]{0,2,1:T(8,128)(2,1)S(1)}, f32[512]{0:T(512)S(1)}) fusion(f32[128,10,512]{2,1,0:T(8,128)} %reshape.128, f32[128,10]{1,0:T(8,128)S(1)} %bitcast.57), kind=kLoop, calls=%fused_computation.4 | loop fusion | flops 2620928 | bytes 3939328 | tf_op jit(solution)/shard_map/convert_element_type | solution.py:275
  116.7 0.0 copy-start.1
  116.8 1.3 convert_element_type.131
  118.1 0.3 copy-done.1
  118.4 2.2 %fusion.5 = bf16[512,2,256]{0,2,1:T(8,128)(2,1)S(1)} fusion(bf16[2,1280,256]{2,0,1:T(2,128)(2,1)S(1)} %bitcast.52, bf16[512,1280]{0,1:T(8,128)(2,1)} %convert_element_type.131), kind=kOutput, calls=%fused_computation.8 | convolution fusion | flops 671350784 | bytes 3145728 | tf_op jit(solution)/shard_map/rk,gkf->gfr/dot_general | solution.py:277
  120.7 0.0 copy-start.2
  120.7 11.1 %all_to_all.41 = bf16[4,130,512]{2,1,0:T(8,128)(2,1)S(1)} all-to-all(bf16[4,130,512]{2,1,0:T(8,128)(2,1)S(1)} %pad_maximum_fusion), channel_id=1, replica_groups=mesh['y'=4,'z'=16,'c'=2,'mdl'=4] {'mdl'}, dimensions={0} | all-to-all | bytes 1064960 | tf_op jit(solution)/shard_map/all_to_all | solution.py:288
  131.8 0.1 convert_reduce_fusion
  131.9 0.1 fusion.14
  132.0 0.7 broadcast_in_dim.11
  132.7 5.4 %all-to-all-start.4 = ((bf16[4,64,512]{2,1,0:T(8,128)(2,1)}), bf16[4,64,512]{2,1,0:T(8,128)(2,1)S(1)}, u32[]{:S(2)}, u32[]{:S(2)}) async-start(bf16[4,64,512]{2,1,0:T(8,128)(2,1)} %broadcast_in_dim.11), calls=%async_computation.4 | async-start | bytes 524288 | tf_op jit(solution)/shard_map/all_to_all | solution.py:295
  138.1 0.0 copy-done.2
  138.1 1.0 copy.26
  139.2 0.2 reshape.125
  139.4 3.3 %all-to-all-done.4 = bf16[4,64,512]{2,1,0:T(8,128)(2,1)S(1)} async-done(((bf16[4,64,512]{2,1,0:T(8,128)(2,1)}), bf16[4,64,512]{2,1,0:T(8,128)(2,1)S(1)}, u32[]{:S(2)}, u32[]{:S(2)}) %all-to-all-start.4) | async-done | bytes 262176 | tf_op jit(solution)/shard_map/all_to_all | solution.py:295
  142.7 0.6 fusion
  143.3 0.7 copy.27
  144.0 0.8 convert_element_type.141
  144.8 0.1 copy.28
  144.9 4.8 %all_to_all.42 = bf16[4,16,2,40,128]{4,3,1,0,2:T(8,128)(2,1)S(1)} all-to-all(bf16[4,16,2,40,128]{4,3,1,0,2:T(8,128)(2,1)S(1)} %copy.28), channel_id=1, replica_groups=mesh['y'=4,'z'=16,'c'=2,'mdl'=4] {'c'}, dimensions={2} | all-to-all | bytes 2621440 | tf_op jit(solution)/shard_map/all_to_all | solution.py:30
  149.7 0.6 reduce_sum.66
  150.3 13.9 %all_to_all.43 = bf16[4,16,1,40,128]{4,3,1,2,0:T(8,128)(2,1)S(1)} all-to-all(bf16[4,16,1,40,128]{4,3,1,2,0:T(8,128)(2,1)S(1)} %bitcast.50), channel_id=1, replica_groups=mesh['y'=4,'z'=16,'c'=2,'mdl'=4] {'y'}, dimensions={0} | all-to-all | bytes 1310720 | tf_op jit(solution)/shard_map/all_to_all | solution.py:30
  164.2 0.1 reduce_sum.67
  164.3 22.4 %all_to_all.44 = bf16[1,16,1,40,128]{4,3,2,0,1:T(8,128)(2,1)S(1)} all-to-all(bf16[1,16,1,40,128]{4,3,2,0,1:T(8,128)(2,1)S(1)} %bitcast.55), channel_id=1, replica_groups=mesh['y'=4,'z'=16,'c'=2,'mdl'=4] {'z'}, dimensions={1} | all-to-all | bytes 327680 | tf_op jit(solution)/shard_map/all_to_all | solution.py:30
  186.7 0.6 fusion.15
  (15 shorter events, 0.2 us)
Async XLA Ops:
  2.3 48.5 %all-to-all-start = ((bf16[4,40,1024]{2,1,0:T(8,128)(2,1)}), bf16[4,40,1024]{2,1,0:T(8,128)(2,1)S(1)}, u32[]{:S(2)}, u32[]{:S(2)}) async-start(bf16[4,40,1024]{2,1,0:T(8,128)(2,1)} %broadcast_in_dim.8), calls=%async_computation | async-start | bytes 655360 | tf_op jit(solution)/shard_map/all_to_all | solution.py:238
  8.0 56.3 %copy-start.4 = (bf16[512,10]{0,1:T(8,128)(2,1)S(1)}, bf16[512,10]{0,1:T(8,128)(2,1)}, u32[]{:S(2)}) copy-start(bf16[512,10]{0,1:T(8,128)(2,1)} %param.15) | copy-start | bytes 30724
  8.0 56.3 %copy-start.5 = (s32[512]{0:T(512)S(1)}, s32[512]{0:T(512)}, u32[]{:S(2)}) copy-start(s32[512]{0:T(512)} %param.11) | copy-start | bytes 6148
  95.8 3.7 %copy-start.3 = (f32[5120]{0:T(1024)S(1)}, f32[5120]{0:T(1024)}, u32[]{:S(2)}) copy-start(f32[5120]{0:T(1024)} %param.17) | copy-start | bytes 61444
  95.8 4.0 %copy-start = (bf16[2,128,1,10,256]{4,1,3,2,0:T(8,128)(2,1)S(1)}, bf16[2,128,1,10,256]{4,1,3,2,0:T(8,128)(2,1)}, u32[]{:S(2)}) copy-start(bf16[2,128,1,10,256]{4,1,3,2,0:T(8,128)(2,1)} %param.18) | copy-start | bytes 3932164
  95.8 15.9 %all-to-all-start.2 = ((bf16[4,1280,128]{2,1,0:T(8,128)(2,1)}), bf16[4,1280,128]{2,1,0:T(8,128)(2,1)S(1)}, u32[]{:S(2)}, u32[]{:S(2)}) async-start(bf16[4,1280,128]{2,1,0:T(8,128)(2,1)} %broadcast_in_dim.9), calls=%async_computation.2 | async-start | bytes 2621440 | tf_op jit(solution)/shard_map/all_to_all | solution.py:24
  116.7 1.6 copy-start.1
  120.7 17.4 %copy-start.2 = (bf16[256,128,1,10]{1,0,3,2:T(8,128)(2,1)S(1)}, bf16[256,128,1,10]{1,0,3,2:T(8,128)(2,1)}, u32[]{:S(2)}) copy-start(bf16[256,128,1,10]{1,0,3,2:T(8,128)(2,1)} %param.19) | copy-start | bytes 1966084
  132.7 10.1 %all-to-all-start.4 = ((bf16[4,64,512]{2,1,0:T(8,128)(2,1)}), bf16[4,64,512]{2,1,0:T(8,128)(2,1)S(1)}, u32[]{:S(2)}, u32[]{:S(2)}) async-start(bf16[4,64,512]{2,1,0:T(8,128)(2,1)} %broadcast_in_dim.11), calls=%async_computation.4 | async-start | bytes 524288 | tf_op jit(solution)/shard_map/all_to_all | solution.py:295

commit v14 on v13

--- a/solution.py
+++ b/solution.py
@@ -68,7 +68,9 @@
             copy.start()
             copies.append(copy)
     slot_count = lengths_ref.shape[0]
-    kv_heads, row_count, head_dim = query_ref.shape
+    head_dim = HEAD_SIZE
+    kv_heads = keys.shape[1] // head_dim
+    row_count = query_ref.shape[1] // kv_heads // head_dim * slot_count
     group_width = row_count // slot_count
     row_slot = lax.broadcasted_iota(jnp.int32, (row_count, 1), 0) // group_width
     first = jnp.zeros((row_count, 1), jnp.int32)
@@ -102,9 +104,17 @@
         writes.append(write)
     score_scale = head_dim ** (-0.5)
     results = []
+    wide_query = query_ref[...].astype(jnp.float32)
     for head in range(kv_heads):
         lanes = pl.ds(head * head_dim, head_dim)
-        query_rows = query_ref[head]
+        query_rows = jnp.concatenate(
+            [
+                wide_query[slot : slot + 1, (head * group_width + g) * head_dim : (head * group_width + g + 1) * head_dim]
+                for slot in range(slot_count)
+                for g in range(group_width)
+            ],
+            axis=0,
+        ).astype(query_ref.dtype)
         scores = lax.dot_general(
             query_rows, keys[:, lanes], (((1,), (1,)), ((), ())), preferred_element_type=jnp.float32
         ) * score_scale
@@ -137,9 +147,6 @@
     kv_heads = kv_width // HEAD_SIZE
     group_width = QUERY_HEADS // KEY_VALUE_HEADS
     rows = kv_cache.shape[1]
-    query_rows = jnp.transpose(
-        query.reshape(slot_count, kv_heads, group_width, HEAD_SIZE), (1, 0, 2, 3)
-    ).reshape(kv_heads, slot_count * group_width, HEAD_SIZE)
     out, store = pl.pallas_call(
         attention_kernel,
         out_shape=(
@@ -164,7 +171,7 @@
             transcendentals=kv_heads * slot_count * group_width * rows,
             bytes_accessed=2 * rows * kv_width * 2,
         ),
-    )(lengths, query_rows, kv_cache, key_value_fresh)
+    )(lengths, query, kv_cache, key_value_fresh)
     return store, out.reshape(slot_count, kv_heads * group_width * HEAD_SIZE)
 
 

time: 190 us -> 188 us (0.989)
  transfers between devices with their start and end apart: 3 -> 3, of which waited for: 2 -> 2; matrix products, arithmetic and copies ran while one was open for 3% -> 2% of each run, Pallas kernels for 2% -> 2%
where the time goes in v14:
time: 188 us; the launch traced here: 186 us
  blocking collectives  134 us (71%)
  starting transfers between devices  13.6 us (7%)
  local copies, waits for them, and re-layouts  13.3 us (7%)
  waiting for transfers between devices  12.8 us (7%)
  other arithmetic  4.34 us (2%)
  Pallas kernels  3.76 us (2%)
  matrix products  3.49 us (2%)
    all_to_all x3, blocking collectives, scatter_sum(): lax.all_to_all(parts.astype(jnp.bfloat16), name, position, position, tile...  41.1 us
    all_gather x1, blocking collectives, body(): flat = lax.all_gather(flat, 'z', axis=0, tiled=True)  36.8 us
    all_gather x1, blocking collectives, gather_rows(): flat = lax.all_gather(flat, 'z', axis=0, tiled=True)  27.8 us
    all_to_all x1, blocking collectives, body(): arrived = lax.all_to_all(outgoing, ('y', 'mdl'), 0, 0, tiled=True)  13.2 us
    all_to_all x1, blocking collectives, body(): lax.all_to_all(payload, 'mdl', 0, 0, tiled=True).astype(jnp.float32).sum(0)  11.1 us
    all_to_all x1, waiting for transfers between devices, gather_rows(): lax.all_to_all(copies, 'y', 0, 0, tiled=True).reshape((count,) + part.shape)  9.45 us
    all_to_all x1, starting transfers between devices, body(): lax.all_to_all(hidden_copies, 'mdl', 0, 0, tiled=True)  5.45 us
    all_to_all x1, starting transfers between devices, body(): lax.all_to_all(weight_copies, 'y', 0, 0, tiled=True)  4.46 us
  transfers between devices with their start and end apart: 3, of which 2 were waited for; matrix products, arithmetic and copies ran while one was open for 2% of the time, Pallas kernels for 2%

profile of v14, /device:TPU:6, one launch (start us, length us, event | category | flops | bytes accessed | tf_op | source)
XLA Modules:
  0.0 186.1 jit_solution(17993661599322499704)
XLA Ops:
  0.6 1.6 broadcast_in_dim.8
  2.3 4.5 %all-to-all-start = ((bf16[4,40,1024]{2,1,0:T(8,128)(2,1)}), bf16[4,40,1024]{2,1,0:T(8,128)(2,1)S(1)}, u32[]{:S(2)}, u32[]{:S(2)}) async-start(bf16[4,40,1024]{2,1,0:T(8,128)(2,1)} %broadcast_in_dim.8), calls=%async_computation | async-start | bytes 655360 | tf_op jit(solution)/shard_map/all_to_all | solution.py:245
  6.7 0.0 copy-start.4
  6.7 0.0 copy-start.5
  6.7 3.8 %shard_map.113 = (bf16[32,128]{1,0:T(8,128)(2,1)}, bf16[2,1024,256]{2,1,0:T(8,128)(2,1)}) custom-call(s32[4]{0:T(128)} %lengths_ref.1, bf16[4,1024]{1,0:T(4,128)(2,1)} %query_ref.1, bf16[2,1024,256]{2,1,0:T(8,128)(2,1)} %cache_hbm.1, bf16[2,4,256]{2,1,0:T(4,128)(2,1)} %fresh_rows.1), custom_call_target="tpu_custom_call" | custom-call | flops 16777216 | bytes 1048576 | tf_op jit(solution)/shard_map/pallas_call | solution.py:150
  10.5 2.0 %all_gather.12 = bf16[64,128]{1,0:T(8,128)(2,1)S(1)} all-gather(bf16[32,128]{1,0:T(8,128)(2,1)} %get-tuple-element.4), channel_id=1, replica_groups=mesh['y'=4,'z'=16,'c'=2,'mdl'=4] {'c'}, dimensions={0}, use_global_device_ids=true | all-gather | bytes 24576 | tf_op jit(solution)/shard_map/all_gather | solution.py:247
  12.5 36.8 %all_gather.13 = bf16[1024,128]{1,0:T(8,128)(2,1)S(1)} all-gather(bf16[64,128]{1,0:T(8,128)(2,1)S(1)} %all_gather.12), channel_id=1, replica_groups=mesh['y'=4,'z'=16,'c'=2,'mdl'=4] {'z'}, dimensions={0}, use_global_device_ids=true | all-gather | bytes 278528 | tf_op jit(solution)/shard_map/all_gather | solution.py:248
  49.3 0.1 reshape.105
  49.4 0.0 all-to-all-done
  49.4 0.2 fusion.10
  49.7 13.2 %all_to_all.40 = bf16[16,10,128]{2,1,0:T(8,128)(2,1)S(1)} all-to-all(bf16[16,10,128]{2,1,0:T(8,128)(2,1)S(1)} %reshape.107), channel_id=1, replica_groups=mesh['y'=4,'z'=16,'c'=2,'mdl'=4] {'y','mdl'}, dimensions={0} | all-to-all | bytes 81920 | tf_op jit(solution)/shard_map/all_to_all | solution.py:256
  63.0 0.0 copy-done.4
  63.0 0.0 copy-done.5
  63.0 0.5 fusion.11
  63.6 1.8 all_gather.14
  65.4 27.8 %all_gather.15 = bf16[1280,128]{1,0:T(8,128)(2,1)S(1)} all-gather(bf16[80,128]{1,0:T(8,128)(2,1)S(1)} %all_gather.14), channel_id=1, replica_groups=mesh['y'=4,'z'=16,'c'=2,'mdl'=4] {'z'}, dimensions={0}, use_global_device_ids=true | all-gather | bytes 348160 | tf_op jit(solution)/shard_map/all_gather | solution.py:22
  93.2 1.2 broadcast_in_dim.9
  94.5 0.0 copy-start.3
  94.5 0.0 copy-start
  94.5 3.7 %all-to-all-start.2 = ((bf16[4,1280,128]{2,1,0:T(8,128)(2,1)}), bf16[4,1280,128]{2,1,0:T(8,128)(2,1)S(1)}, u32[]{:S(2)}, u32[]{:S(2)}) async-start(bf16[4,1280,128]{2,1,0:T(8,128)(2,1)} %broadcast_in_dim.9), calls=%async_computation.2 | async-start | bytes 2621440 | tf_op jit(solution)/shard_map/all_to_all | solution.py:24
  98.1 0.0 copy-done.3
  98.2 0.3 reshape.112
  98.5 0.0 copy-done
  98.5 2.4 %copy.19 = bf16[2,128,1,10,256]{4,0,3,1,2:T(2,128)(2,1)} copy(bf16[2,128,1,10,256]{4,1,3,2,0:T(8,128)(2,1)S(1)} %copy-done) | data formatting | bytes 2621440 | tf_op args[8]
  100.9 0.1 constant_dynamic-slice_fusion
  101.0 9.5 %all-to-all-done.2 = bf16[4,1280,128]{2,1,0:T(8,128)(2,1)S(1)} async-done(((bf16[4,1280,128]{2,1,0:T(8,128)(2,1)}), bf16[4,1280,128]{2,1,0:T(8,128)(2,1)S(1)}, u32[]{:S(2)}, u32[]{:S(2)}) %all-to-all-start.2) | async-done | bytes 1310752 | tf_op jit(solution)/shard_map/all_to_all | solution.py:24
  110.4 2.2 %reshape.120 = f32[128,10,512]{2,1,0:T(8,128)} reshape(bf16[4,1280,128]{2,1,0:T(8,128)(2,1)S(1)} %all-to-all-done.2) | data formatting | bytes 3932160 | tf_op jit(solution)/shard_map/convert_element_type | solution.py:276
  112.7 2.8 %fusion.1 = (bf16[512,128,10]{0,2,1:T(8,128)(2,1)S(1)}, f32[512]{0:T(512)S(1)}) fusion(f32[128,10,512]{2,1,0:T(8,128)} %reshape.120, f32[128,10]{1,0:T(8,128)S(1)} %bitcast.54), kind=kLoop, calls=%fused_computation.4 | loop fusion | flops 2620928 | bytes 3939328 | tf_op jit(solution)/shard_map/convert_element_type | solution.py:282
  115.4 0.0 copy-start.1
  115.5 1.3 convert_element_type.131
  116.8 0.3 copy-done.1
  117.1 2.2 %fusion.5 = bf16[512,2,256]{0,2,1:T(8,128)(2,1)S(1)} fusion(bf16[2,1280,256]{2,0,1:T(2,128)(2,1)S(1)} %bitcast.49, bf16[512,1280]{0,1:T(8,128)(2,1)} %convert_element_type.131), kind=kOutput, calls=%fused_computation.8 | convolution fusion | flops 671350784 | bytes 3145728 | tf_op jit(solution)/shard_map/rk,gkf->gfr/dot_general | solution.py:284
  119.4 0.0 copy-start.2
  119.4 11.1 %all_to_all.41 = bf16[4,130,512]{2,1,0:T(8,128)(2,1)S(1)} all-to-all(bf16[4,130,512]{2,1,0:T(8,128)(2,1)S(1)} %pad_maximum_fusion), channel_id=1, replica_groups=mesh['y'=4,'z'=16,'c'=2,'mdl'=4] {'mdl'}, dimensions={0} | all-to-all | bytes 1064960 | tf_op jit(solution)/shard_map/all_to_all | solution.py:295
  130.5 0.1 convert_reduce_fusion
  130.6 0.1 fusion.14
  130.7 0.7 broadcast_in_dim.11
  131.4 5.5 %all-to-all-start.4 = ((bf16[4,64,512]{2,1,0:T(8,128)(2,1)}), bf16[4,64,512]{2,1,0:T(8,128)(2,1)S(1)}, u32[]{:S(2)}, u32[]{:S(2)}) async-start(bf16[4,64,512]{2,1,0:T(8,128)(2,1)} %broadcast_in_dim.11), calls=%async_computation.4 | async-start | bytes 524288 | tf_op jit(solution)/shard_map/all_to_all | solution.py:302
  136.8 0.0 copy-done.2
  136.8 1.0 copy.23
  137.9 0.2 reshape.117
  138.1 3.3 %all-to-all-done.4 = bf16[4,64,512]{2,1,0:T(8,128)(2,1)S(1)} async-done(((bf16[4,64,512]{2,1,0:T(8,128)(2,1)}), bf16[4,64,512]{2,1,0:T(8,128)(2,1)S(1)}, u32[]{:S(2)}, u32[]{:S(2)}) %all-to-all-start.4) | async-done | bytes 262176 | tf_op jit(solution)/shard_map/all_to_all | solution.py:302
  141.4 0.6 fusion
  142.0 0.7 copy.24
  142.7 0.8 convert_element_type.141
  143.5 0.1 copy.25
  143.6 4.8 %all_to_all.42 = bf16[4,16,2,40,128]{4,3,1,0,2:T(8,128)(2,1)S(1)} all-to-all(bf16[4,16,2,40,128]{4,3,1,0,2:T(8,128)(2,1)S(1)} %copy.25), channel_id=1, replica_groups=mesh['y'=4,'z'=16,'c'=2,'mdl'=4] {'c'}, dimensions={2} | all-to-all | bytes 2621440 | tf_op jit(solution)/shard_map/all_to_all | solution.py:30
  148.4 0.6 reduce_sum.66
  149.0 13.9 %all_to_all.43 = bf16[4,16,1,40,128]{4,3,1,2,0:T(8,128)(2,1)S(1)} all-to-all(bf16[4,16,1,40,128]{4,3,1,2,0:T(8,128)(2,1)S(1)} %bitcast.47), channel_id=1, replica_groups=mesh['y'=4,'z'=16,'c'=2,'mdl'=4] {'y'}, dimensions={0} | all-to-all | bytes 1310720 | tf_op jit(solution)/shard_map/all_to_all | solution.py:30
  162.9 0.1 reduce_sum.67
  163.0 22.4 %all_to_all.44 = bf16[1,16,1,40,128]{4,3,2,0,1:T(8,128)(2,1)S(1)} all-to-all(bf16[1,16,1,40,128]{4,3,2,0,1:T(8,128)(2,1)S(1)} %bitcast.52), channel_id=1, replica_groups=mesh['y'=4,'z'=16,'c'=2,'mdl'=4] {'z'}, dimensions={1} | all-to-all | bytes 327680 | tf_op jit(solution)/shard_map/all_to_all | solution.py:30
  185.4 0.6 fusion.15
  (15 shorter events, 0.2 us)
Async XLA Ops:
  2.3 47.2 %all-to-all-start = ((bf16[4,40,1024]{2,1,0:T(8,128)(2,1)}), bf16[4,40,1024]{2,1,0:T(8,128)(2,1)S(1)}, u32[]{:S(2)}, u32[]{:S(2)}) async-start(bf16[4,40,1024]{2,1,0:T(8,128)(2,1)} %broadcast_in_dim.8), calls=%async_computation | async-start | bytes 655360 | tf_op jit(solution)/shard_map/all_to_all | solution.py:245
  6.7 56.3 %copy-start.4 = (bf16[512,10]{0,1:T(8,128)(2,1)S(1)}, bf16[512,10]{0,1:T(8,128)(2,1)}, u32[]{:S(2)}) copy-start(bf16[512,10]{0,1:T(8,128)(2,1)} %param.15) | copy-start | bytes 30724
  6.7 56.3 %copy-start.5 = (s32[512]{0:T(512)S(1)}, s32[512]{0:T(512)}, u32[]{:S(2)}) copy-start(s32[512]{0:T(512)} %param.11) | copy-start | bytes 6148
  94.5 3.7 %copy-start.3 = (f32[5120]{0:T(1024)S(1)}, f32[5120]{0:T(1024)}, u32[]{:S(2)}) copy-start(f32[5120]{0:T(1024)} %param.17) | copy-start | bytes 61444
  94.5 4.0 %copy-start = (bf16[2,128,1,10,256]{4,1,3,2,0:T(8,128)(2,1)S(1)}, bf16[2,128,1,10,256]{4,1,3,2,0:T(8,128)(2,1)}, u32[]{:S(2)}) copy-start(bf16[2,128,1,10,256]{4,1,3,2,0:T(8,128)(2,1)} %param.18) | copy-start | bytes 3932164
  94.5 15.9 %all-to-all-start.2 = ((bf16[4,1280,128]{2,1,0:T(8,128)(2,1)}), bf16[4,1280,128]{2,1,0:T(8,128)(2,1)S(1)}, u32[]{:S(2)}, u32[]{:S(2)}) async-start(bf16[4,1280,128]{2,1,0:T(8,128)(2,1)} %broadcast_in_dim.9), calls=%async_computation.2 | async-start | bytes 2621440 | tf_op jit(solution)/shard_map/all_to_all | solution.py:24
  115.4 1.6 copy-start.1
  119.4 17.4 %copy-start.2 = (bf16[256,128,1,10]{1,0,3,2:T(8,128)(2,1)S(1)}, bf16[256,128,1,10]{1,0,3,2:T(8,128)(2,1)}, u32[]{:S(2)}) copy-start(bf16[256,128,1,10]{1,0,3,2:T(8,128)(2,1)} %param.19) | copy-start | bytes 1966084
  131.4 10.1 %all-to-all-start.4 = ((bf16[4,64,512]{2,1,0:T(8,128)(2,1)}), bf16[4,64,512]{2,1,0:T(8,128)(2,1)S(1)}, u32[]{:S(2)}, u32[]{:S(2)}) async-start(bf16[4,64,512]{2,1,0:T(8,128)(2,1)} %broadcast_in_dim.11), calls=%async_computation.4 | async-start | bytes 524288 | tf_op jit(solution)/shard_map/all_to_all | solution.py:302

commit v15 on v14

--- a/solution.py
+++ b/solution.py
@@ -52,7 +52,7 @@
     return moved.astype(jnp.float32).sum(0).reshape(height, value.shape[1])
 
 
-CHUNK_ROWS = 256
+CHUNK_ROWS = 512
 
 
 def attention_kernel(

time: 188 us -> 188 us (level)
  no operation moved by 1% of the time
where the time goes in v15:
time: 188 us; the launch traced here: 186 us
  blocking collectives  134 us (71%)
  starting transfers between devices  13.6 us (7%)
  local copies, waits for them, and re-layouts  13.3 us (7%)
  waiting for transfers between devices  12.8 us (7%)
  other arithmetic  4.34 us (2%)
  Pallas kernels  3.63 us (2%)
  matrix products  3.49 us (2%)
    all_to_all x3, blocking collectives, scatter_sum(): lax.all_to_all(parts.astype(jnp.bfloat16), name, position, position, tile...  41.1 us
    all_gather x1, blocking collectives, body(): flat = lax.all_gather(flat, 'z', axis=0, tiled=True)  36.8 us
    all_gather x1, blocking collectives, gather_rows(): flat = lax.all_gather(flat, 'z', axis=0, tiled=True)  27.8 us
    all_to_all x1, blocking collectives, body(): arrived = lax.all_to_all(outgoing, ('y', 'mdl'), 0, 0, tiled=True)  13.2 us
    all_to_all x1, blocking collectives, body(): lax.all_to_all(payload, 'mdl', 0, 0, tiled=True).astype(jnp.float32).sum(0)  11.1 us
    all_to_all x1, waiting for transfers between devices, gather_rows(): lax.all_to_all(copies, 'y', 0, 0, tiled=True).reshape((count,) + part.shape)  9.45 us
    all_to_all x1, starting transfers between devices, body(): lax.all_to_all(hidden_copies, 'mdl', 0, 0, tiled=True)  5.45 us
    all_to_all x1, starting transfers between devices, body(): lax.all_to_all(weight_copies, 'y', 0, 0, tiled=True)  4.46 us
  transfers between devices with their start and end apart: 3, of which 2 were waited for; matrix products, arithmetic and copies ran while one was open for 2% of the time, Pallas kernels for 2%

profile of v15, /device:TPU:6, one launch (start us, length us, event | category | flops | bytes accessed | tf_op | source)
XLA Modules:
  0.0 185.9 jit_solution(10857704304955872088)
XLA Ops:
  0.6 1.6 broadcast_in_dim.8
  2.3 4.5 %all-to-all-start = ((bf16[4,40,1024]{2,1,0:T(8,128)(2,1)}), bf16[4,40,1024]{2,1,0:T(8,128)(2,1)S(1)}, u32[]{:S(2)}, u32[]{:S(2)}) async-start(bf16[4,40,1024]{2,1,0:T(8,128)(2,1)} %broadcast_in_dim.8), calls=%async_computation | async-start | bytes 655360 | tf_op jit(solution)/shard_map/all_to_all | solution.py:245
  6.7 0.0 copy-start.4
  6.7 0.0 copy-start.5
  6.7 3.6 %shard_map.113 = (bf16[32,128]{1,0:T(8,128)(2,1)}, bf16[2,1024,256]{2,1,0:T(8,128)(2,1)}) custom-call(s32[4]{0:T(128)} %lengths_ref.1, bf16[4,1024]{1,0:T(4,128)(2,1)} %query_ref.1, bf16[2,1024,256]{2,1,0:T(8,128)(2,1)} %cache_hbm.1, bf16[2,4,256]{2,1,0:T(4,128)(2,1)} %fresh_rows.1), custom_call_target="tpu_custom_call" | custom-call | flops 16777216 | bytes 1048576 | tf_op jit(solution)/shard_map/pallas_call | solution.py:150
  10.4 2.0 %all_gather.12 = bf16[64,128]{1,0:T(8,128)(2,1)S(1)} all-gather(bf16[32,128]{1,0:T(8,128)(2,1)} %get-tuple-element.4), channel_id=1, replica_groups=mesh['y'=4,'z'=16,'c'=2,'mdl'=4] {'c'}, dimensions={0}, use_global_device_ids=true | all-gather | bytes 24576 | tf_op jit(solution)/shard_map/all_gather | solution.py:247
  12.4 36.8 %all_gather.13 = bf16[1024,128]{1,0:T(8,128)(2,1)S(1)} all-gather(bf16[64,128]{1,0:T(8,128)(2,1)S(1)} %all_gather.12), channel_id=1, replica_groups=mesh['y'=4,'z'=16,'c'=2,'mdl'=4] {'z'}, dimensions={0}, use_global_device_ids=true | all-gather | bytes 278528 | tf_op jit(solution)/shard_map/all_gather | solution.py:248
  49.2 0.1 reshape.105
  49.3 0.0 all-to-all-done
  49.3 0.2 fusion.10
  49.6 13.2 %all_to_all.40 = bf16[16,10,128]{2,1,0:T(8,128)(2,1)S(1)} all-to-all(bf16[16,10,128]{2,1,0:T(8,128)(2,1)S(1)} %reshape.107), channel_id=1, replica_groups=mesh['y'=4,'z'=16,'c'=2,'mdl'=4] {'y','mdl'}, dimensions={0} | all-to-all | bytes 81920 | tf_op jit(solution)/shard_map/all_to_all | solution.py:256
  62.9 0.0 copy-done.4
  62.9 0.0 copy-done.5
  62.9 0.5 fusion.11
  63.4 1.8 all_gather.14
  65.3 27.8 %all_gather.15 = bf16[1280,128]{1,0:T(8,128)(2,1)S(1)} all-gather(bf16[80,128]{1,0:T(8,128)(2,1)S(1)} %all_gather.14), channel_id=1, replica_groups=mesh['y'=4,'z'=16,'c'=2,'mdl'=4] {'z'}, dimensions={0}, use_global_device_ids=true | all-gather | bytes 348160 | tf_op jit(solution)/shard_map/all_gather | solution.py:22
  93.1 1.2 broadcast_in_dim.9
  94.3 0.0 copy-start.3
  94.3 0.0 copy-start
  94.3 3.7 %all-to-all-start.2 = ((bf16[4,1280,128]{2,1,0:T(8,128)(2,1)}), bf16[4,1280,128]{2,1,0:T(8,128)(2,1)S(1)}, u32[]{:S(2)}, u32[]{:S(2)}) async-start(bf16[4,1280,128]{2,1,0:T(8,128)(2,1)} %broadcast_in_dim.9), calls=%async_computation.2 | async-start | bytes 2621440 | tf_op jit(solution)/shard_map/all_to_all | solution.py:24
  98.0 0.0 copy-done.3
  98.0 0.3 reshape.112
  98.3 0.0 copy-done
  98.4 2.4 %copy.19 = bf16[2,128,1,10,256]{4,0,3,1,2:T(2,128)(2,1)} copy(bf16[2,128,1,10,256]{4,1,3,2,0:T(8,128)(2,1)S(1)} %copy-done) | data formatting | bytes 2621440 | tf_op args[8]
  100.8 0.1 constant_dynamic-slice_fusion
  100.8 9.5 %all-to-all-done.2 = bf16[4,1280,128]{2,1,0:T(8,128)(2,1)S(1)} async-done(((bf16[4,1280,128]{2,1,0:T(8,128)(2,1)}), bf16[4,1280,128]{2,1,0:T(8,128)(2,1)S(1)}, u32[]{:S(2)}, u32[]{:S(2)}) %all-to-all-start.2) | async-done | bytes 1310752 | tf_op jit(solution)/shard_map/all_to_all | solution.py:24
  110.3 2.2 %reshape.120 = f32[128,10,512]{2,1,0:T(8,128)} reshape(bf16[4,1280,128]{2,1,0:T(8,128)(2,1)S(1)} %all-to-all-done.2) | data formatting | bytes 3932160 | tf_op jit(solution)/shard_map/convert_element_type | solution.py:276
  112.5 2.8 %fusion.1 = (bf16[512,128,10]{0,2,1:T(8,128)(2,1)S(1)}, f32[512]{0:T(512)S(1)}) fusion(f32[128,10,512]{2,1,0:T(8,128)} %reshape.120, f32[128,10]{1,0:T(8,128)S(1)} %bitcast.54), kind=kLoop, calls=%fused_computation.4 | loop fusion | flops 2620928 | bytes 3939328 | tf_op jit(solution)/shard_map/convert_element_type | solution.py:282
  115.3 0.0 copy-start.1
  115.3 1.3 convert_element_type.131
  116.7 0.3 copy-done.1
  116.9 2.2 %fusion.5 = bf16[512,2,256]{0,2,1:T(8,128)(2,1)S(1)} fusion(bf16[2,1280,256]{2,0,1:T(2,128)(2,1)S(1)} %bitcast.49, bf16[512,1280]{0,1:T(8,128)(2,1)} %convert_element_type.131), kind=kOutput, calls=%fused_computation.8 | convolution fusion | flops 671350784 | bytes 3145728 | tf_op jit(solution)/shard_map/rk,gkf->gfr/dot_general | solution.py:284
  119.3 0.0 copy-start.2
  119.3 11.1 %all_to_all.41 = bf16[4,130,512]{2,1,0:T(8,128)(2,1)S(1)} all-to-all(bf16[4,130,512]{2,1,0:T(8,128)(2,1)S(1)} %pad_maximum_fusion), channel_id=1, replica_groups=mesh['y'=4,'z'=16,'c'=2,'mdl'=4] {'mdl'}, dimensions={0} | all-to-all | bytes 1064960 | tf_op jit(solution)/shard_map/all_to_all | solution.py:295
  130.4 0.1 convert_reduce_fusion
  130.5 0.1 fusion.14
  130.5 0.7 broadcast_in_dim.11
  131.2 5.4 %all-to-all-start.4 = ((bf16[4,64,512]{2,1,0:T(8,128)(2,1)}), bf16[4,64,512]{2,1,0:T(8,128)(2,1)S(1)}, u32[]{:S(2)}, u32[]{:S(2)}) async-start(bf16[4,64,512]{2,1,0:T(8,128)(2,1)} %broadcast_in_dim.11), calls=%async_computation.4 | async-start | bytes 524288 | tf_op jit(solution)/shard_map/all_to_all | solution.py:302
  136.7 0.0 copy-done.2
  136.7 1.0 copy.23
  137.7 0.2 reshape.117
  138.0 3.3 %all-to-all-done.4 = bf16[4,64,512]{2,1,0:T(8,128)(2,1)S(1)} async-done(((bf16[4,64,512]{2,1,0:T(8,128)(2,1)}), bf16[4,64,512]{2,1,0:T(8,128)(2,1)S(1)}, u32[]{:S(2)}, u32[]{:S(2)}) %all-to-all-start.4) | async-done | bytes 262176 | tf_op jit(solution)/shard_map/all_to_all | solution.py:302
  141.3 0.6 fusion
  141.9 0.7 copy.24
  142.5 0.8 convert_element_type.141
  143.4 0.1 copy.25
  143.5 4.8 %all_to_all.42 = bf16[4,16,2,40,128]{4,3,1,0,2:T(8,128)(2,1)S(1)} all-to-all(bf16[4,16,2,40,128]{4,3,1,0,2:T(8,128)(2,1)S(1)} %copy.25), channel_id=1, replica_groups=mesh['y'=4,'z'=16,'c'=2,'mdl'=4] {'c'}, dimensions={2} | all-to-all | bytes 2621440 | tf_op jit(solution)/shard_map/all_to_all | solution.py:30
  148.3 0.6 reduce_sum.66
  148.9 13.9 %all_to_all.43 = bf16[4,16,1,40,128]{4,3,1,2,0:T(8,128)(2,1)S(1)} all-to-all(bf16[4,16,1,40,128]{4,3,1,2,0:T(8,128)(2,1)S(1)} %bitcast.47), channel_id=1, replica_groups=mesh['y'=4,'z'=16,'c'=2,'mdl'=4] {'y'}, dimensions={0} | all-to-all | bytes 1310720 | tf_op jit(solution)/shard_map/all_to_all | solution.py:30
  162.8 0.1 reduce_sum.67
  162.9 22.4 %all_to_all.44 = bf16[1,16,1,40,128]{4,3,2,0,1:T(8,128)(2,1)S(1)} all-to-all(bf16[1,16,1,40,128]{4,3,2,0,1:T(8,128)(2,1)S(1)} %bitcast.52), channel_id=1, replica_groups=mesh['y'=4,'z'=16,'c'=2,'mdl'=4] {'z'}, dimensions={1} | all-to-all | bytes 327680 | tf_op jit(solution)/shard_map/all_to_all | solution.py:30
  185.3 0.6 fusion.15
  (15 shorter events, 0.2 us)
Async XLA Ops:
  2.3 47.0 %all-to-all-start = ((bf16[4,40,1024]{2,1,0:T(8,128)(2,1)}), bf16[4,40,1024]{2,1,0:T(8,128)(2,1)S(1)}, u32[]{:S(2)}, u32[]{:S(2)}) async-start(bf16[4,40,1024]{2,1,0:T(8,128)(2,1)} %broadcast_in_dim.8), calls=%async_computation | async-start | bytes 655360 | tf_op jit(solution)/shard_map/all_to_all | solution.py:245
  6.7 56.2 %copy-start.4 = (bf16[512,10]{0,1:T(8,128)(2,1)S(1)}, bf16[512,10]{0,1:T(8,128)(2,1)}, u32[]{:S(2)}) copy-start(bf16[512,10]{0,1:T(8,128)(2,1)} %param.15) | copy-start | bytes 30724
  6.7 56.2 %copy-start.5 = (s32[512]{0:T(512)S(1)}, s32[512]{0:T(512)}, u32[]{:S(2)}) copy-start(s32[512]{0:T(512)} %param.11) | copy-start | bytes 6148
  94.3 3.7 %copy-start.3 = (f32[5120]{0:T(1024)S(1)}, f32[5120]{0:T(1024)}, u32[]{:S(2)}) copy-start(f32[5120]{0:T(1024)} %param.17) | copy-start | bytes 61444
  94.3 4.0 %copy-start = (bf16[2,128,1,10,256]{4,1,3,2,0:T(8,128)(2,1)S(1)}, bf16[2,128,1,10,256]{4,1,3,2,0:T(8,128)(2,1)}, u32[]{:S(2)}) copy-start(bf16[2,128,1,10,256]{4,1,3,2,0:T(8,128)(2,1)} %param.18) | copy-start | bytes 3932164
  94.3 15.9 %all-to-all-start.2 = ((bf16[4,1280,128]{2,1,0:T(8,128)(2,1)}), bf16[4,1280,128]{2,1,0:T(8,128)(2,1)S(1)}, u32[]{:S(2)}, u32[]{:S(2)}) async-start(bf16[4,1280,128]{2,1,0:T(8,128)(2,1)} %broadcast_in_dim.9), calls=%async_computation.2 | async-start | bytes 2621440 | tf_op jit(solution)/shard_map/all_to_all | solution.py:24
  115.3 1.6 copy-start.1
  119.3 17.4 %copy-start.2 = (bf16[256,128,1,10]{1,0,3,2:T(8,128)(2,1)S(1)}, bf16[256,128,1,10]{1,0,3,2:T(8,128)(2,1)}, u32[]{:S(2)}) copy-start(bf16[256,128,1,10]{1,0,3,2:T(8,128)(2,1)} %param.19) | copy-start | bytes 1966084
  131.2 10.1 %all-to-all-start.4 = ((bf16[4,64,512]{2,1,0:T(8,128)(2,1)}), bf16[4,64,512]{2,1,0:T(8,128)(2,1)S(1)}, u32[]{:S(2)}, u32[]{:S(2)}) async-start(bf16[4,64,512]{2,1,0:T(8,128)(2,1)} %broadcast_in_dim.11), calls=%async_computation.4 | async-start | bytes 524288 | tf_op jit(solution)/shard_map/all_to_all | solution.py:302

commit v16 on v15

--- a/solution.py
+++ b/solution.py
@@ -52,7 +52,7 @@
     return moved.astype(jnp.float32).sum(0).reshape(height, value.shape[1])
 
 
-CHUNK_ROWS = 512
+CHUNK_ROWS = 1024
 
 
 def attention_kernel(

time: 188 us -> 188 us (level)
  no operation moved by 1% of the time
where the time goes in v16:
time: 188 us; the launch traced here: 186 us
  blocking collectives  134 us (71%)
  starting transfers between devices  13.6 us (7%)
  local copies, waits for them, and re-layouts  13.3 us (7%)
  waiting for transfers between devices  12.8 us (7%)
  other arithmetic  4.34 us (2%)
  Pallas kernels  3.63 us (2%)
  matrix products  3.49 us (2%)
    all_to_all x3, blocking collectives, scatter_sum(): lax.all_to_all(parts.astype(jnp.bfloat16), name, position, position, tile...  41.1 us
    all_gather x1, blocking collectives, body(): flat = lax.all_gather(flat, 'z', axis=0, tiled=True)  36.8 us
    all_gather x1, blocking collectives, gather_rows(): flat = lax.all_gather(flat, 'z', axis=0, tiled=True)  27.8 us
    all_to_all x1, blocking collectives, body(): arrived = lax.all_to_all(outgoing, ('y', 'mdl'), 0, 0, tiled=True)  13.2 us
    all_to_all x1, blocking collectives, body(): lax.all_to_all(payload, 'mdl', 0, 0, tiled=True).astype(jnp.float32).sum(0)  11.1 us
    all_to_all x1, waiting for transfers between devices, gather_rows(): lax.all_to_all(copies, 'y', 0, 0, tiled=True).reshape((count,) + part.shape)  9.45 us
    all_to_all x1, starting transfers between devices, body(): lax.all_to_all(hidden_copies, 'mdl', 0, 0, tiled=True)  5.45 us
    all_to_all x1, starting transfers between devices, body(): lax.all_to_all(weight_copies, 'y', 0, 0, tiled=True)  4.46 us
  transfers between devices with their start and end apart: 3, of which 2 were waited for; matrix products, arithmetic and copies ran while one was open for 2% of the time, Pallas kernels for 2%

profile of v16, /device:TPU:6, one launch (start us, length us, event | category | flops | bytes accessed | tf_op | source)
XLA Modules:
  0.0 185.9 jit_solution(10494816665144769895)
XLA Ops:
  0.6 1.6 broadcast_in_dim.8
  2.3 4.5 %all-to-all-start = ((bf16[4,40,1024]{2,1,0:T(8,128)(2,1)}), bf16[4,40,1024]{2,1,0:T(8,128)(2,1)S(1)}, u32[]{:S(2)}, u32[]{:S(2)}) async-start(bf16[4,40,1024]{2,1,0:T(8,128)(2,1)} %broadcast_in_dim.8), calls=%async_computation | async-start | bytes 655360 | tf_op jit(solution)/shard_map/all_to_all | solution.py:245
  6.7 0.0 copy-start.4
  6.7 0.0 copy-start.5
  6.7 3.6 %shard_map.113 = (bf16[32,128]{1,0:T(8,128)(2,1)}, bf16[2,1024,256]{2,1,0:T(8,128)(2,1)}) custom-call(s32[4]{0:T(128)} %lengths_ref.1, bf16[4,1024]{1,0:T(4,128)(2,1)} %query_ref.1, bf16[2,1024,256]{2,1,0:T(8,128)(2,1)} %cache_hbm.1, bf16[2,4,256]{2,1,0:T(4,128)(2,1)} %fresh_rows.1), custom_call_target="tpu_custom_call" | custom-call | flops 16777216 | bytes 1048576 | tf_op jit(solution)/shard_map/pallas_call | solution.py:150
  10.4 2.0 %all_gather.12 = bf16[64,128]{1,0:T(8,128)(2,1)S(1)} all-gather(bf16[32,128]{1,0:T(8,128)(2,1)} %get-tuple-element.4), channel_id=1, replica_groups=mesh['y'=4,'z'=16,'c'=2,'mdl'=4] {'c'}, dimensions={0}, use_global_device_ids=true | all-gather | bytes 24576 | tf_op jit(solution)/shard_map/all_gather | solution.py:247
  12.4 36.8 %all_gather.13 = bf16[1024,128]{1,0:T(8,128)(2,1)S(1)} all-gather(bf16[64,128]{1,0:T(8,128)(2,1)S(1)} %all_gather.12), channel_id=1, replica_groups=mesh['y'=4,'z'=16,'c'=2,'mdl'=4] {'z'}, dimensions={0}, use_global_device_ids=true | all-gather | bytes 278528 | tf_op jit(solution)/shard_map/all_gather | solution.py:248
  49.2 0.1 reshape.105
  49.3 0.0 all-to-all-done
  49.3 0.3 fusion.10
  49.6 13.2 %all_to_all.40 = bf16[16,10,128]{2,1,0:T(8,128)(2,1)S(1)} all-to-all(bf16[16,10,128]{2,1,0:T(8,128)(2,1)S(1)} %reshape.107), channel_id=1, replica_groups=mesh['y'=4,'z'=16,'c'=2,'mdl'=4] {'y','mdl'}, dimensions={0} | all-to-all | bytes 81920 | tf_op jit(solution)/shard_map/all_to_all | solution.py:256
  62.9 0.0 copy-done.4
  62.9 0.0 copy-done.5
  62.9 0.5 fusion.11
  63.4 1.8 all_gather.14
  65.3 27.8 %all_gather.15 = bf16[1280,128]{1,0:T(8,128)(2,1)S(1)} all-gather(bf16[80,128]{1,0:T(8,128)(2,1)S(1)} %all_gather.14), channel_id=1, replica_groups=mesh['y'=4,'z'=16,'c'=2,'mdl'=4] {'z'}, dimensions={0}, use_global_device_ids=true | all-gather | bytes 348160 | tf_op jit(solution)/shard_map/all_gather | solution.py:22
  93.1 1.2 broadcast_in_dim.9
  94.3 0.0 copy-start.3
  94.3 0.0 copy-start
  94.3 3.7 %all-to-all-start.2 = ((bf16[4,1280,128]{2,1,0:T(8,128)(2,1)}), bf16[4,1280,128]{2,1,0:T(8,128)(2,1)S(1)}, u32[]{:S(2)}, u32[]{:S(2)}) async-start(bf16[4,1280,128]{2,1,0:T(8,128)(2,1)} %broadcast_in_dim.9), calls=%async_computation.2 | async-start | bytes 2621440 | tf_op jit(solution)/shard_map/all_to_all | solution.py:24
  98.0 0.0 copy-done.3
  98.0 0.3 reshape.112
  98.3 0.0 copy-done
  98.3 2.4 %copy.19 = bf16[2,128,1,10,256]{4,0,3,1,2:T(2,128)(2,1)} copy(bf16[2,128,1,10,256]{4,1,3,2,0:T(8,128)(2,1)S(1)} %copy-done) | data formatting | bytes 2621440 | tf_op args[8]
  100.8 0.1 constant_dynamic-slice_fusion
  100.8 9.5 %all-to-all-done.2 = bf16[4,1280,128]{2,1,0:T(8,128)(2,1)S(1)} async-done(((bf16[4,1280,128]{2,1,0:T(8,128)(2,1)}), bf16[4,1280,128]{2,1,0:T(8,128)(2,1)S(1)}, u32[]{:S(2)}, u32[]{:S(2)}) %all-to-all-start.2) | async-done | bytes 1310752 | tf_op jit(solution)/shard_map/all_to_all | solution.py:24
  110.3 2.2 %reshape.120 = f32[128,10,512]{2,1,0:T(8,128)} reshape(bf16[4,1280,128]{2,1,0:T(8,128)(2,1)S(1)} %all-to-all-done.2) | data formatting | bytes 3932160 | tf_op jit(solution)/shard_map/convert_element_type | solution.py:276
  112.5 2.8 %fusion.1 = (bf16[512,128,10]{0,2,1:T(8,128)(2,1)S(1)}, f32[512]{0:T(512)S(1)}) fusion(f32[128,10,512]{2,1,0:T(8,128)} %reshape.120, f32[128,10]{1,0:T(8,128)S(1)} %bitcast.54), kind=kLoop, calls=%fused_computation.4 | loop fusion | flops 2620928 | bytes 3939328 | tf_op jit(solution)/shard_map/convert_element_type | solution.py:282
  115.3 0.0 copy-start.1
  115.3 1.3 convert_element_type.131
  116.7 0.3 copy-done.1
  116.9 2.2 %fusion.5 = bf16[512,2,256]{0,2,1:T(8,128)(2,1)S(1)} fusion(bf16[2,1280,256]{2,0,1:T(2,128)(2,1)S(1)} %bitcast.49, bf16[512,1280]{0,1:T(8,128)(2,1)} %convert_element_type.131), kind=kOutput, calls=%fused_computation.8 | convolution fusion | flops 671350784 | bytes 3145728 | tf_op jit(solution)/shard_map/rk,gkf->gfr/dot_general | solution.py:284
  119.3 0.0 copy-start.2
  119.3 11.1 %all_to_all.41 = bf16[4,130,512]{2,1,0:T(8,128)(2,1)S(1)} all-to-all(bf16[4,130,512]{2,1,0:T(8,128)(2,1)S(1)} %pad_maximum_fusion), channel_id=1, replica_groups=mesh['y'=4,'z'=16,'c'=2,'mdl'=4] {'mdl'}, dimensions={0} | all-to-all | bytes 1064960 | tf_op jit(solution)/shard_map/all_to_all | solution.py:295
  130.4 0.1 convert_reduce_fusion
  130.5 0.1 fusion.14
  130.5 0.7 broadcast_in_dim.11
  131.2 5.4 %all-to-all-start.4 = ((bf16[4,64,512]{2,1,0:T(8,128)(2,1)}), bf16[4,64,512]{2,1,0:T(8,128)(2,1)S(1)}, u32[]{:S(2)}, u32[]{:S(2)}) async-start(bf16[4,64,512]{2,1,0:T(8,128)(2,1)} %broadcast_in_dim.11), calls=%async_computation.4 | async-start | bytes 524288 | tf_op jit(solution)/shard_map/all_to_all | solution.py:302
  136.7 0.0 copy-done.2
  136.7 1.0 copy.23
  137.7 0.2 reshape.117
  138.0 3.3 %all-to-all-done.4 = bf16[4,64,512]{2,1,0:T(8,128)(2,1)S(1)} async-done(((bf16[4,64,512]{2,1,0:T(8,128)(2,1)}), bf16[4,64,512]{2,1,0:T(8,128)(2,1)S(1)}, u32[]{:S(2)}, u32[]{:S(2)}) %all-to-all-start.4) | async-done | bytes 262176 | tf_op jit(solution)/shard_map/all_to_all | solution.py:302
  141.3 0.6 fusion
  141.9 0.7 copy.24
  142.5 0.8 convert_element_type.141
  143.3 0.1 copy.25
  143.5 4.8 %all_to_all.42 = bf16[4,16,2,40,128]{4,3,1,0,2:T(8,128)(2,1)S(1)} all-to-all(bf16[4,16,2,40,128]{4,3,1,0,2:T(8,128)(2,1)S(1)} %copy.25), channel_id=1, replica_groups=mesh['y'=4,'z'=16,'c'=2,'mdl'=4] {'c'}, dimensions={2} | all-to-all | bytes 2621440 | tf_op jit(solution)/shard_map/all_to_all | solution.py:30
  148.3 0.6 reduce_sum.66
  148.9 13.9 %all_to_all.43 = bf16[4,16,1,40,128]{4,3,1,2,0:T(8,128)(2,1)S(1)} all-to-all(bf16[4,16,1,40,128]{4,3,1,2,0:T(8,128)(2,1)S(1)} %bitcast.47), channel_id=1, replica_groups=mesh['y'=4,'z'=16,'c'=2,'mdl'=4] {'y'}, dimensions={0} | all-to-all | bytes 1310720 | tf_op jit(solution)/shard_map/all_to_all | solution.py:30
  162.7 0.1 reduce_sum.67
  162.8 22.4 %all_to_all.44 = bf16[1,16,1,40,128]{4,3,2,0,1:T(8,128)(2,1)S(1)} all-to-all(bf16[1,16,1,40,128]{4,3,2,0,1:T(8,128)(2,1)S(1)} %bitcast.52), channel_id=1, replica_groups=mesh['y'=4,'z'=16,'c'=2,'mdl'=4] {'z'}, dimensions={1} | all-to-all | bytes 327680 | tf_op jit(solution)/shard_map/all_to_all | solution.py:30
  185.3 0.6 fusion.15
  (15 shorter events, 0.2 us)
Async XLA Ops:
  2.3 47.0 %all-to-all-start = ((bf16[4,40,1024]{2,1,0:T(8,128)(2,1)}), bf16[4,40,1024]{2,1,0:T(8,128)(2,1)S(1)}, u32[]{:S(2)}, u32[]{:S(2)}) async-start(bf16[4,40,1024]{2,1,0:T(8,128)(2,1)} %broadcast_in_dim.8), calls=%async_computation | async-start | bytes 655360 | tf_op jit(solution)/shard_map/all_to_all | solution.py:245
  6.7 56.2 %copy-start.4 = (bf16[512,10]{0,1:T(8,128)(2,1)S(1)}, bf16[512,10]{0,1:T(8,128)(2,1)}, u32[]{:S(2)}) copy-start(bf16[512,10]{0,1:T(8,128)(2,1)} %param.15) | copy-start | bytes 30724
  6.7 56.2 %copy-start.5 = (s32[512]{0:T(512)S(1)}, s32[512]{0:T(512)}, u32[]{:S(2)}) copy-start(s32[512]{0:T(512)} %param.11) | copy-start | bytes 6148
  94.3 3.7 %copy-start.3 = (f32[5120]{0:T(1024)S(1)}, f32[5120]{0:T(1024)}, u32[]{:S(2)}) copy-start(f32[5120]{0:T(1024)} %param.17) | copy-start | bytes 61444
  94.3 4.0 %copy-start = (bf16[2,128,1,10,256]{4,1,3,2,0:T(8,128)(2,1)S(1)}, bf16[2,128,1,10,256]{4,1,3,2,0:T(8,128)(2,1)}, u32[]{:S(2)}) copy-start(bf16[2,128,1,10,256]{4,1,3,2,0:T(8,128)(2,1)} %param.18) | copy-start | bytes 3932164
  94.3 15.9 %all-to-all-start.2 = ((bf16[4,1280,128]{2,1,0:T(8,128)(2,1)}), bf16[4,1280,128]{2,1,0:T(8,128)(2,1)S(1)}, u32[]{:S(2)}, u32[]{:S(2)}) async-start(bf16[4,1280,128]{2,1,0:T(8,128)(2,1)} %broadcast_in_dim.9), calls=%async_computation.2 | async-start | bytes 2621440 | tf_op jit(solution)/shard_map/all_to_all | solution.py:24
  115.3 1.6 copy-start.1
  119.3 17.4 %copy-start.2 = (bf16[256,128,1,10]{1,0,3,2:T(8,128)(2,1)S(1)}, bf16[256,128,1,10]{1,0,3,2:T(8,128)(2,1)}, u32[]{:S(2)}) copy-start(bf16[256,128,1,10]{1,0,3,2:T(8,128)(2,1)} %param.19) | copy-start | bytes 1966084
  131.2 10.1 %all-to-all-start.4 = ((bf16[4,64,512]{2,1,0:T(8,128)(2,1)}), bf16[4,64,512]{2,1,0:T(8,128)(2,1)S(1)}, u32[]{:S(2)}, u32[]{:S(2)}) async-start(bf16[4,64,512]{2,1,0:T(8,128)(2,1)} %broadcast_in_dim.11), calls=%async_computation.4 | async-start | bytes 524288 | tf_op jit(solution)/shard_map/all_to_all | solution.py:302
